TPU v7x, 256 devices: a whole 4x4x8 slice. The times are simulated.
256 devices in a mesh: rows: 32 (over z, y), cols: 8 (over x, core).
Axes of the slice: x: 4, y: 4, z: 8, core: 2. Of those that a mesh axis runs over, the one named last changes fastest.
Arguments:
- points: bfloat16 [131072, 128], P(('rows', 'cols')), may hold values from -6 to 6
- gradient: float32 [131072, 128], P(('rows', 'cols')), may hold values from -6 to 6
- panel_index: int32 [16, 1024], P('cols'), may hold values from 0 to 131071, as said below
Outputs:
- new_gradient: float32 [131072, 128], P(('rows', 'cols'))
- update: float32 [16384, 128], P('cols')
Inputs may be any that keep to these rules, and one draw needn't show every extreme that they name: `panel_index`: all 16384 indices are distinct.
All inputs are finite; a program needn't handle non-finite values.
Results may differ from a plain program's by a relative error of at most 0.0015.
The roundings to bfloat16 on the way count: a program that leaves them out, or rounds other values in their place, can miss the bound.
Values may be sent and summed in bfloat16 or wider, within the bound.
No kernel may reach another device: no remote copies, remote signals or barrier semaphores. Data moves between devices by JAX's collectives and lax.ppermute only.
A program may use at most 128 MiB of HBM per device.

v0:
```python
import math

import jax
import jax.numpy as jnp
from jax import lax
from jax.sharding import PartitionSpec as P

ITERS = 8


ridge_weight = 1.0


def kernel_tile(left_points, right_points):
    left_square = jnp.sum(jnp.square(left_points.astype(jnp.float32)), axis=-1)
    right_square = jnp.sum(jnp.square(right_points.astype(jnp.float32)), axis=-1)
    inner = jnp.dot(left_points, right_points.T, preferred_element_type=jnp.float32)
    distance = jnp.maximum(left_square[:, None] + right_square[None, :] - 2.0 * inner, 0.0)
    return jnp.exp(distance * (-2.0 / left_points.shape[-1]))


def diagonal_mask(count, width):
    return (jnp.arange(width)[None, :] == jnp.arange(count)[:, None]).astype(jnp.float32)


def run_chebyshev(matrix, right_side):
    upper = jnp.max(jnp.sum(matrix, axis=2), axis=1)
    center = ((upper + ridge_weight) / 2.0)[:, None, None]
    radius = ((upper - ridge_weight) / 2.0)[:, None, None]
    ratio = center / radius
    factor = 1.0 / ratio
    residual = right_side
    direction = residual / center
    solution = jnp.zeros_like(right_side)
    for iteration in range(ITERS):
        solution = solution + direction
        if iteration < ITERS - 1:
            residual = residual - jnp.einsum(
                "bij,bjc->bic", matrix, direction, precision=lax.Precision.HIGHEST
            )
            following = 1.0 / (2.0 * ratio - factor)
            direction = following * factor * direction + 2.0 * following / radius * residual
            factor = following
    return solution


def on_device(points, gradient, panel_index):
    row_points = lax.all_gather(points, "cols", axis=0, tiled=True)
    row_grads = lax.all_gather(gradient, "cols", axis=0, tiled=True)
    group_rows = row_points.shape[0]
    group_start = lax.axis_index("rows") * group_rows
    indices = panel_index.reshape(-1)
    offset = indices - group_start
    inside = (offset >= 0) & (offset < group_rows)
    clipped = jnp.clip(offset, 0, group_rows - 1)
    picked_points = jnp.where(
        inside[:, None], jnp.take(row_points, clipped, axis=0), jnp.zeros((), jnp.bfloat16)
    )
    picked_grads = jnp.where(inside[:, None], jnp.take(row_grads, clipped, axis=0), 0.0)
    summed_points = lax.psum(picked_points, "rows").astype(jnp.float32)
    summed_grads = lax.psum(picked_grads, "rows")
    chosen = summed_points.astype(jnp.bfloat16)
    blocks = panel_index.shape[0]
    width = panel_index.shape[1]
    targets = summed_grads.shape[1]
    chosen_blocks = chosen.reshape(blocks, width, -1)
    right_side = -summed_grads.reshape(blocks, width, targets)
    matrix = (
        jax.vmap(kernel_tile)(chosen_blocks, chosen_blocks)
        + ridge_weight * diagonal_mask(width, width)[None]
    )
    solution = run_chebyshev(matrix, right_side)
    update = solution.reshape(-1, targets)
    update_half = update.astype(jnp.bfloat16)
    count = gradient.shape[0] * lax.axis_size("cols")
    piece_rows = math.gcd(count, 256)

    def piece_term(number):
        piece_start = number * piece_rows
        block_points = lax.dynamic_slice_in_dim(row_points, piece_start, piece_rows, 0)
        row_ids = group_start + piece_start + jnp.arange(piece_rows, dtype=jnp.int32)
        tile = kernel_tile(block_points, chosen) + ridge_weight * (
            row_ids[:, None] == indices[None, :]
        ).astype(jnp.float32)
        return jnp.dot(tile.astype(jnp.bfloat16), update_half, preferred_element_type=jnp.float32)

    pieces = lax.map(piece_term, jnp.arange(count // piece_rows, dtype=jnp.int32))
    summed = lax.psum_scatter(
        pieces.reshape(count, targets), "cols", scatter_dimension=0, tiled=True
    )
    return (gradient + summed, update)


def solution(mesh):
    in_specs = (P(("rows", "cols"), None), P(("rows", "cols"), None), P("cols", None))
    out_specs = (P(("rows", "cols"), None), P("cols", None))
    return jax.shard_map(
        on_device, mesh=mesh, in_specs=in_specs, out_specs=out_specs, check_vma=False
    )
```

profile of v0, /device:TPU:8, one launch (start us, length us, event | category | flops | bytes accessed | tf_op | source)
XLA Modules:
  0.0 614.6 jit_solution(3024469153142710923)
XLA Ops:
  9.4 29.1 %all-gather.3.cloned.1.call-done = bf16[4096,128]{1,0:T(8,128)(2,1)} async-done(((bf16[512,128]{1,0:T(8,128)(2,1)}), bf16[4096,128]{1,0:T(8,128)(2,1)}) %all-gather.3.cloned.1.call-update) | async-done | bytes 1048592 | tf_op jit(solution)/shard_map/all_gather | solution.py:48
  38.5 7.0 %gather_fusion = bf16[2048,128]{1,0:T(8,128)(2,1)S(1)} fusion(bf16[4096,128]{1,0:T(8,128)(2,1)} %all-gather.3.cloned.1.call-done, s32[2048]{0:T(1024)S(1)} %broadcast_clamp_fusion), kind=kCustom, calls=%fused_computation | custom fusion | bytes 1056768 | tf_op jit(solution)/shard_map/jit(_take)/gather | solution.py:57
  45.5 2.3 select_select_fusion.1
  48.6 2.5 fusion.23
  51.1 144.4 %all-reduce.3.cloned.1.call-done = bf16[2048,128]{1,0:T(8,128)(2,1)} async-done(((bf16[2048,128]{1,0:T(8,128)(2,1)}), bf16[2048,128]{1,0:T(8,128)(2,1)}) %all-reduce.3.cloned.1.call-update) | async-done | bytes 524304 | tf_op jit(solution)/shard_map/psum | solution.py:60
  195.5 1.5 multiply_reduce_fusion.2
  197.0 26.4 %all-gather.5.cloned.1.call-done = f32[4096,128]{1,0:T(8,128)} async-done(((f32[512,128]{1,0:T(8,128)}), f32[4096,128]{1,0:T(8,128)}) %all-gather.5.cloned.1.call-update) | async-done | bytes 2097168 | tf_op jit(solution)/shard_map/all_gather | solution.py:49
  223.4 7.0 %gather_fusion.1 = f32[2048,128]{1,0:T(8,128)S(1)} fusion(f32[4096,128]{1,0:T(8,128)} %all-gather.5.cloned.1.call-done, s32[2048]{0:T(1024)S(1)} %broadcast_clamp_fusion), kind=kCustom, calls=%fused_computation.1 | custom fusion | bytes 2105344 | tf_op jit(solution)/shard_map/jit(_take)/gather | solution.py:59
  230.5 2.4 select_select_fusion
  233.0 6.5 %fusion.42 = (f32[2,1024]{1,0:T(2,128)S(1)}, f32[2,1024,1024]{1,2,0:T(8,128)}) fusion(f32[1024,1024]{0,1:T(8,128)} %fusion.23, bf16[2,1024,128]{2,1,0:T(8,128)(2,1)S(1)} %bitcast.50, f32[2,1024]{1,0:T(2,128)S(1)} %add.225), kind=kOutput, calls=%fused_computation.88 | convolution fusion | flops 551548928 | bytes 13123584 | tf_op jit(solution)/shard_map/vmap()/dot_general | solution.py:17
  239.6 143.0 %all-reduce.5.cloned.1.call-done = f32[2048,128]{1,0:T(8,128)} async-done(((f32[2048,128]{1,0:T(8,128)}), f32[2048,128]{1,0:T(8,128)}) %all-reduce.5.cloned.1.call-update) | async-done | bytes 1048592 | tf_op jit(solution)/shard_map/psum | solution.py:61
  382.7 1.4 neg.6
  384.1 17.0 %convolution_subtract_fusion.6 = f32[2,1024,128]{2,1,0:T(8,128)S(1)} fusion(f32[2,1024,128]{2,1,0:T(8,128)S(1)} %bitcast.51, f32[2,1024,1024]{1,2,0:T(8,128)} %get-tuple-element.88, f32[2]{0:T(128)S(1)} %get-tuple-element.86), kind=kOutput, calls=%fused_computation.40 | convolution fusion | flops 3221749760 | bytes 10485768 | tf_op jit(solution)/shard_map/bij,bjc->bic/dot_general | solution.py:38
  401.1 13.9 %multiply_add_fusion.3 = (f32[2,1024,128]{2,1,0:T(8,128)S(1)}, f32[2,1024,128]{2,1,0:T(8,128)S(1)}) fusion(f32[2,1024,128]{2,1,0:T(8,128)S(1)} %convolution_subtract_fusion.6, f32[2]{0:T(128)S(1)} %get-tuple-element.81, f32[2]{0:T(128)S(1)} %get-tuple-element.82, f32[2]{0:T(128)S(1)} %get-tuple-element.83, f32[2]{0:T(128)S(1)} %get-tuple-element.84, ...), kind=kOutput, calls=%fused_computation.47 | convolution fusion | flops 3224371200 | bytes 12582952 | tf_op jit(solution)/shard_map/bij,bjc->bic/dot_general | solution.py:38
  414.9 13.8 %convolution_subtract_fusion.4 = f32[2,1024,128]{2,1,0:T(8,128)S(1)} fusion(f32[2,1024,128]{2,1,0:T(8,128)S(1)} %get-tuple-element.90, f32[2,1024,1024]{1,2,0:T(8,128)S(1)} %copy-done, f32[2,1024,128]{2,1,0:T(8,128)S(1)} %get-tuple-element.89), kind=kOutput, calls=%fused_computation.38 | convolution fusion | flops 3221487616 | bytes 11534336 | tf_op jit(solution)/shard_map/bij,bjc->bic/dot_general | solution.py:38
  428.7 14.0 %convolution_subtract_fusion.3 = f32[2,1024,128]{2,1,0:T(8,128)S(1)} fusion(f32[2,1024,128]{2,1,0:T(8,128)S(1)} %convolution_subtract_fusion.4, f32[2,1024,1024]{1,2,0:T(8,128)S(1)} %copy-done, f32[2,1024,128]{2,1,0:T(8,128)S(1)} %get-tuple-element.89, f32[2]{0:T(128)S(1)} %get-tuple-element.75, f32[2]{0:T(128)S(1)} %get-tuple-element.80), kind=kOutput, calls=%fused_computation.37 | convolution fusion | flops 3222274048 | bytes 11534352 | tf_op jit(solution)/shard_map/bij,bjc->bic/dot_general | solution.py:38
  442.7 13.7 %convolution_subtract_fusion.2 = f32[2,1024,128]{2,1,0:T(8,128)S(1)} fusion(f32[2,1024,128]{2,1,0:T(8,128)S(1)} %convolution_subtract_fusion.3, f32[2,1024,1024]{1,2,0:T(8,128)S(1)} %copy-done, f32[2]{0:T(128)S(1)} %get-tuple-element.77, f32[2]{0:T(128)S(1)} %get-tuple-element.76, f32[2,1024,128]{2,1,0:T(8,128)S(1)} %convolution_subtract_fusion.4, ...), kind=kOutput, calls=%fused_computation.36 | convolution fusion | flops 3223060480 | bytes 12582944 | tf_op jit(solution)/shard_map/bij,bjc->bic/dot_general | solution.py:38
  456.4 13.8 %convolution_subtract_fusion.1 = f32[2,1024,128]{2,1,0:T(8,128)S(1)} fusion(f32[2,1024,128]{2,1,0:T(8,128)S(1)} %convolution_subtract_fusion.2, f32[2,1024,1024]{1,2,0:T(8,128)S(1)} %copy-done, f32[2]{0:T(128)S(1)} %get-tuple-element.79, f32[2]{0:T(128)S(1)} %get-tuple-element.78, f32[2,1024,128]{2,1,0:T(8,128)S(1)} %convolution_subtract_fusion.3, ...), kind=kOutput, calls=%fused_computation.35 | convolution fusion | flops 3223846912 | bytes 13631536 | tf_op jit(solution)/shard_map/bij,bjc->bic/dot_general | solution.py:38
  470.2 15.1 %fusion.26 = f32[2,1024,128]{2,1,0:T(8,128)S(1)} fusion(f32[2,1024,128]{2,1,0:T(8,128)S(1)} %convolution_subtract_fusion.1, f32[2,1024,1024]{1,2,0:T(8,128)S(1)} %copy-done, f32[2,1024,128]{2,1,0:T(8,128)S(1)} %get-tuple-element.89, f32[2,1024,128]{2,1,0:T(8,128)S(1)} %convolution_subtract_fusion.2, f32[2,1024,128]{2,1,0:T(8,128)S(1)} %convolution_subtract_fusion.6, ...), kind=kOutput, calls=%fused_computation.34 | convolution fusion | flops 3231449088 | bytes 16777320 | tf_op jit(solution)/shard_map/bij,bjc->bic/dot_general | solution.py:38
  486.2 84.6 %while.10 = (s32[]{:T(128)}, f32[16,256,128]{2,1,0:T(8,128)}, s32[16]{0:T(128)S(1)}, bf16[4096,128]{1,0:T(8,128)(2,1)}, bf16[2048,128]{1,0:T(8,128)(2,1)S(1)}, /...) while((s32[]{:T(128)}, f32[16,256,128]{2,1,0:T(8,128)}, ...), condition=%wide.region_8.9_spmd, body=%wide.region_5.8_spmd.sunk | while | flops 274036736 | bytes 1880775 | solution.py:87
  487.6 1.0 multiply_reduce_fusion.6
  488.9 2.6 fusion.62
  492.9 1.0 multiply_reduce_fusion.6
  494.2 2.6 fusion.62
  498.2 1.0 multiply_reduce_fusion.6
  499.5 2.6 fusion.62
  503.5 1.0 multiply_reduce_fusion.6
  504.8 2.6 fusion.62
  508.8 1.0 multiply_reduce_fusion.6
  510.1 2.6 fusion.62
  515.4 2.6 fusion.62
  519.4 1.0 multiply_reduce_fusion.6
  520.7 2.6 fusion.62
  526.0 2.6 fusion.62
  531.3 2.6 fusion.62
  535.2 1.0 multiply_reduce_fusion.6
  536.5 2.6 fusion.62
  540.5 1.0 multiply_reduce_fusion.6
  541.8 2.6 fusion.62
  545.8 1.0 multiply_reduce_fusion.6
  547.1 2.6 fusion.62
  552.4 2.6 fusion.62
  557.7 2.6 fusion.62
  561.6 1.0 multiply_reduce_fusion.6
  563.0 2.6 fusion.62
  568.3 2.6 fusion.62
  570.9 35.1 %reduce-scatter.2.cloned.1.call-done = f32[512,128]{1,0:T(8,128)} async-done(((f32[4096,128]{1,0:T(8,128)}), f32[512,128]{1,0:T(8,128)}) %reduce-scatter.2.cloned.1.call-update) | async-done | bytes 262160 | tf_op jit(solution)/shard_map/reduce_scatter | solution.py:88
  606.0 1.7 add.246
  (105 shorter events, 26.2 us)
Async XLA Ops:
  7.2 31.3 %all-gather.3.cloned.1.call-start = ((), (), s32[]{:S(2)}) async-start(), calls=%async_computation.1 | async-start | bytes 1179648 | tf_op jit(solution)/shard_map/all_gather | solution.py:48
  7.9 187.6 %all-reduce.3.cloned.1.call-start = ((), (), s32[]{:S(2)}) async-start(), calls=%async_computation.2 | async-start | bytes 1048576 | tf_op jit(solution)/shard_map/psum | solution.py:60
  47.8 175.6 %all-gather.5.cloned.1.call-start = ((), (), s32[]{:S(2)}) async-start(), calls=%async_computation.3 | async-start | bytes 2359296 | tf_op jit(solution)/shard_map/all_gather | solution.py:49
  48.5 334.1 %all-reduce.5.cloned.1.call-start = ((), (), s32[]{:S(2)}) async-start(), calls=%async_computation.4 | async-start | bytes 2097152 | tf_op jit(solution)/shard_map/psum | solution.py:61
  195.5 37.5 %copy-start.1 = (bf16[2048,128]{1,0:T(8,128)(2,1)S(1)}, bf16[2048,128]{1,0:T(8,128)(2,1)}, u32[]{:S(2)}) copy-start(bf16[2048,128]{1,0:T(8,128)(2,1)} %all-reduce.3.cloned.1.call-done) | copy-start | bytes 1572868
  232.9 373.0 %reduce-scatter.2.cloned.1.call-start = ((), (), s32[]{:S(2)}) async-start(), calls=%async_computation.5 | async-start | bytes 2359296 | tf_op jit(solution)/shard_map/reduce_scatter | solution.py:88
  382.7 18.4 %copy-start = (f32[2,1024,1024]{1,2,0:T(8,128)S(1)}, f32[2,1024,1024]{1,2,0:T(8,128)}, u32[]{:S(2)}) copy-start(f32[2,1024,1024]{1,2,0:T(8,128)} %get-tuple-element.88) | copy-start | bytes 25165828
  470.2 15.2 %copy-start.4 = (s32[2,1024]{1,0:T(2,128)S(1)}, s32[2,1024]{1,0:T(2,128)}, u32[]{:S(2)}) copy-start(s32[2,1024]{1,0:T(2,128)} %param.7) | copy-start | bytes 24580
  485.3 1.0 copy-start.2
  485.4 120.6 %copy-start.3 = (f32[512,128]{1,0:T(8,128)S(1)}, f32[512,128]{1,0:T(8,128)}, u32[]{:S(2)}) copy-start(f32[512,128]{1,0:T(8,128)} %param.6) | copy-start | bytes 786436
Sparse Core Ops, SparseCore 0:
  9.8 28.6 all-gather.2
  47.9 147.5 all-reduce.2
  197.4 26.0 all-gather.4
  233.0 149.5 all-reduce.4
  571.0 34.8 reduce-scatter.1
where the time goes:
time: 624 us; the launch traced here: 615 us
  waiting for transfers between devices  379 us (61%)
  matrix products  149 us (24%)
  other arithmetic  34.3 us (5%)
  local copies, waits for them, and re-layouts  25.6 us (4%)
  between operations  14.4 us (2%)
  loops' own time  11.7 us (2%)
    psum x1, waiting for transfers between devices, on_device(): summed_points = lax.psum(picked_points, 'rows').astype(jnp.float32)  144 us
    psum x1, waiting for transfers between devices, on_device(): summed_grads = lax.psum(picked_grads, 'rows')  143 us
    dot_general x7, matrix products, run_chebyshev(): jnp.einsum('bij,bjc->bic', matrix, direction, precision=lax.Precision.HIG...  101 us
    dot_general x16, matrix products, piece_term(): jnp.dot(tile.astype(jnp.bfloat16), update_half, preferred_element_type=jn...  41.4 us
    reduce_scatter x1, waiting for transfers between devices, on_device(): lax.psum_scatter(pieces.reshape(count, targets), 'cols', scatter_dimensio...  35.1 us
    all_gather x1, waiting for transfers between devices, on_device(): row_points = lax.all_gather(points, 'cols', axis=0, tiled=True)  29.1 us
    all_gather x1, waiting for transfers between devices, on_device(): row_grads = lax.all_gather(gradient, 'cols', axis=0, tiled=True)  26.4 us
    reduce_sum x17, other arithmetic, kernel_tile(): left_square = jnp.sum(jnp.square(left_points.astype(jnp.float32)), axis=-1)  16.7 us
  transfers between devices with their start and end apart: 5, of which 5 were waited for; matrix products, arithmetic and copies ran while one was open for 2% of the time, Pallas kernels for 0%

commit v1 on v0

v1 whole, which is shorter than its diff:
```python
import functools

import jax
import jax.numpy as jnp
from jax import lax
from jax.experimental import pallas as pl
from jax.experimental.pallas import tpu as pltpu
from jax.sharding import Mesh
from jax.sharding import PartitionSpec as P

ITERS = 8
RIDGE = 1.0
LOG2E = 1.4426950408889634
ROWS = ("z", "y")
DEVICES = ("z", "y", "x", "k")
TRANSPOSED = (((1,), (1,)), ((), ()))


def solve_kernel(points_ref, column_ref, row_ref, right_ref, update_ref, high_ref, low_ref):
    width = points_ref.shape[0]
    scale = -2.0 / points_ref.shape[1] * LOG2E
    step = 256
    upper = jnp.zeros((1, 1), jnp.float32)
    for start in range(0, width, step):
        piece = pl.ds(start, step)
        inner = lax.dot_general(
            points_ref[piece, :], points_ref[...], TRANSPOSED, preferred_element_type=jnp.float32
        )
        distance = jnp.maximum(column_ref[piece, :] + row_ref[...] - 2.0 * inner, 0.0)
        values = jnp.exp2(distance * scale)
        sums = jnp.sum(values, axis=1, keepdims=True)
        upper = jnp.maximum(upper, jnp.max(sums, axis=0, keepdims=True))
        high = values.astype(jnp.bfloat16)
        high_ref[piece, :] = high
        low_ref[piece, :] = (values - high.astype(jnp.float32)).astype(jnp.bfloat16)
    upper = upper + RIDGE
    center = (upper + RIDGE) / 2.0
    radius = (upper - RIDGE) / 2.0
    ratio = center / radius
    factor = 1.0 / ratio
    residual = right_ref[...]
    targets = residual.shape[0]
    direction = residual / center
    update = jnp.zeros_like(residual)
    for iteration in range(ITERS):
        update = update + direction
        if iteration < ITERS - 1:
            high = direction.astype(jnp.bfloat16)
            low = (direction - high.astype(jnp.float32)).astype(jnp.bfloat16)
            both = jnp.concatenate([high, low], axis=0)
            main = jnp.dot(both, high_ref[...], preferred_element_type=jnp.float32)
            rest = jnp.dot(high, low_ref[...], preferred_element_type=jnp.float32)
            product = main[:targets] + (main[targets:] + rest)
            residual = residual - (product + RIDGE * direction)
            following = 1.0 / (2.0 * ratio - factor)
            direction = following * factor * direction + 2.0 * following / radius * residual
            factor = following
    update_ref[...] = update


def solve(points, right_side):
    width, _ = points.shape
    squares = jnp.sum(jnp.square(points.astype(jnp.float32)), axis=-1)
    return pl.pallas_call(
        solve_kernel,
        out_shape=jax.ShapeDtypeStruct(right_side.shape, jnp.float32),
        in_specs=[pl.BlockSpec(memory_space=pltpu.VMEM)] * 4,
        out_specs=pl.BlockSpec(memory_space=pltpu.VMEM),
        scratch_shapes=[pltpu.VMEM((width, width), jnp.bfloat16)] * 2,
        compiler_params=pltpu.CompilerParams(vmem_limit_bytes=40 << 20),
        name="solve",
    )(points, squares[:, None], squares[None, :], right_side)


def change_kernel(points_ref, column_ref, ids_ref, chosen_ref, row_ref, panel_ref, update_ref, out_ref):
    scale = -2.0 / points_ref.shape[1] * LOG2E
    step = 512
    total = jnp.zeros(out_ref.shape, jnp.float32)
    for start in range(0, chosen_ref.shape[0], step):
        piece = pl.ds(start, step)
        inner = lax.dot_general(
            points_ref[...], chosen_ref[piece, :], TRANSPOSED, preferred_element_type=jnp.float32
        )
        distance = jnp.maximum(column_ref[...] + row_ref[:, piece] - 2.0 * inner, 0.0)
        values = jnp.exp2(distance * scale)
        values = jnp.where(ids_ref[...] == panel_ref[:, piece], values + RIDGE, values)
        total = total + lax.dot_general(
            values.astype(jnp.bfloat16),
            update_ref[:, piece],
            TRANSPOSED,
            preferred_element_type=jnp.float32,
        )
    out_ref[...] = total


def change(points, ids, chosen, panel, update):
    count, features = points.shape
    width = chosen.shape[0]
    targets = update.shape[0]
    block = 256
    point_squares = jnp.sum(jnp.square(points.astype(jnp.float32)), axis=-1)
    panel_squares = jnp.sum(jnp.square(chosen.astype(jnp.float32)), axis=-1)
    return pl.pallas_call(
        change_kernel,
        grid=(count // block,),
        out_shape=jax.ShapeDtypeStruct((count, targets), jnp.float32),
        in_specs=[
            pl.BlockSpec((block, features), lambda i: (i, 0)),
            pl.BlockSpec((block, 1), lambda i: (i, 0)),
            pl.BlockSpec((block, 1), lambda i: (i, 0)),
            pl.BlockSpec((width, features), lambda i: (0, 0)),
            pl.BlockSpec((1, width), lambda i: (0, 0)),
            pl.BlockSpec((1, width), lambda i: (0, 0)),
            pl.BlockSpec((targets, width), lambda i: (0, 0)),
        ],
        out_specs=pl.BlockSpec((block, targets), lambda i: (i, 0)),
        compiler_params=pltpu.CompilerParams(vmem_limit_bytes=40 << 20),
        name="change",
    )(points, point_squares[:, None], ids[:, None], chosen, panel_squares[None, :], panel[None, :], update)


def spread(piece, axes):
    count = lax.axis_size(axes)
    return lax.all_to_all(jnp.broadcast_to(piece[None], (count, *piece.shape)), axes, 0, 0)


def on_device(points, gradient, panel_index):
    own, features = points.shape
    targets = gradient.shape[1]
    blocks, width = panel_index.shape
    xs, ks = lax.axis_size("x"), lax.axis_size("k")
    rows = lax.axis_size(ROWS)
    row = lax.axis_index(ROWS)
    core = lax.axis_index("k")
    group = own * xs * ks

    core_points = lax.all_gather(points, "x")
    row_points = lax.all_gather(core_points, "k", axis=1).reshape(group, features)
    core_grads = lax.all_gather(gradient, "x")
    row_grads = lax.all_gather(core_grads, "k", axis=1).reshape(group, targets)

    indices = panel_index.reshape(-1)
    offset = indices - row * group
    inside = ((offset >= 0) & (offset < group))[:, None]
    clipped = jnp.clip(offset, 0, group - 1)
    picked_points = jnp.where(inside, jnp.take(row_points, clipped, axis=0), jnp.zeros((), jnp.bfloat16))
    picked_grads = jnp.where(inside, jnp.take(row_grads, clipped, axis=0), 0.0)

    shard = blocks * width
    pieces = lax.all_to_all(picked_points.reshape(rows, shard // rows, features), ROWS, 0, 0)
    piece = jnp.sum(pieces.astype(jnp.float32), axis=0).astype(jnp.bfloat16)
    chosen = spread(piece, ROWS).reshape(shard, features)

    groups = rows // blocks
    slices = picked_grads.T.reshape(groups, targets // groups, blocks, width)
    slices = slices.transpose(0, 2, 1, 3).reshape(rows, targets // groups, width)
    right_side = -jnp.sum(lax.all_to_all(slices, ROWS, 0, 0), axis=0)

    own_block = lax.dynamic_index_in_dim(chosen.reshape(blocks, width, features), row % blocks, 0, False)
    solved = solve(own_block, right_side)
    half = spread(solved.astype(jnp.bfloat16), ROWS)
    half = half.reshape(groups, blocks, targets // groups, width).transpose(0, 2, 1, 3)
    half = half.reshape(targets, shard)

    both_chosen = lax.all_gather(chosen, "k", axis=0, tiled=True)
    both_panel = lax.all_gather(indices, "k", axis=0, tiled=True)
    both_half = lax.all_gather(half, "k", axis=1, tiled=True)
    ids = row * group + core * own
    ids = ids + ks * own * jnp.arange(xs, dtype=jnp.int32)[:, None] + jnp.arange(own, dtype=jnp.int32)[None, :]
    term = change(core_points.reshape(xs * own, features), ids.reshape(-1), both_chosen, both_panel, both_half)
    terms = lax.all_to_all(term.reshape(xs, own, targets), "x", 0, 0)
    new_gradient = gradient + jnp.sum(terms, axis=0)

    full = spread(solved, ROWS).reshape(groups, blocks, targets // groups, width)
    update = full.transpose(1, 3, 0, 2).reshape(shard, targets)
    return new_gradient, update


def solution(mesh):
    fine = Mesh(mesh.devices.reshape(8, 4, 4, 2), DEVICES)
    in_specs = (P(DEVICES, None), P(DEVICES, None), P(("x", "k"), None))
    out_specs = (P(DEVICES, None), P(("x", "k"), None))
    return jax.shard_map(on_device, mesh=fine, in_specs=in_specs, out_specs=out_specs, check_vma=False)
```

time: 624 us -> 243 us (0.39); the launches traced: 615 us -> 242 us
  waiting for transfers between devices: 379 us -> 105 us
  matrix products: 149 us -> 0 us
  blocking collectives: 0 us -> 44.1 us
  other arithmetic: 34.3 us -> 6.35 us
  starting transfers between devices: 0.2 us -> 26.9 us
  Pallas kernels: 0 us -> 19.7 us
  loops' own time: 11.7 us -> 0 us
    psum x2 -> x0, waiting for transfers between devices: 287 us -> none  [the longest x1 144 us: on_device(): summed_points = lax.psum(picked_points, 'rows').astype(jnp.float32)]
    dot_general x24 -> x0, matrix products: 149 us -> none  [the longest x7 101 us: run_chebyshev(): jnp.einsum('bij,bjc->bic', matrix, direction, precision=lax.Precision.HIG...]
    all_to_all x0 -> x5, waiting for transfers between devices: none -> 60.4 us  [the longest x1 26.7 us: on_device(): right_side = -jnp.sum(lax.all_to_all(slices, ROWS, 0, 0), axis=0)]
    reduce_scatter x1 -> x0, waiting for transfers between devices: 35.1 us -> none  [on_device(): lax.psum_scatter(pieces.reshape(count, targets), 'cols', scatter_dimensio...]
    all_to_all x0 -> x1, blocking collectives: none -> 27.2 us  [on_device(): lax.all_to_all(picked_points.reshape(rows, shard // rows, features), ROWS...]
    all_to_all x0 -> x5, starting transfers between devices: none -> 26.7 us  [the longest x3 16.9 us: spread(): lax.all_to_all(jnp.broadcast_to(piece[None], (count, *piece.shape)), axes...]
    pallas_call x0 -> x2, Pallas kernels: none -> 19.7 us  [the longest x1 14.3 us: change(): pl.pallas_call(change_kernel, grid=(count // block,), out_shape=jax.Shape...]
    reduce_sum x33 -> x6, other arithmetic: 22.2 us -> 2.63 us  [the longest x1 1.84 us: change(): panel_squares = jnp.sum(jnp.square(chosen.astype(jnp.float32)), axis=-1)]
  transfers between devices with their start and end apart: 5 -> 10, of which waited for: 5 -> 7; matrix products, arithmetic and copies ran while one was open for 2% -> 11% of each run, Pallas kernels for 0% -> 6%
where the time goes in v1:
time: 243 us; the launch traced here: 242 us
  waiting for transfers between devices  105 us (43%)
  blocking collectives  44.1 us (18%)
  starting transfers between devices  26.9 us (11%)
  local copies, waits for them, and re-layouts  25.6 us (11%)
  Pallas kernels  19.7 us (8%)
  between operations  14.1 us (6%)
  other arithmetic  6.35 us (3%)
    all_to_all x1, blocking collectives, on_device(): lax.all_to_all(picked_points.reshape(rows, shard // rows, features), ROWS...  27.2 us
    all_to_all x1, waiting for transfers between devices, on_device(): right_side = -jnp.sum(lax.all_to_all(slices, ROWS, 0, 0), axis=0)  26.7 us
    all_to_all x3, waiting for transfers between devices, spread(): lax.all_to_all(jnp.broadcast_to(piece[None], (count, *piece.shape)), axes...  20.6 us
    all_to_all x3, starting transfers between devices, spread(): lax.all_to_all(jnp.broadcast_to(piece[None], (count, *piece.shape)), axes...  16.9 us
    all_gather x1, waiting for transfers between devices, on_device(): lax.all_gather(core_points, 'k', axis=1).reshape(group, features)  16.3 us
    all_gather x1, waiting for transfers between devices, on_device(): core_grads = lax.all_gather(gradient, 'x')  15 us
    all_gather x1, blocking collectives, on_device(): core_points = lax.all_gather(points, 'x')  14.8 us
    pallas_call x1, Pallas kernels, change(): pl.pallas_call(change_kernel, grid=(count // block,), out_shape=jax.Shape...  14.3 us
  transfers between devices with their start and end apart: 10, of which 7 were waited for; matrix products, arithmetic and copies ran while one was open for 11% of the time, Pallas kernels for 6%

profile of v1, /device:TPU:8, one launch (start us, length us, event | category | flops | bytes accessed | tf_op | source)
XLA Modules:
  0.0 242.1 jit_solution(12150781044096784405)
XLA Ops:
  7.2 0.7 all-gather.16.cloned.1.call-update
  8.0 14.8 %all-gather.points_ref = bf16[2048,128]{1,0:T(8,128)(2,1)} all-gather(bf16[512,128]{1,0:T(8,128)(2,1)} %param.3), channel_id=2, replica_groups=mesh['z'=8,'y'=4,'x'=4,'k'=2] {'x'}, dimensions={0}, use_global_device_ids=true | all-gather | bytes 655360 | tf_op jit(solution)/shard_map/all_gather | solution.py:137
  22.9 0.7 fusion
  23.6 0.7 subtract_clamp_fusion
  24.3 15.0 %all-gather.16.cloned.1.call-done = f32[2048,128]{1,0:T(8,128)} async-done(((f32[512,128]{1,0:T(8,128)}), f32[2048,128]{1,0:T(8,128)}) %all-gather.16.cloned.1.call-update) | async-done | bytes 1048592 | tf_op jit(solution)/shard_map/all_gather | solution.py:139
  39.4 0.1 min.20
  39.5 0.1 and.34
  39.6 16.3 %all-gather.14.cloned.1.call-done = bf16[4,1024,128]{2,1,0:T(8,128)(2,1)} async-done(((bf16[4,512,128]{2,1,0:T(8,128)(2,1)}), bf16[4,1024,128]{2,1,0:T(8,128)(2,1)}) %all-gather.14.cloned.1.call-update) | async-done | bytes 1048592 | tf_op jit(solution)/shard_map/all_gather | solution.py:138
  55.9 7.0 %gather_fusion = bf16[2048,128]{1,0:T(8,128)(2,1)S(1)} fusion(bf16[4096,128]{1,0:T(8,128)(2,1)} %bitcast.61, s32[2048]{0:T(1024)S(1)} %broadcast_clamp_fusion), kind=kCustom, calls=%fused_computation | custom fusion | bytes 1056768 | tf_op jit(solution)/shard_map/jit(_take)/gather | solution.py:146
  62.9 0.7 select_select_fusion
  63.6 27.2 %all_to_all.30 = bf16[32,64,128]{2,1,0:T(8,128)(2,1)S(1)} all-to-all(bf16[32,64,128]{2,1,0:T(8,128)(2,1)S(1)} %select_select_fusion), channel_id=1, replica_groups=mesh['z'=8,'y'=4,'x'=4,'k'=2] {'z','y'}, dimensions={0} | all-to-all | bytes 1048576 | tf_op jit(solution)/shard_map/all_to_all | solution.py:150
  90.8 0.1 reduce_sum.58
  90.9 0.9 broadcast_in_dim.85
  91.8 5.6 %all-to-all-start.1 = ((bf16[32,64,128]{2,1,0:T(8,128)(2,1)}), bf16[32,64,128]{2,1,0:T(8,128)(2,1)S(1)}, u32[]{:S(2)}, u32[]{:S(2)}) async-start(bf16[32,64,128]{2,1,0:T(8,128)(2,1)} %broadcast_in_dim.85), calls=%async_computation.1 | async-start | bytes 1048576 | tf_op jit(solution)/shard_map/all_to_all | solution.py:124
  97.5 7.1 %gather_fusion.1 = f32[2048,128]{1,0:T(8,128)S(1)} fusion(f32[4096,128]{1,0:T(8,128)} %bitcast.60, s32[2048]{0:T(1024)S(1)} %broadcast_clamp_fusion), kind=kCustom, calls=%fused_computation.1 | custom fusion | bytes 2105344 | tf_op jit(solution)/shard_map/jit(_take)/gather | solution.py:147
  104.5 0.7 select_bitcast_fusion
  105.2 0.3 copy.11
  105.6 0.9 reshape.141
  106.5 1.3 copy.12
  107.8 5.7 %all-to-all-done.1 = bf16[32,64,128]{2,1,0:T(8,128)(2,1)S(1)} async-done(((bf16[32,64,128]{2,1,0:T(8,128)(2,1)}), bf16[32,64,128]{2,1,0:T(8,128)(2,1)S(1)}, u32[]{:S(2)}, u32[]{:S(2)}) %all-to-all-start.1) | async-done | bytes 524320 | tf_op jit(solution)/shard_map/all_to_all | solution.py:124
  113.5 5.6 %all-to-all-start.2 = ((f32[32,8,1024]{2,1,0:T(8,128)}), f32[32,8,1024]{2,1,0:T(8,128)S(1)}, u32[]{:S(2)}, u32[]{:S(2)}) async-start(f32[32,8,1024]{2,1,0:T(8,128)} %bitcast.15), calls=%async_computation.2 | async-start | bytes 2097152 | tf_op jit(solution)/shard_map/all_to_all | solution.py:157
  119.1 0.2 multiply_reduce_fusion.2
  119.3 0.2 copy.13.column_ref
  119.5 26.7 %all-to-all-done.2 = f32[32,8,1024]{2,1,0:T(8,128)S(1)} async-done(((f32[32,8,1024]{2,1,0:T(8,128)}), f32[32,8,1024]{2,1,0:T(8,128)S(1)}, u32[]{:S(2)}, u32[]{:S(2)}) %all-to-all-start.2) | async-done | bytes 1048608 | tf_op jit(solution)/shard_map/all_to_all | solution.py:157
  146.3 0.1 reduce_sum.61
  146.3 5.4 %solve.1 = f32[8,1024]{1,0:T(8,128)S(1)} custom-call(bf16[1024,128]{1,0:T(8,128)(2,1)S(1)} %get-tuple-element.7.points_ref, f32[1024,1]{1,0:T(8,128)S(1)} %copy.13.column_ref, f32[1,1024]{1,0:T(1,128)S(1)} %bitcast.59, f32[8,1024]{1,0:T(8,128)S(1)} %neg.3.right_ref), custom_call_target="tpu_custom_call" | custom-call | tf_op jit(solution)/shard_map/solve/pallas_call | solution.py:64
  151.8 0.9 broadcast_in_dim.94
  152.6 5.6 %all-to-all-start.3 = ((bf16[32,8,1024]{2,1,0:T(8,128)(2,1)}), bf16[32,8,1024]{2,1,0:T(8,128)(2,1)S(1)}, u32[]{:S(2)}, u32[]{:S(2)}) async-start(bf16[32,8,1024]{2,1,0:T(8,128)(2,1)} %broadcast_in_dim.94), calls=%async_computation.3 | async-start | bytes 1048576 | tf_op jit(solution)/shard_map/all_to_all | solution.py:124
  158.3 0.5 all-gather.10.cloned.1.call-update
  158.8 15.0 %all-to-all-done.3 = bf16[32,8,1024]{2,1,0:T(8,128)(2,1)S(1)} async-done(((bf16[32,8,1024]{2,1,0:T(8,128)(2,1)}), bf16[32,8,1024]{2,1,0:T(8,128)(2,1)S(1)}, u32[]{:S(2)}, u32[]{:S(2)}) %all-to-all-start.3) | async-done | bytes 524320 | tf_op jit(solution)/shard_map/all_to_all | solution.py:124
  173.8 1.1 broadcast_in_dim.95
  174.9 5.8 %all-to-all-start.5 = ((f32[32,8,1024]{2,1,0:T(8,128)}), f32[32,8,1024]{2,1,0:T(8,128)}, u32[]{:S(2)}, u32[]{:S(2)}) async-start(f32[32,8,1024]{2,1,0:T(8,128)} %broadcast_in_dim.95), calls=%async_computation.5 | async-start | bytes 2097152 | tf_op jit(solution)/shard_map/all_to_all | solution.py:124
  180.7 0.5 all-gather.12.cloned.1.call-update
  181.3 0.1 add_bitcast_fusion
  181.4 0.4 copy.20
  181.8 0.4 multiply_reduce_fusion.1
  182.1 0.4 copy.18
  182.5 2.0 all_gather.38
  184.5 1.8 multiply_reduce_fusion
  186.4 11.9 %all-gather.12.cloned.1.call-done.update_ref = bf16[128,4096]{1,0:T(8,128)(2,1)} async-done(((bf16[128,2048]{1,0:T(8,128)(2,1)}), bf16[128,4096]{1,0:T(8,128)(2,1)}) %all-gather.12.cloned.1.call-update) | async-done | bytes 1048592 | tf_op jit(solution)/shard_map/all_gather | solution.py:167
  198.3 1.2 copy-done.1
  199.5 1.2 copy-done.2
  200.7 14.3 %change.1 = f32[2048,128]{1,0:T(8,128)} custom-call(bf16[2048,128]{1,0:T(8,128)(2,1)S(1)} %copy-done, f32[2048,1]{1,0:T(8,128)S(1)} %bitcast.55, s32[2048,1]{1,0:T(8,128)S(1)} %bitcast.54, bf16[4096,128]{1,0:T(8,128)(2,1)S(1)} %copy-done.1, f32[1,4096]{1,0:T(1,128)S(1)} %bitcast.56, s32[1,4096]{1,0:T(1,128)S(1)} %bitcast.57, bf16[128,4096]{1,0:T(8,128)(2,1)S(1)} %copy-done.2), custom_call_target="tpu_custom_call" | custom-call | tf_op jit(solution)/shard_map/change/pallas_call | solution.py:103
  215.0 4.2 %all-to-all-start.4 = ((f32[4,512,128]{2,1,0:T(8,128)}), f32[4,512,128]{2,1,0:T(8,128)S(1)}, u32[]{:S(2)}, u32[]{:S(2)}) async-start(f32[4,512,128]{2,1,0:T(8,128)} %bitcast.19), calls=%async_computation.4 | async-start | bytes 2097152 | tf_op jit(solution)/shard_map/all_to_all | solution.py:171
  219.2 2.6 %copy.16 = f32[2048,128]{1,0:T(8,128)} copy(f32[2048,128]{0,1:T(8,128)} %bitcast.22) | data formatting | bytes 2097152
  221.8 13.0 %all-to-all-done.4 = f32[4,512,128]{2,1,0:T(8,128)S(1)} async-done(((f32[4,512,128]{2,1,0:T(8,128)}), f32[4,512,128]{2,1,0:T(8,128)S(1)}, u32[]{:S(2)}, u32[]{:S(2)}) %all-to-all-start.4) | async-done | bytes 1048608 | tf_op jit(solution)/shard_map/all_to_all | solution.py:171
  234.8 0.1 reduce_sum.62
  234.9 0.7 add.88
  (34 shorter events, 0.4 us)
Async XLA Ops:
  7.2 32.2 %copy-start.6 = (s32[2,1024]{1,0:T(2,128)S(1)}, s32[2,1024]{1,0:T(2,128)}, u32[]{:S(2)}) copy-start(s32[2,1024]{1,0:T(2,128)} %param.5) | copy-start | bytes 24580
  7.2 32.2 %all-gather.16.cloned.1.call-start = ((), (), s32[]{:S(2)}) async-start(), calls=%async_computation.9 | async-start | bytes 1310720 | tf_op jit(solution)/shard_map/all_gather | solution.py:139
  7.9 48.0 %all-gather.14.cloned.1.call-start = ((), (), s32[]{:S(2)}) async-start(), calls=%async_computation.8 | async-start | bytes 1572864 | tf_op jit(solution)/shard_map/all_gather | solution.py:138
  22.8 74.6 %all-gather.18.cloned.1.call-start = ((), (), s32[]{:S(2)}) async-start(), calls=%async_computation.10 | async-start | bytes 3145728 | tf_op jit(solution)/shard_map/all_gather | solution.py:140
  91.8 21.6 %all-to-all-start.1 = ((bf16[32,64,128]{2,1,0:T(8,128)(2,1)}), bf16[32,64,128]{2,1,0:T(8,128)(2,1)S(1)}, u32[]{:S(2)}, u32[]{:S(2)}) async-start(bf16[32,64,128]{2,1,0:T(8,128)(2,1)} %broadcast_in_dim.85), calls=%async_computation.1 | async-start | bytes 1048576 | tf_op jit(solution)/shard_map/all_to_all | solution.py:124
  113.5 32.9 %copy-start.3 = (bf16[32,64,128]{2,1,0:T(8,128)(2,1)}, bf16[32,64,128]{2,1,0:T(8,128)(2,1)S(1)}, u32[]{:S(2)}) copy-start(bf16[32,64,128]{2,1,0:T(8,128)(2,1)S(1)} %all-to-all-done.1) | copy-start | bytes 1572868
  113.5 32.8 %all-to-all-start.2 = ((f32[32,8,1024]{2,1,0:T(8,128)}), f32[32,8,1024]{2,1,0:T(8,128)S(1)}, u32[]{:S(2)}, u32[]{:S(2)}) async-start(f32[32,8,1024]{2,1,0:T(8,128)} %bitcast.15), calls=%async_computation.2 | async-start | bytes 2097152 | tf_op jit(solution)/shard_map/all_to_all | solution.py:157
  152.6 21.1 %all-to-all-start.3 = ((bf16[32,8,1024]{2,1,0:T(8,128)(2,1)}), bf16[32,8,1024]{2,1,0:T(8,128)(2,1)S(1)}, u32[]{:S(2)}, u32[]{:S(2)}) async-start(bf16[32,8,1024]{2,1,0:T(8,128)(2,1)} %broadcast_in_dim.94), calls=%async_computation.3 | async-start | bytes 1048576 | tf_op jit(solution)/shard_map/all_to_all | solution.py:124
  158.2 26.3 %all-gather.10.cloned.1.call-start = ((), (), s32[]{:S(2)}) async-start(), calls=%async_computation.6 | async-start | bytes 1572864 | tf_op jit(solution)/shard_map/all_gather | solution.py:165
  173.8 7.0 %copy-start.4 = (bf16[32,8,1024]{2,1,0:T(8,128)(2,1)}, bf16[32,8,1024]{2,1,0:T(8,128)(2,1)S(1)}, u32[]{:S(2)}) copy-start(bf16[32,8,1024]{2,1,0:T(8,128)(2,1)S(1)} %all-to-all-done.3) | copy-start | bytes 1572868
  174.9 6.8 %copy-start = (bf16[2048,128]{1,0:T(8,128)(2,1)S(1)}, bf16[2048,128]{1,0:T(8,128)(2,1)}, u32[]{:S(2)}) copy-start(bf16[2048,128]{1,0:T(8,128)(2,1)} %all-gather.points_ref) | copy-start | bytes 1572868
  174.9 40.1 %all-to-all-start.5 = ((f32[32,8,1024]{2,1,0:T(8,128)}), f32[32,8,1024]{2,1,0:T(8,128)}, u32[]{:S(2)}, u32[]{:S(2)}) async-start(f32[32,8,1024]{2,1,0:T(8,128)} %broadcast_in_dim.95), calls=%async_computation.5 | async-start | bytes 2097152 | tf_op jit(solution)/shard_map/all_to_all | solution.py:124
  180.7 17.6 %all-gather.12.cloned.1.call-start = ((), (), s32[]{:S(2)}) async-start(), calls=%async_computation.7 | async-start | bytes 1572864 | tf_op jit(solution)/shard_map/all_gather | solution.py:167
  198.3 1.2 copy-start.1
  199.5 1.2 copy-start.2
  215.0 19.8 %all-to-all-start.4 = ((f32[4,512,128]{2,1,0:T(8,128)}), f32[4,512,128]{2,1,0:T(8,128)S(1)}, u32[]{:S(2)}, u32[]{:S(2)}) async-start(f32[4,512,128]{2,1,0:T(8,128)} %bitcast.19), calls=%async_computation.4 | async-start | bytes 2097152 | tf_op jit(solution)/shard_map/all_to_all | solution.py:171
  219.2 15.6 %copy-start.5 = (f32[512,128]{1,0:T(8,128)S(1)}, f32[512,128]{1,0:T(8,128)}, u32[]{:S(2)}) copy-start(f32[512,128]{1,0:T(8,128)} %param.4) | copy-start | bytes 786436
Sparse Core Ops, SparseCore 0:
  9.8 29.4 all-gather.15
  41.1 14.7 all-gather.13
  57.7 17.1 all-gather.17
  160.5 15.2 all-gather.9
  183.0 15.2 all-gather.11

commit v2 on v1

v2 whole, which is shorter than its diff:
```python
import jax
import jax.numpy as jnp
from jax import lax
from jax.experimental import pallas as pl
from jax.experimental.pallas import tpu as pltpu
from jax.sharding import Mesh
from jax.sharding import PartitionSpec as P

ITERS = 8
RIDGE = 1.0
LOG2E = 1.4426950408889634
DEVICES = ("z", "y", "x", "k")
ROUTE = ("x", "z", "y")
ROWS = ("z", "y")
TRANSPOSED = (((1,), (1,)), ((), ()))
FIRST = (((0,), (0,)), ((), ()))
MIB = 1 << 20
POINT_SLOTS = 10
GRAD_SLOTS = 32
SLOTS = 16
FEW = 8
CHIPS = 128
XS = 4
OWN = 1024
NONE = 1 << 20


def iota(shape, axis):
    return lax.broadcasted_iota(jnp.int32, shape, axis)


def owner_place(index, own, xs, rows):
    chip = index // own
    return (chip % xs) * rows + chip // xs


def pack_kernel(
    scalar_ref, here_ref, one_ref, two_ref, three_ref, points_ref, other_points_ref, grads_ref, other_grads_ref,
    out_ref, values_ref, rows_ref, table_ref,
):
    tables = (here_ref, one_ref, two_ref, three_ref)
    per_shard, width = here_ref.shape
    each, targets = grads_ref.shape
    own = 2 * each
    groups = targets // FEW
    blocks = len(tables) * per_shard
    devices = blocks * groups
    share = width // groups
    per = 128 // FEW
    number = scalar_ref[0]
    for back, table in enumerate(tables):
        shard = (scalar_ref[2] - back) & (len(tables) - 1)
        for lane in range(0, width, 128):
            pair = table[:, lane : lane + 128]
            turned = pltpu.roll(pair, share, 1)
            for block in range(per_shard):
                line = (shard * per_shard + block) * groups + lane // share
                table_ref[pl.ds(line, 1), :] = pair[block : block + 1]
                table_ref[pl.ds(line + 1, 1), :] = turned[block : block + 1]
    offset = table_ref[:, :share] - scalar_ref[1]
    mine = (offset >= 0) & (offset < own)
    held = mine.astype(jnp.bfloat16)
    offset = jnp.where(scalar_ref[3] == 0, offset, jnp.where(offset < each, offset + each, offset - each))
    code = jnp.where(mine, (offset + 1).astype(jnp.float32), 0.0)
    upper = (iota((share, share), 0) < iota((share, share), 1)).astype(jnp.bfloat16)
    rank = jnp.dot(held, upper, preferred_element_type=jnp.float32)
    count = jnp.dot(held, jnp.ones((share, share), jnp.bfloat16), preferred_element_type=jnp.float32)
    left, right = iota((devices, devices), 0), iota((devices, devices), 1)
    earlier = ((left // groups == right // groups) & (right < left)).astype(jnp.bfloat16)
    before = jnp.dot(earlier, count.astype(jnp.bfloat16), preferred_element_type=jnp.float32)
    block_rank = rank + before

    lanes = iota((devices, own), 1)
    first = (number * POINT_SLOTS).astype(jnp.float32)
    for slot in range(POINT_SLOTS):
        chosen = jnp.sum(jnp.where(rank == first + slot, code, 0.0), axis=1, keepdims=True)
        pick = (lanes + 1 == chosen.astype(jnp.int32)).astype(jnp.bfloat16)
        rows_ref[pl.ds(slot, devices, stride=SLOTS), :] = jnp.dot(
            pick[:, :each], points_ref[...], preferred_element_type=jnp.float32
        ) + jnp.dot(pick[:, each:], other_points_ref[...], preferred_element_type=jnp.float32)

    lanes = iota((devices, 128), 1)
    keep = iota((blocks, 128), 1) // per == iota((blocks, 128), 0)
    parts = []
    left = jnp.concatenate([grads_ref[...], other_grads_ref[...]], axis=0)
    for _ in range(3):
        part = left.astype(jnp.bfloat16)
        left = left - part.astype(jnp.float32)
        parts.append(part)
    for turn in range(GRAD_SLOTS // per):
        first = (number * GRAD_SLOTS + turn * per).astype(jnp.float32)
        found = jnp.zeros((devices, 128), jnp.float32)
        for slot in range(per):
            chosen = jnp.sum(jnp.where(block_rank == first + slot, code, 0.0), axis=1, keepdims=True)
            found = jnp.where(lanes % per == slot, chosen, found)
        found = jnp.sum(found.reshape(blocks, groups, 128), axis=1)
        found = jnp.sum(jnp.where(keep, found, 0.0), axis=0, keepdims=True).astype(jnp.int32)
        pick = (iota((own, 128), 0) + 1 == found).astype(jnp.bfloat16)
        values = jnp.zeros((targets, 128), jnp.float32)
        for part in parts:
            values = values + lax.dot_general(part, pick, FIRST, preferred_element_type=jnp.float32)
        values_ref[...] = values
        places = iota((groups, 128), 1) // per
        message = [jnp.zeros((groups, 128), jnp.float32) for _ in range(blocks)]
        for target in range(FEW):
            taken = values_ref[pl.ds(target, groups, stride=FEW), :]
            for block in range(blocks):
                by = (target - block) * per % 128
                turned = pltpu.roll(taken, by, 1) if by else taken
                message[block] = jnp.where(places == target, turned, message[block])
        left = jnp.concatenate(message, axis=0)
        for place in range(3):
            part = left.astype(jnp.bfloat16).astype(jnp.float32)
            left = left - part
            rows_ref[pl.ds(POINT_SLOTS + 3 * turn + place, devices, stride=SLOTS), :] = part
    out_ref[...] = rows_ref[...].astype(jnp.bfloat16)


def pack(scalars, tables, points, other_points, grads, other_grads):
    targets = grads.shape[1]
    devices = len(tables) * tables[0].shape[0] * targets // FEW
    vmem = pl.BlockSpec(memory_space=pltpu.VMEM)
    return pl.pallas_call(
        pack_kernel,
        out_shape=jax.ShapeDtypeStruct((devices * SLOTS, 128), jnp.bfloat16),
        in_specs=[pl.BlockSpec(memory_space=pltpu.SMEM)] + [vmem] * 8,
        out_specs=vmem,
        scratch_shapes=[
            pltpu.VMEM((targets, 128), jnp.float32),
            pltpu.VMEM((devices * SLOTS, 128), jnp.float32),
            pltpu.VMEM((devices, 128), jnp.int32),
        ],
        compiler_params=pltpu.CompilerParams(vmem_limit_bytes=16 * MIB),
        name="pack",
    )(scalars, *tables, points, other_points, grads, other_grads)


def ranks_kernel(here_ref, one_ref, two_ref, three_ref, block_row_ref, block_column_ref, rounds_ref, rank_ref):
    tables = (here_ref, one_ref, two_ref, three_ref)
    per_shard, width = here_ref.shape
    share = width // 16
    segments = iota((width, 128), 0) // share == iota((width, 128), 1)
    segments = segments | (iota((width, 128), 1) == 127)
    segments = segments.astype(jnp.bfloat16)
    most = jnp.zeros((CHIPS, 128), jnp.float32)
    chip = iota((CHIPS, width), 0)

    def count(block, most):
        for table in tables:
            hit = (chip == table[pl.ds(block, 1), :] // OWN).astype(jnp.bfloat16)
            most = jnp.maximum(most, jnp.dot(hit, segments, preferred_element_type=jnp.float32))
        return most

    most = lax.fori_loop(0, per_shard, count, most)
    whole = iota((CHIPS, 128), 1) == 127
    most_block = jnp.max(jnp.where(whole, most, 0.0), keepdims=True).astype(jnp.int32)
    most_share = jnp.max(jnp.where(whole, 0.0, most), keepdims=True).astype(jnp.int32)
    rounds_ref[...] = jnp.maximum(
        (most_block + GRAD_SLOTS - 1) // GRAD_SLOTS, (most_share + POINT_SLOTS - 1) // POINT_SLOTS
    )
    owners = block_row_ref[...] // OWN
    step = 128

    def compare(number, total):
        start = pl.multiple_of(number * step, step)
        others = block_column_ref[pl.ds(start, step), :] // OWN
        earlier = iota((step, width), 0) + start < iota((step, width), 1)
        same = jnp.where((others == owners) & earlier, 1, 0)
        return total + jnp.sum(same.reshape(step // 8, 8, width), axis=0)

    total = lax.fori_loop(0, width // step, compare, jnp.zeros((8, width), jnp.int32))
    rank_ref[...] = jnp.sum(total, axis=0, keepdims=True)


def ranks(tables, block_index):
    vmem = pl.BlockSpec(memory_space=pltpu.VMEM)
    width = block_index.shape[0]
    return pl.pallas_call(
        ranks_kernel,
        out_shape=(
            jax.ShapeDtypeStruct((1, 1), jnp.int32),
            jax.ShapeDtypeStruct((1, width), jnp.int32),
        ),
        in_specs=[vmem] * 6,
        out_specs=(vmem, vmem),
        compiler_params=pltpu.CompilerParams(vmem_limit_bytes=16 * MIB),
        cost_estimate=pl.CostEstimate(flops=4 * 10**9, bytes_accessed=10**5, transcendentals=0),
        name="ranks",
    )(*tables, block_index[None, :], block_index[:, None])


def place_kernel(scalar_ref, message_ref, row_ref, column_ref, block_ref, rank_ref, piece_ref, right_ref):
    length = message_ref.shape[0]
    share = column_ref.shape[0]
    width = block_ref.shape[1]
    per = 128 // FEW
    turns = GRAD_SLOTS // per
    number = scalar_ref[0]
    row_owner = owner_place(row_ref[...], OWN, XS, CHIPS // XS)
    column_owner = owner_place(column_ref[...], OWN, XS, CHIPS // XS)
    earlier = iota((share, share), 1) < iota((share, share), 0)
    rank = jnp.sum(
        jnp.where((row_owner == column_owner) & earlier, 1.0, 0.0), axis=1, keepdims=True
    ).astype(jnp.int32)
    slot = rank - number * POINT_SLOTS
    code = jnp.where((slot >= 0) & (slot < POINT_SLOTS), column_owner * SLOTS + slot, -1)
    pick = (iota((share, length), 1) == code).astype(jnp.bfloat16)
    piece = jnp.dot(pick, message_ref[...], preferred_element_type=jnp.float32).astype(jnp.bfloat16)
    for copy in range(piece_ref.shape[0]):
        piece_ref[copy] = piece

    slot = rank_ref[...] - number * GRAD_SLOTS
    wanted = owner_place(block_ref[...], OWN, XS, CHIPS // XS) * turns + slot // per
    wanted = jnp.where((slot >= 0) & (slot < GRAD_SLOTS), wanted, -NONE)
    step = 256
    def gather(number, found):
        start = pl.multiple_of(number * step, step)
        line = iota((step, width), 0)
        turn = (line % SLOTS - POINT_SLOTS + 3) // 3 - 1
        source = jnp.where((turn >= 0) & (turn < turns), line // SLOTS * turns + turn, 2 * NONE)
        pick = (source == wanted - number * (step // SLOTS * turns)).astype(jnp.bfloat16)
        return found + lax.dot_general(
            message_ref[pl.ds(start, step), :], pick, FIRST, preferred_element_type=jnp.float32
        )

    found = lax.fori_loop(0, length // step, gather, jnp.zeros((128, width), jnp.float32), unroll=2)
    here = iota((per, width), 0) == slot % per
    for target in range(FEW):
        part = found[target * per : (target + 1) * per]
        right_ref[pl.ds(target, 1), :] = -jnp.sum(jnp.where(here, part, 0.0), axis=0, keepdims=True)


def place(scalars, message, index, block_index, rank, copies):
    vmem = pl.BlockSpec(memory_space=pltpu.VMEM)
    share, width = index.shape[0], block_index.shape[0]
    return pl.pallas_call(
        place_kernel,
        out_shape=(
            jax.ShapeDtypeStruct((copies, share, 128), jnp.bfloat16),
            jax.ShapeDtypeStruct((FEW, width), jnp.float32),
        ),
        in_specs=[pl.BlockSpec(memory_space=pltpu.SMEM)] + [vmem] * 5,
        out_specs=(vmem, vmem),
        compiler_params=pltpu.CompilerParams(vmem_limit_bytes=16 * MIB),
        name="place",
    )(scalars, message, index[None, :], index[:, None], block_index[None, :], rank)


def solve_kernel(points_ref, right_ref, half_ref, rest_ref, high_ref, low_ref):
    width = points_ref.shape[0]
    scale = -2.0 / points_ref.shape[1] * LOG2E
    step = 256
    same = iota((step, step), 0) == iota((step, step), 1)
    columns, lines = [], []
    for start in range(0, width, step):
        part = points_ref[pl.ds(start, step), :]
        inner = lax.dot_general(part, part, TRANSPOSED, preferred_element_type=jnp.float32)
        inner = jnp.where(same, inner, 0.0)
        columns.append(jnp.sum(inner, axis=1, keepdims=True))
        lines.append(jnp.sum(inner, axis=0, keepdims=True))
    line = jnp.concatenate(lines, axis=1)
    upper = jnp.zeros((1, 1), jnp.float32)
    for number, start in enumerate(range(0, width, step)):
        piece = pl.ds(start, step)
        inner = lax.dot_general(
            points_ref[piece, :], points_ref[...], TRANSPOSED, preferred_element_type=jnp.float32
        )
        distance = jnp.maximum(columns[number] + line - 2.0 * inner, 0.0)
        values = jnp.exp2(distance * scale)
        sums = jnp.sum(values, axis=1, keepdims=True)
        upper = jnp.maximum(upper, jnp.max(sums, axis=0, keepdims=True))
        high = values.astype(jnp.bfloat16)
        high_ref[piece, :] = high
        low_ref[piece, :] = (values - high.astype(jnp.float32)).astype(jnp.bfloat16)
    upper = upper + RIDGE
    center = (upper + RIDGE) / 2.0
    radius = (upper - RIDGE) / 2.0
    ratio = center / radius
    factor = 1.0 / ratio
    residual = right_ref[...]
    targets = residual.shape[0]
    direction = residual / center
    update = jnp.zeros_like(residual)
    for iteration in range(ITERS):
        update = update + direction
        if iteration < ITERS - 1:
            high = direction.astype(jnp.bfloat16)
            low = (direction - high.astype(jnp.float32)).astype(jnp.bfloat16)
            both = jnp.concatenate([high, low], axis=0)
            main = jnp.dot(both, high_ref[...], preferred_element_type=jnp.float32)
            rest = jnp.dot(high, low_ref[...], preferred_element_type=jnp.float32)
            product = main[:targets] + (main[targets:] + rest)
            residual = residual - (product + RIDGE * direction)
            following = 1.0 / (2.0 * ratio - factor)
            direction = following * factor * direction + 2.0 * following / radius * residual
            factor = following
    half = update.astype(jnp.bfloat16)
    rest = (update - half.astype(jnp.float32)).astype(jnp.bfloat16)
    for copy in range(half_ref.shape[0]):
        half_ref[copy] = half
        rest_ref[copy] = rest


def solve(points, right_side, copies):
    width, _ = points.shape
    vmem = pl.BlockSpec(memory_space=pltpu.VMEM)
    return pl.pallas_call(
        solve_kernel,
        out_shape=(jax.ShapeDtypeStruct((copies, *right_side.shape), jnp.bfloat16),) * 2,
        in_specs=[vmem] * 2,
        out_specs=(vmem, vmem),
        scratch_shapes=[pltpu.VMEM((width, width), jnp.bfloat16)] * 2,
        compiler_params=pltpu.CompilerParams(vmem_limit_bytes=16 * MIB),
        cost_estimate=pl.CostEstimate(flops=6 * 10**9, bytes_accessed=10**6, transcendentals=width * width),
        name="solve",
    )(points, right_side)


def tile_kernel(points_ref, column_ref, ids_ref, chosen_ref, row_ref, panel_ref, out_ref):
    scale = -2.0 / points_ref.shape[1] * LOG2E
    step = 512
    for start in range(0, chosen_ref.shape[0], step):
        piece = pl.ds(start, step)
        inner = lax.dot_general(
            points_ref[...], chosen_ref[piece, :], TRANSPOSED, preferred_element_type=jnp.float32
        )
        distance = jnp.maximum(column_ref[...] + row_ref[:, piece] - 2.0 * inner, 0.0)
        values = jnp.exp2(distance * scale)
        values = jnp.where(ids_ref[...] == panel_ref[:, piece], values + RIDGE, values)
        out_ref[:, piece] = values.astype(jnp.bfloat16)


def build_tile(points, ids, chosen, panel):
    count, features = points.shape
    width = chosen.shape[0]
    block = 256
    point_squares = jnp.sum(jnp.square(points.astype(jnp.float32)), axis=-1)
    panel_squares = jnp.sum(jnp.square(chosen.astype(jnp.float32)), axis=-1)
    return pl.pallas_call(
        tile_kernel,
        grid=(count // block,),
        out_shape=jax.ShapeDtypeStruct((count, width), jnp.bfloat16),
        in_specs=[
            pl.BlockSpec((block, features), lambda i: (i, 0)),
            pl.BlockSpec((block, 1), lambda i: (i, 0)),
            pl.BlockSpec((block, 1), lambda i: (i, 0)),
            pl.BlockSpec((width, features), lambda i: (0, 0)),
            pl.BlockSpec((1, width), lambda i: (0, 0)),
            pl.BlockSpec((1, width), lambda i: (0, 0)),
        ],
        out_specs=pl.BlockSpec((block, width), lambda i: (i, 0)),
        compiler_params=pltpu.CompilerParams(vmem_limit_bytes=52 * MIB),
        cost_estimate=pl.CostEstimate(
            flops=8 * count * width * features, bytes_accessed=2 * count * width, transcendentals=count * width
        ),
        name="tile",
    )(points, point_squares[:, None], ids[:, None], chosen, panel_squares[None, :], panel[None, :])


def product_kernel(*refs):
    *tile_refs, here_ref, there_ref, out_ref = refs
    blocks = here_ref.shape[0]
    total = jnp.zeros(out_ref.shape, jnp.float32)
    for part, tile_ref in enumerate(tile_refs):
        update = here_ref[part] if part < blocks else there_ref[part - blocks]
        total = total + lax.dot_general(
            tile_ref[...], update, TRANSPOSED, preferred_element_type=jnp.float32
        )
    out_ref[...] = total


def product(tile, here, there, first, count):
    blocks, targets, width = here.shape
    line = 256
    skip = first // line
    panel = tile.shape[1]
    whole = pl.BlockSpec(here.shape, lambda i: (0, 0, 0))
    parts = [pl.BlockSpec((line, width), lambda i, part=part: (i + skip, part)) for part in range(2 * blocks)]
    return pl.pallas_call(
        product_kernel,
        grid=(count // line,),
        out_shape=jax.ShapeDtypeStruct((count, targets), jnp.float32),
        in_specs=[*parts, whole, whole],
        out_specs=pl.BlockSpec((line, targets), lambda i: (i, 0)),
        compiler_params=pltpu.CompilerParams(vmem_limit_bytes=52 * MIB),
        cost_estimate=pl.CostEstimate(
            flops=4 * count * panel * targets, bytes_accessed=2 * count * panel, transcendentals=0
        ),
        name="product",
    )(*[tile] * len(parts), here, there)


def finish_kernel(half_ref, rest_ref, out_ref):
    blocks, _, width = half_ref.shape
    for block in range(blocks):
        whole = half_ref[block].astype(jnp.float32) + rest_ref[block].astype(jnp.float32)
        out_ref[pl.ds(block * width, width), :] = whole.T


def finish(half, rest):
    blocks, targets, width = half.shape
    vmem = pl.BlockSpec(memory_space=pltpu.VMEM)
    return pl.pallas_call(
        finish_kernel,
        out_shape=jax.ShapeDtypeStruct((blocks * width, targets), jnp.float32),
        in_specs=[vmem] * 2,
        out_specs=vmem,
        compiler_params=pltpu.CompilerParams(vmem_limit_bytes=16 * MIB),
        cost_estimate=pl.CostEstimate(flops=10**6, bytes_accessed=2 * 10**6, transcendentals=0),
        name="finish",
    )(half, rest)


def shift(value, axis, by):
    size = lax.axis_size(axis)
    return lax.ppermute(value, axis, [(i, (i + by) % size) for i in range(size)])


def ring_gather(value, axis):
    half = value.shape[0] // 2
    before = shift(value, axis, 1)
    after = shift(value, axis, -1)
    top = shift(before[:half], axis, 1)
    bottom = shift(after[half:], axis, -1)
    return [value, after, jnp.concatenate([top, bottom], axis=0), before]


def on_device(points, gradient, panel_index):
    own, features = points.shape
    targets = gradient.shape[1]
    blocks, width = panel_index.shape
    shard = blocks * width
    zs, ys, xs, ks = (lax.axis_size(name) for name in DEVICES)
    z, y, x, core = (lax.axis_index(name) for name in DEVICES)
    rows, cols = zs * ys, xs * ks
    row = z * ys + y
    group_start = row * own * cols
    share = shard // rows
    groups = targets // FEW

    tables = [panel_index] + [shift(panel_index, "x", by) for by in range(1, xs)]
    other_points = shift(points, "k", 1)
    other_grads = shift(gradient, "k", 1)
    own_share = lax.dynamic_index_in_dim(panel_index.reshape(rows, share), row, 0, False)
    block = row // groups
    block_index = lax.dynamic_index_in_dim(panel_index, block, 0, False)
    start = (row * xs + x) * own * ks
    rounds, rank = ranks(tables, block_index)
    rounds = jnp.maximum(rounds, shift(rounds, "k", 1))

    def exchange(message):
        return lax.all_to_all(message, ROUTE, 0, 0)

    def exchange_by_axis(message):
        message = message.reshape(xs, zs, ys, SLOTS, 128)
        for dim, axis in enumerate(ROUTE):
            message = lax.all_to_all(message, axis, dim, dim, tiled=True)
        return message

    def route(number, exchange):
        scalars = jnp.stack([number, start, x, core]).astype(jnp.int32)
        message = pack(scalars, tables, points, other_points, gradient, other_grads).reshape(rows * xs, SLOTS, 128)
        message = exchange(message).reshape(rows * xs * SLOTS, 128)
        return place(scalars, message, own_share, block_index, rank, rows)

    def further(state):
        number, piece, right = state
        more_piece, more_right = route(number, exchange_by_axis)
        return number + 1, piece + more_piece, right + more_right

    piece, right_side = route(jnp.int32(0), exchange)
    last = rounds[0, 0]
    _, piece, right_side = lax.while_loop(
        lambda state: state[0] < last, further, (jnp.int32(1), piece, right_side)
    )
    chosen = lax.all_to_all(piece, ROWS, 0, 0).reshape(shard, features)

    own_block = lax.dynamic_index_in_dim(chosen.reshape(blocks, width, features), block, 0, False)
    half, rest = solve(own_block, right_side, rows)
    half = lax.all_to_all(half, ROWS, 0, 0).reshape(blocks, targets, width)

    calm_points, _ = lax.optimization_barrier((points, tables))
    mine, after, far, before = ring_gather(calm_points, "x")
    core_points = jnp.concatenate([far, after, before, mine])
    indices = panel_index.reshape(-1)
    both_chosen = jnp.concatenate([chosen, shift(chosen, "k", 1)])
    both_panel = jnp.concatenate([indices, shift(indices, "k", 1)])
    ahead = (x + jnp.array([2, 1, 3, 0], jnp.int32)) % xs
    ids = group_start + (ahead * ks + core)[:, None] * own + jnp.arange(own, dtype=jnp.int32)[None, :]
    tile = build_tile(core_points, ids.reshape(-1), both_chosen, both_panel)

    half, tile, rest = lax.optimization_barrier((half, tile, rest))
    rest = lax.all_to_all(rest, ROWS, 0, 0).reshape(blocks, targets, width)
    other = shift(half, "k", 1)

    far = product(tile, half, other, 0, own)
    near = product(tile, half, other, own, 2 * own)
    mine = product(tile, half, other, 3 * own, own)
    middle = own // 2
    top = shift(far[:middle], "x", 1)
    bottom = shift(far[middle:], "x", -1)
    send_after = jnp.concatenate([near[:middle] + top, near[middle:own]])
    send_before = jnp.concatenate([near[own : own + middle], near[own + middle :] + bottom])
    from_before = shift(send_after, "x", 1)
    from_after = shift(send_before, "x", -1)
    new_gradient = gradient + (mine + from_before + from_after)
    return new_gradient, finish(half, rest)


def solution(mesh):
    fine = Mesh(mesh.devices.reshape(8, 4, 4, 2), DEVICES)
    in_specs = (P(DEVICES, None), P(DEVICES, None), P(("x", "k"), None))
    out_specs = (P(DEVICES, None), P(("x", "k"), None))
    return jax.shard_map(on_device, mesh=fine, in_specs=in_specs, out_specs=out_specs, check_vma=False)
```

time: 243 us -> 133 us (0.55)
  waiting for transfers between devices: 105 us -> 23.1 us
  blocking collectives: 44.1 us -> 0 us
  starting transfers between devices: 26.9 us -> 54.1 us
  Pallas kernels: 19.7 us -> 44.3 us
  local copies, waits for them, and re-layouts: 25.6 us -> 5.35 us
  between operations: 14.1 us -> 2.21 us
  other arithmetic: 6.35 us -> 3.01 us
    all_gather x5 -> x0, waiting for transfers between devices: 43.3 us -> none  [the longest x1 16.3 us: on_device(): lax.all_gather(core_points, 'k', axis=1).reshape(group, features)]
    all_to_all x5 -> x4, waiting for transfers between devices: 60.4 us -> 17.1 us  [the longest x1 8.77 us: exchange(): return lax.all_to_all(message, ROUTE, 0, 0)]
    all_to_all x1 -> x0, blocking collectives: 27.2 us -> none  [on_device(): lax.all_to_all(picked_points.reshape(rows, shard // rows, features), ROWS...]
    pallas_call x2 -> x9, Pallas kernels: 19.7 us -> 44.3 us  [the longest x1 14.7 us: build_tile(): pl.pallas_call(tile_kernel, grid=(count // block,), out_shape=jax.ShapeDt...]
    ppermute x0 -> x17, starting transfers between devices: none -> 19.8 us  [shift(): lax.ppermute(value, axis, [(i, (i + by) % size) for i in range(size)])]
    all_gather x2 -> x0, blocking collectives: 16.8 us -> none  [the longest x1 14.8 us: on_device(): core_points = lax.all_gather(points, 'x')]
    gather x2 -> x0, local copies, waits for them, and re-layouts: 14 us -> none  [the longest x1 7.05 us: on_device(): picked_grads = jnp.where(inside, jnp.take(row_grads, clipped, axis=0), 0.0)]
    all_to_all x5 -> x4, starting transfers between devices: 26.7 us -> 34.3 us  [the longest x1 14.4 us: exchange(): return lax.all_to_all(message, ROUTE, 0, 0)]
  transfers between devices with their start and end apart: 10 -> 21, of which waited for: 7 -> 6; matrix products, arithmetic and copies ran while one was open for 11% -> 6% of each run, Pallas kernels for 6% -> 33%
where the time goes in v2:
time: 133 us; the launch traced here: 132 us
  starting transfers between devices  54.1 us (41%)
  Pallas kernels  44.3 us (33%)
  waiting for transfers between devices  23.1 us (17%)
  local copies, waits for them, and re-layouts  5.35 us (4%)
  other arithmetic  3.01 us (2%)
  between operations  2.21 us (2%)
    ppermute x17, starting transfers between devices, shift(): lax.ppermute(value, axis, [(i, (i + by) % size) for i in range(size)])  19.8 us
    pallas_call x1, Pallas kernels, build_tile(): pl.pallas_call(tile_kernel, grid=(count // block,), out_shape=jax.ShapeDt...  14.7 us
    all_to_all x1, starting transfers between devices, exchange(): return lax.all_to_all(message, ROUTE, 0, 0)  14.4 us
    pallas_call x3, Pallas kernels, product(): pl.pallas_call(product_kernel, grid=(count // line,), out_shape=jax.Shape...  11.4 us
    all_to_all x1, waiting for transfers between devices, exchange(): return lax.all_to_all(message, ROUTE, 0, 0)  8.77 us
    all_to_all x1, starting transfers between devices, on_device(): rest = lax.all_to_all(rest, ROWS, 0, 0).reshape(blocks, targets, width)  8.66 us
    all_to_all x1, waiting for transfers between devices, on_device(): chosen = lax.all_to_all(piece, ROWS, 0, 0).reshape(shard, features)  7.18 us
    pallas_call x1, Pallas kernels, solve(): pl.pallas_call(solve_kernel, out_shape=(jax.ShapeDtypeStruct((copies, *ri...  6.59 us
  transfers between devices with their start and end apart: 21, of which 6 were waited for; matrix products, arithmetic and copies ran while one was open for 6% of the time, Pallas kernels for 33%

profile of v2, /device:TPU:8, one launch (start us, length us, event | category | flops | bytes accessed | tf_op | source)
XLA Modules:
  0.0 132.0 jit_solution(6799513527084206645)
XLA Ops:
  0.6 0.0 copy-start.2
  0.7 0.1 collective-permute-start.4
  0.8 1.6 %collective-permute-start = (s32[2,1024]{1,0:T(2,128)}, s32[2,1024]{1,0:T(2,128)S(1)}, u32[]{:S(2)}, u32[]{:S(2)}) collective-permute-start(s32[2,1024]{1,0:T(2,128)} %here_ref.3), channel_id=1, source_target_pairs={{0,2},{2,4},{4,6},{6,0},{1,3},{3,5},{5,7},{7,1},{8,10},{10,12},{12... | collective-permute-start | bytes 24584 | tf_op jit(solution)/shard_map/ppermute | solution.py:416
  2.3 2.7 %collective-permute-start.1 = (s32[2,1024]{1,0:T(2,128)}, s32[2,1024]{1,0:T(2,128)S(1)}, u32[]{:S(2)}, u32[]{:S(2)}) collective-permute-start(s32[2,1024]{1,0:T(2,128)} %here_ref.3), channel_id=1, source_target_pairs={{0,4},{2,6},{4,0},{6,2},{1,5},{3,7},{5,1},{7,3},{8,12},{10,14},{12... | collective-permute-start | bytes 24584 | tf_op jit(solution)/shard_map/ppermute | solution.py:416
  5.1 1.4 %collective-permute-start.2 = (s32[2,1024]{1,0:T(2,128)}, s32[2,1024]{1,0:T(2,128)S(1)}, u32[]{:S(2)}, u32[]{:S(2)}) collective-permute-start(s32[2,1024]{1,0:T(2,128)} %here_ref.3), channel_id=1, source_target_pairs={{0,6},{2,0},{4,2},{6,4},{1,7},{3,1},{5,3},{7,5},{8,14},{10,8},{12,... | collective-permute-start | bytes 24584 | tf_op jit(solution)/shard_map/ppermute | solution.py:416
  6.5 0.7 fusion.7
  7.2 0.1 pad_add_fusion.2.scalar_ref
  7.3 0.8 reshape.60
  8.1 0.2 copy.25.block_column_ref
  8.3 0.7 copy.33
  9.0 0.5 collective-permute-start.11
  9.5 4.3 %pack.2 = bf16[2048,128]{1,0:T(8,128)(2,1)} custom-call(s32[4]{0:T(128)S(1)} %pad_add_fusion.2.scalar_ref, s32[2,1024]{1,0:T(2,128)} %here_ref.3, s32[2,1024]{1,0:T(2,128)S(1)} %collective-permute-done.one_ref, s32[2,1024]{1,0:T(2,128)S(1)} %collective-permute-done.1.two_ref, s32[2,1024]{1,0:T(2,128)S(1)} %collective-permute-done.2.three_ref, ...), custom_call_target="tpu_custom_call" | custom-call | tf_op jit(solution)/shard_map/pack/pallas_call | solution.py:123
  13.8 14.4 %all-to-all-start.3 = ((bf16[128,16,128]{2,1,0:T(8,128)(2,1)}), bf16[128,16,128]{2,1,0:T(8,128)(2,1)S(1)}, u32[]{:S(2)}, u32[]{:S(2)}) async-start(bf16[128,16,128]{2,1,0:T(8,128)(2,1)} %bitcast.12), calls=%async_computation.3 | async-start | bytes 1048576 | tf_op jit(solution)/shard_map/all_to_all | solution.py:452
  28.2 0.1 copy.26.column_ref
  28.4 0.0 copy-start
  28.4 1.6 %collective-permute-start.6 = (bf16[512,128]{1,0:T(8,128)(2,1)}, bf16[512,128]{1,0:T(8,128)(2,1)S(1)}, u32[]{:S(2)}, u32[]{:S(2)}) collective-permute-start(bf16[512,128]{1,0:T(8,128)(2,1)} %points_ref.1), channel_id=1, source_target_pairs={{0,2},{2,4},{4,6},{6,0},{1,3},{3,5},{5,7},{7,1},{8,10},{10,12},{12... | collective-permute-start | bytes 393224 | tf_op jit(solution)/shard_map/ppermute | solution.py:416
  30.0 1.7 %collective-permute-start.8 = (bf16[512,128]{1,0:T(8,128)(2,1)}, bf16[512,128]{1,0:T(8,128)(2,1)S(1)}, u32[]{:S(2)}, u32[]{:S(2)}) collective-permute-start(bf16[512,128]{1,0:T(8,128)(2,1)} %points_ref.1), channel_id=1, source_target_pairs={{0,6},{2,0},{4,2},{6,4},{1,7},{3,1},{5,3},{7,5},{8,14},{10,8},{12,... | collective-permute-start | bytes 393224 | tf_op jit(solution)/shard_map/ppermute | solution.py:416
  31.8 2.7 %ranks.1 = (s32[1,1]{1,0:T(1,128)}, s32[1,1024]{1,0:T(1,128)S(1)}) custom-call(s32[2,1024]{1,0:T(2,128)S(1)} %copy-done.1, s32[2,1024]{1,0:T(2,128)S(1)} %collective-permute-done.one_ref, s32[2,1024]{1,0:T(2,128)S(1)} %collective-permute-done.1.two_ref, s32[2,1024]{1,0:T(2,128)S(1)} %collective-permute-done.2.three_ref, ...), custom_call_target="tpu_custom_call" | custom-call | flops 4000000000 | bytes 100000 | tf_op jit(solution)/shard_map/ranks/pallas_call | solution.py:178
  34.5 1.3 %collective-permute-done.5 = s32[1,1]{1,0:T(1,128)} collective-permute-done((s32[1,1]{1,0:T(1,128)}, s32[1,1]{1,0:T(1,128)}, u32[]{:S(2)}, u32[]{:S(2)}) %collective-permute-start.5) | collective-permute-done | bytes 36 | tf_op jit(solution)/shard_map/ppermute | solution.py:416
  37.1 8.8 %all-to-all-done.3 = bf16[128,16,128]{2,1,0:T(8,128)(2,1)S(1)} async-done(((bf16[128,16,128]{2,1,0:T(8,128)(2,1)}), bf16[128,16,128]{2,1,0:T(8,128)(2,1)S(1)}, u32[]{:S(2)}, u32[]{:S(2)}) %all-to-all-start.3) | async-done | bytes 524320 | tf_op jit(solution)/shard_map/all_to_all | solution.py:452
  45.9 3.4 %place.2 = (bf16[32,64,128]{2,1,0:T(8,128)(2,1)}, f32[8,1024]{1,0:T(8,128)S(1)}) custom-call(s32[4]{0:T(128)S(1)} %pad_add_fusion.2.scalar_ref, bf16[2048,128]{1,0:T(8,128)(2,1)S(1)} %bitcast.65, s32[1,64]{1,0:T(1,128)S(1)} %constant_dynamic-slice_fusion.1.row_ref, s32[64,1]{1,0:T(8,128)S(1)} %copy.26.column_ref, ...), custom_call_target="tpu_custom_call" | custom-call | tf_op jit(solution)/shard_map/place/pallas_call | solution.py:236
  49.2 5.5 %all-to-all-start.4 = ((bf16[32,64,128]{2,1,0:T(8,128)(2,1)}), bf16[32,64,128]{2,1,0:T(8,128)(2,1)S(1)}, u32[]{:S(2)}, u32[]{:S(2)}) async-start(bf16[32,64,128]{2,1,0:T(8,128)(2,1)} %get-tuple-element.112), calls=%async_computation.4 | async-start | bytes 1048576 | tf_op jit(solution)/shard_map/all_to_all | solution.py:476
  54.8 0.1 add_bitcast_fusion
  54.8 1.3 %copy.30 = s32[1,2048]{0,1:T(8,128)} copy(s32[1,2048]{1,0:T(1,128)S(1)} %bitcast.80) | data formatting | bytes 16384
  56.2 0.8 collective-permute-start.7
  57.0 2.6 %collective-permute-start.9 = (bf16[256,128]{1,0:T(8,128)(2,1)S(1)}, bf16[256,128]{1,0:T(8,128)(2,1)S(1)}, u32[]{:S(2)}, u32[]{:S(2)}) collective-permute-start(bf16[256,128]{1,0:T(8,128)(2,1)S(1)} %slice.33), channel_id=1, source_target_pairs={{0,6},{2,0},{4,2},{6,4},{1,7},{3,1},{5,3},{7,5},{8,14},{10,8},{12,... | collective-permute-start | bytes 196616 | tf_op jit(solution)/shard_map/ppermute | solution.py:416
  59.6 2.1 %collective-permute-done.7 = bf16[256,128]{1,0:T(8,128)(2,1)S(1)} collective-permute-done((bf16[256,128]{1,0:T(8,128)(2,1)S(1)}, bf16[256,128]{1,0:T(8,128)(2,1)S(1)}, u32[]{:S(2)}, u32[]{:S(2)}) %collective-permute-start.7) | collective-permute-done | bytes 65568 | tf_op jit(solution)/shard_map/ppermute | solution.py:416
  61.8 0.9 constant_dynamic-update-slice_fusion.points_ref
  62.8 0.3 multiply_reduce_fusion.1
  63.1 0.4 copy.27.column_ref
  63.5 7.2 %all-to-all-done.4 = bf16[32,64,128]{2,1,0:T(8,128)(2,1)S(1)} async-done(((bf16[32,64,128]{2,1,0:T(8,128)(2,1)}), bf16[32,64,128]{2,1,0:T(8,128)(2,1)S(1)}, u32[]{:S(2)}, u32[]{:S(2)}) %all-to-all-start.4) | async-done | bytes 524320 | tf_op jit(solution)/shard_map/all_to_all | solution.py:476
  70.7 6.6 %solve.1 = (bf16[32,8,1024]{2,1,0:T(8,128)(2,1)}, bf16[32,8,1024]{2,1,0:T(8,128)(2,1)}) custom-call(bf16[1024,128]{1,0:T(8,128)(2,1)S(1)} %dynamic-slice_bitcast_fusion.points_ref, f32[8,1024]{1,0:T(8,128)S(1)} %get-tuple-element.113.right_ref), custom_call_target="tpu_custom_call" | custom-call | flops 6000000000 | bytes 1000000 | tf_op jit(solution)/shard_map/solve/pallas_call | solution.py:307
  77.3 5.8 %all-to-all-start.5 = ((bf16[32,8,1024]{2,1,0:T(8,128)(2,1)}), bf16[32,8,1024]{2,1,0:T(8,128)(2,1)S(1)}, u32[]{:S(2)}, u32[]{:S(2)}) async-start(bf16[32,8,1024]{2,1,0:T(8,128)(2,1)} %get-tuple-element.114), calls=%async_computation.5 | async-start | bytes 1048576 | tf_op jit(solution)/shard_map/all_to_all | solution.py:480
  83.1 1.1 pad_maximum_fusion.chosen_ref
  84.1 0.6 multiply_reduce_fusion
  84.8 14.7 %tile.1.refs_0_.refs_1_.refs_2_.refs_3_ = bf16[2048,4096]{1,0:T(8,128)(2,1)} custom-call(bf16[2048,128]{1,0:T(8,128)(2,1)S(1)} %constant_dynamic-update-slice_fusion.points_ref, f32[2048,1]{1,0:T(8,128)S(1)} %copy.27.column_ref, s32[2048,1]{1,0:T(8,128)} %bitcast.73, bf16[4096,128]{1,0:T(8,128)(2,1)} %pad_maximum_fusion.chosen_ref, f32[1,4096]{1,0:T(1,128)S(1)} %bitcast.67, ...), custom_call_target="tpu_custom_call" | custom-call | flops 8589934592 | bytes 16777216 | tf_op jit(solution)/shard_map/tile/pallas_call | solution.py:339
  99.4 1.1 all-to-all-done.5
  100.6 8.7 %all-to-all-start.6 = ((bf16[32,8,1024]{2,1,0:T(8,128)(2,1)}), bf16[32,8,1024]{2,1,0:T(8,128)(2,1)S(1)}, u32[]{:S(2)}, u32[]{:S(2)}) async-start(bf16[32,8,1024]{2,1,0:T(8,128)(2,1)} %get-tuple-element.119), calls=%async_computation.6 | async-start | bytes 1048576 | tf_op jit(solution)/shard_map/all_to_all | solution.py:493
  109.3 3.0 %product.5 = f32[512,128]{1,0:T(8,128)S(1)} custom-call(bf16[2048,4096]{1,0:T(8,128)(2,1)} %tile.1.refs_0_.refs_1_.refs_2_.refs_3_, bf16[2048,4096]{1,0:T(8,128)(2,1)} %tile.1.refs_0_.refs_1_.refs_2_.refs_3_, bf16[2048,4096]{1,0:T(8,128)(2,1)} %tile.1.refs_0_.refs_1_.refs_2_.refs_3_, bf16[2048,4096]{1,0:T(8,128)(2,1)} %tile.1.refs_0_.refs_1_.refs_2_.refs_3_, ...), custom_call_target="tpu_custom_call" | custom-call | flops 1073741824 | bytes 4194304 | tf_op jit(solution)/shard_map/product/pallas_call | solution.py:379
  112.3 0.1 collective-permute-start.13
  112.4 3.2 %collective-permute-start.15 = (f32[256,128]{1,0:T(8,128)S(1)}, f32[256,128]{1,0:T(8,128)S(1)}, u32[]{:S(2)}, u32[]{:S(2)}) collective-permute-start(f32[256,128]{1,0:T(8,128)S(1)} %get-tuple-element.161), channel_id=1, source_target_pairs={{0,6},{2,0},{4,2},{6,4},{1,7},{3,1},{5,3},{7,5},{8,14},{10,8},{12,... | collective-permute-start | bytes 393224 | tf_op jit(solution)/shard_map/ppermute | solution.py:416
  115.6 5.4 %product.4 = f32[1024,128]{1,0:T(8,128)S(1)} custom-call(bf16[2048,4096]{1,0:T(8,128)(2,1)} %tile.1.refs_0_.refs_1_.refs_2_.refs_3_, bf16[2048,4096]{1,0:T(8,128)(2,1)} %tile.1.refs_0_.refs_1_.refs_2_.refs_3_, bf16[2048,4096]{1,0:T(8,128)(2,1)} %tile.1.refs_0_.refs_1_.refs_2_.refs_3_, bf16[2048,4096]{1,0:T(8,128)(2,1)} %tile.1.refs_0_.refs_1_.refs_2_.refs_3_, ...), custom_call_target="tpu_custom_call" | custom-call | flops 2147483648 | bytes 8388608 | tf_op jit(solution)/shard_map/product/pallas_call | solution.py:379
  121.1 0.1 collective-permute-start.14
  121.2 3.3 %collective-permute-start.16 = (f32[512,128]{1,0:T(8,128)S(1)}, f32[512,128]{1,0:T(8,128)S(1)}, u32[]{:S(2)}, u32[]{:S(2)}) collective-permute-start(f32[512,128]{1,0:T(8,128)S(1)} %pad_maximum_fusion.2), channel_id=1, source_target_pairs={{0,6},{2,0},{4,2},{6,4},{1,7},{3,1},{5,3},{7,5},{8,14},{10,8},{12,... | collective-permute-start | bytes 786440 | tf_op jit(solution)/shard_map/ppermute | solution.py:416
  124.5 3.0 %product.3 = f32[512,128]{1,0:T(8,128)S(1)} custom-call(bf16[2048,4096]{1,0:T(8,128)(2,1)} %tile.1.refs_0_.refs_1_.refs_2_.refs_3_, bf16[2048,4096]{1,0:T(8,128)(2,1)} %tile.1.refs_0_.refs_1_.refs_2_.refs_3_, bf16[2048,4096]{1,0:T(8,128)(2,1)} %tile.1.refs_0_.refs_1_.refs_2_.refs_3_, bf16[2048,4096]{1,0:T(8,128)(2,1)} %tile.1.refs_0_.refs_1_.refs_2_.refs_3_, ...), custom_call_target="tpu_custom_call" | custom-call | flops 1073741824 | bytes 4194304 | tf_op jit(solution)/shard_map/product/pallas_call | solution.py:379
  127.5 2.5 %collective-permute-done.14 = f32[512,128]{1,0:T(8,128)S(1)} collective-permute-done((f32[512,128]{1,0:T(8,128)S(1)}, f32[512,128]{1,0:T(8,128)S(1)}, u32[]{:S(2)}, u32[]{:S(2)}) %collective-permute-start.14) | collective-permute-done | bytes 262176 | tf_op jit(solution)/shard_map/ppermute | solution.py:416
  130.0 0.8 add_add_fusion
  130.7 1.3 finish.1
  (42 shorter events, 0.3 us)
Async XLA Ops:
  0.6 27.7 %copy-start.2 = (s32[4]{0:T(128)S(1)}, s32[4]{0:T(128)}, u32[]{:S(2)}) copy-start(s32[4]{0:T(128)} %constant.78.clone) | copy-start | bytes 52
  0.6 27.7 %copy-start.1 = (s32[2,1024]{1,0:T(2,128)S(1)}, s32[2,1024]{1,0:T(2,128)}, u32[]{:S(2)}) copy-start(s32[2,1024]{1,0:T(2,128)} %here_ref.3) | copy-start | bytes 24580
  0.7 8.9 %collective-permute-start.4 = (f32[512,128]{1,0:T(8,128)}, f32[512,128]{1,0:T(8,128)S(1)}, u32[]{:S(2)}, u32[]{:S(2)}) collective-permute-start(f32[512,128]{1,0:T(8,128)} %grads_ref.1), channel_id=1, source_target_pairs={{0,1},{1,0},{2,3},{3,2},{4,5},{5,4},{6,7},{7,6},{8,9},{9,8},{10,11... | collective-permute-start | bytes 786440 | tf_op jit(solution)/shard_map/ppermute | solution.py:416
  0.8 8.3 %collective-permute-start = (s32[2,1024]{1,0:T(2,128)}, s32[2,1024]{1,0:T(2,128)S(1)}, u32[]{:S(2)}, u32[]{:S(2)}) collective-permute-start(s32[2,1024]{1,0:T(2,128)} %here_ref.3), channel_id=1, source_target_pairs={{0,2},{2,4},{4,6},{6,0},{1,3},{3,5},{5,7},{7,1},{8,10},{10,12},{12... | collective-permute-start | bytes 24584 | tf_op jit(solution)/shard_map/ppermute | solution.py:416
  2.3 7.2 %collective-permute-start.1 = (s32[2,1024]{1,0:T(2,128)}, s32[2,1024]{1,0:T(2,128)S(1)}, u32[]{:S(2)}, u32[]{:S(2)}) collective-permute-start(s32[2,1024]{1,0:T(2,128)} %here_ref.3), channel_id=1, source_target_pairs={{0,4},{2,6},{4,0},{6,2},{1,5},{3,7},{5,1},{7,3},{8,12},{10,14},{12... | collective-permute-start | bytes 24584 | tf_op jit(solution)/shard_map/ppermute | solution.py:416
  5.1 4.4 %collective-permute-start.2 = (s32[2,1024]{1,0:T(2,128)}, s32[2,1024]{1,0:T(2,128)S(1)}, u32[]{:S(2)}, u32[]{:S(2)}) collective-permute-start(s32[2,1024]{1,0:T(2,128)} %here_ref.3), channel_id=1, source_target_pairs={{0,6},{2,0},{4,2},{6,4},{1,7},{3,1},{5,3},{7,5},{8,14},{10,8},{12,... | collective-permute-start | bytes 24584 | tf_op jit(solution)/shard_map/ppermute | solution.py:416
  6.5 3.0 %collective-permute-start.3 = (bf16[512,128]{1,0:T(8,128)(2,1)}, bf16[512,128]{1,0:T(8,128)(2,1)S(1)}, u32[]{:S(2)}, u32[]{:S(2)}) collective-permute-start(bf16[512,128]{1,0:T(8,128)(2,1)} %points_ref.1), channel_id=1, source_target_pairs={{0,1},{1,0},{2,3},{3,2},{4,5},{5,4},{6,7},{7,6},{8,9},{9,8},{10,11... | collective-permute-start | bytes 393224 | tf_op jit(solution)/shard_map/ppermute | solution.py:416
  9.0 48.0 %collective-permute-start.11 = (s32[2048]{0:T(1024)S(1)}, s32[2048]{0:T(1024)S(1)}, u32[]{:S(2)}, u32[]{:S(2)}) collective-permute-start(s32[2048]{0:T(1024)S(1)} %bitcast.81), channel_id=1, source_target_pairs={{0,1},{1,0},{2,3},{3,2},{4,5},{5,4},{6,7},{7,6},{8,9},{9,8},{10,11... | collective-permute-start | bytes 24584 | tf_op jit(solution)/shard_map/ppermute | solution.py:416
  13.8 32.1 %all-to-all-start.3 = ((bf16[128,16,128]{2,1,0:T(8,128)(2,1)}), bf16[128,16,128]{2,1,0:T(8,128)(2,1)S(1)}, u32[]{:S(2)}, u32[]{:S(2)}) async-start(bf16[128,16,128]{2,1,0:T(8,128)(2,1)} %bitcast.12), calls=%async_computation.3 | async-start | bytes 1048576 | tf_op jit(solution)/shard_map/all_to_all | solution.py:452
  28.4 20.9 %copy-start = (f32[512,128]{1,0:T(8,128)S(1)}, f32[512,128]{1,0:T(8,128)}, u32[]{:S(2)}) copy-start(f32[512,128]{1,0:T(8,128)} %grads_ref.1) | copy-start | bytes 786436
  28.4 27.8 %collective-permute-start.6 = (bf16[512,128]{1,0:T(8,128)(2,1)}, bf16[512,128]{1,0:T(8,128)(2,1)S(1)}, u32[]{:S(2)}, u32[]{:S(2)}) collective-permute-start(bf16[512,128]{1,0:T(8,128)(2,1)} %points_ref.1), channel_id=1, source_target_pairs={{0,2},{2,4},{4,6},{6,0},{1,3},{3,5},{5,7},{7,1},{8,10},{10,12},{12... | collective-permute-start | bytes 393224 | tf_op jit(solution)/shard_map/ppermute | solution.py:416
  30.0 27.0 %collective-permute-start.8 = (bf16[512,128]{1,0:T(8,128)(2,1)}, bf16[512,128]{1,0:T(8,128)(2,1)S(1)}, u32[]{:S(2)}, u32[]{:S(2)}) collective-permute-start(bf16[512,128]{1,0:T(8,128)(2,1)} %points_ref.1), channel_id=1, source_target_pairs={{0,6},{2,0},{4,2},{6,4},{1,7},{3,1},{5,3},{7,5},{8,14},{10,8},{12,... | collective-permute-start | bytes 393224 | tf_op jit(solution)/shard_map/ppermute | solution.py:416
  34.5 1.4 %collective-permute-start.5 = (s32[1,1]{1,0:T(1,128)}, s32[1,1]{1,0:T(1,128)}, u32[]{:S(2)}, u32[]{:S(2)}) collective-permute-start(s32[1,1]{1,0:T(1,128)} %get-tuple-element.111), channel_id=1, source_target_pairs={{0,1},{1,0},{2,3},{3,2},{4,5},{5,4},{6,7},{7,6},{8,9},{9,8},{10,11... | collective-permute-start | bytes 20 | tf_op jit(solution)/shard_map/ppermute | solution.py:416
  49.2 21.5 %all-to-all-start.4 = ((bf16[32,64,128]{2,1,0:T(8,128)(2,1)}), bf16[32,64,128]{2,1,0:T(8,128)(2,1)S(1)}, u32[]{:S(2)}, u32[]{:S(2)}) async-start(bf16[32,64,128]{2,1,0:T(8,128)(2,1)} %get-tuple-element.112), calls=%async_computation.4 | async-start | bytes 1048576 | tf_op jit(solution)/shard_map/all_to_all | solution.py:476
  56.2 5.6 %collective-permute-start.7 = (bf16[256,128]{1,0:T(8,128)(2,1)S(1)}, bf16[256,128]{1,0:T(8,128)(2,1)S(1)}, u32[]{:S(2)}, u32[]{:S(2)}) collective-permute-start(bf16[256,128]{1,0:T(8,128)(2,1)S(1)} %slice.32), channel_id=1, source_target_pairs={{0,2},{2,4},{4,6},{6,0},{1,3},{3,5},{5,7},{7,1},{8,10},{10,12},{12... | collective-permute-start | bytes 196616 | tf_op jit(solution)/shard_map/ppermute | solution.py:416
  57.0 4.7 %collective-permute-start.9 = (bf16[256,128]{1,0:T(8,128)(2,1)S(1)}, bf16[256,128]{1,0:T(8,128)(2,1)S(1)}, u32[]{:S(2)}, u32[]{:S(2)}) collective-permute-start(bf16[256,128]{1,0:T(8,128)(2,1)S(1)} %slice.33), channel_id=1, source_target_pairs={{0,6},{2,0},{4,2},{6,4},{1,7},{3,1},{5,3},{7,5},{8,14},{10,8},{12,... | collective-permute-start | bytes 196616 | tf_op jit(solution)/shard_map/ppermute | solution.py:416
  70.7 12.4 %collective-permute-start.10 = (bf16[2048,128]{1,0:T(8,128)(2,1)S(1)}, bf16[2048,128]{1,0:T(8,128)(2,1)S(1)}, u32[]{:S(2)}, u32[]{:S(2)}) collective-permute-start(bf16[2048,128]{1,0:T(8,128)(2,1)S(1)} %bitcast.69), channel_id=1, source_target_pairs={{0,1},{1,0},{2,3},{3,2},{4,5},{5,4},{6,7},{7,6},{8,9},{9,8},{10,11... | collective-permute-start | bytes 1572872 | tf_op jit(solution)/shard_map/ppermute | solution.py:416
  77.3 23.3 %all-to-all-start.5 = ((bf16[32,8,1024]{2,1,0:T(8,128)(2,1)}), bf16[32,8,1024]{2,1,0:T(8,128)(2,1)S(1)}, u32[]{:S(2)}, u32[]{:S(2)}) async-start(bf16[32,8,1024]{2,1,0:T(8,128)(2,1)} %get-tuple-element.114), calls=%async_computation.5 | async-start | bytes 1048576 | tf_op jit(solution)/shard_map/all_to_all | solution.py:480
  100.6 8.7 %collective-permute-start.12 = (bf16[2,128,1024]{2,1,0:T(8,128)(2,1)S(1)}, bf16[2,128,1024]{2,1,0:T(8,128)(2,1)S(1)}, u32[]{:S(2)}, u32[]{:S(2)}) collective-permute-start(bf16[2,128,1024]{2,1,0:T(8,128)(2,1)S(1)} %bitcast.60), channel_id=1, source_target_pairs={{0,1},{1,0},{2,3},{3,2},{4,5},{5,4},{6,7},{7,6},{8,9},{9,8},{10,11... | collective-permute-start | bytes 1572872 | tf_op jit(solution)/shard_map/ppermute | solution.py:416
  100.6 30.1 %all-to-all-start.6 = ((bf16[32,8,1024]{2,1,0:T(8,128)(2,1)}), bf16[32,8,1024]{2,1,0:T(8,128)(2,1)S(1)}, u32[]{:S(2)}, u32[]{:S(2)}) async-start(bf16[32,8,1024]{2,1,0:T(8,128)(2,1)} %get-tuple-element.119), calls=%async_computation.6 | async-start | bytes 1048576 | tf_op jit(solution)/shard_map/all_to_all | solution.py:493
  112.3 8.7 %collective-permute-start.13 = (f32[256,128]{1,0:T(8,128)S(1)}, f32[256,128]{1,0:T(8,128)S(1)}, u32[]{:S(2)}, u32[]{:S(2)}) collective-permute-start(f32[256,128]{1,0:T(8,128)S(1)} %get-tuple-element.160), channel_id=1, source_target_pairs={{0,2},{2,4},{4,6},{6,0},{1,3},{3,5},{5,7},{7,1},{8,10},{10,12},{12... | collective-permute-start | bytes 393224 | tf_op jit(solution)/shard_map/ppermute | solution.py:416
  112.4 8.6 %collective-permute-start.15 = (f32[256,128]{1,0:T(8,128)S(1)}, f32[256,128]{1,0:T(8,128)S(1)}, u32[]{:S(2)}, u32[]{:S(2)}) collective-permute-start(f32[256,128]{1,0:T(8,128)S(1)} %get-tuple-element.161), channel_id=1, source_target_pairs={{0,6},{2,0},{4,2},{6,4},{1,7},{3,1},{5,3},{7,5},{8,14},{10,8},{12,... | collective-permute-start | bytes 393224 | tf_op jit(solution)/shard_map/ppermute | solution.py:416
  121.1 8.9 %collective-permute-start.14 = (f32[512,128]{1,0:T(8,128)S(1)}, f32[512,128]{1,0:T(8,128)S(1)}, u32[]{:S(2)}, u32[]{:S(2)}) collective-permute-start(f32[512,128]{1,0:T(8,128)S(1)} %pad_maximum_fusion.1), channel_id=1, source_target_pairs={{0,2},{2,4},{4,6},{6,0},{1,3},{3,5},{5,7},{7,1},{8,10},{10,12},{12... | collective-permute-start | bytes 786440 | tf_op jit(solution)/shard_map/ppermute | solution.py:416
  121.2 8.8 %collective-permute-start.16 = (f32[512,128]{1,0:T(8,128)S(1)}, f32[512,128]{1,0:T(8,128)S(1)}, u32[]{:S(2)}, u32[]{:S(2)}) collective-permute-start(f32[512,128]{1,0:T(8,128)S(1)} %pad_maximum_fusion.2), channel_id=1, source_target_pairs={{0,6},{2,0},{4,2},{6,4},{1,7},{3,1},{5,3},{7,5},{8,14},{10,8},{12,... | collective-permute-start | bytes 786440 | tf_op jit(solution)/shard_map/ppermute | solution.py:416

commit v3 on v2

--- a/solution.py
+++ b/solution.py
@@ -9,19 +9,22 @@
 ITERS = 8
 RIDGE = 1.0
 LOG2E = 1.4426950408889634
-DEVICES = ("z", "y", "x", "k")
-ROUTE = ("x", "z", "y")
-ROWS = ("z", "y")
+DEVICES = ("zh", "zl", "y", "x", "k")
+ROUTE = ("x", "zh", "zl", "y")
+ROWS = ("zh", "zl", "y")
+NEAR = ("zl", "y")
 TRANSPOSED = (((1,), (1,)), ((), ()))
 FIRST = (((0,), (0,)), ((), ()))
 MIB = 1 << 20
-POINT_SLOTS = 10
+POINT_SLOTS = 12
+PIECES = 2
 GRAD_SLOTS = 32
 SLOTS = 16
 FEW = 8
 CHIPS = 128
 XS = 4
 OWN = 1024
+SHARE = 256
 NONE = 1 << 20
 
 
@@ -69,11 +72,24 @@
     earlier = ((left // groups == right // groups) & (right < left)).astype(jnp.bfloat16)
     before = jnp.dot(earlier, count.astype(jnp.bfloat16), preferred_element_type=jnp.float32)
     block_rank = rank + before
-
-    lanes = iota((devices, own), 1)
+    span = SHARE // share
+    earlier = ((left // span == right // span) & (right < left)).astype(jnp.bfloat16)
+    rank = rank + jnp.dot(earlier, count.astype(jnp.bfloat16), preferred_element_type=jnp.float32)
+
+    lanes = iota((devices, 128), 1)
     first = (number * POINT_SLOTS).astype(jnp.float32)
+    found = jnp.zeros((devices, 128), jnp.float32)
     for slot in range(POINT_SLOTS):
         chosen = jnp.sum(jnp.where(rank == first + slot, code, 0.0), axis=1, keepdims=True)
+        high = jnp.floor(chosen * 0.125)
+        found = jnp.where(lanes == slot, high, jnp.where(lanes == slot + 64, chosen - 8.0 * high, found))
+    lines = devices // len(tables)
+    shares = lines // span
+    reach = ((left // lines == right // lines) & (left % shares == right % lines // span)).astype(jnp.bfloat16)
+    found = jnp.dot(reach, found.astype(jnp.bfloat16), preferred_element_type=jnp.float32)
+    lanes = iota((devices, own), 1)
+    for slot in range(POINT_SLOTS):
+        chosen = 8.0 * found[:, slot : slot + 1] + found[:, slot + 64 : slot + 65]
         pick = (lanes + 1 == chosen.astype(jnp.int32)).astype(jnp.bfloat16)
         rows_ref[pl.ds(slot, devices, stride=SLOTS), :] = jnp.dot(
             pick[:, :each], points_ref[...], preferred_element_type=jnp.float32
@@ -83,11 +99,13 @@
     keep = iota((blocks, 128), 1) // per == iota((blocks, 128), 0)
     parts = []
     left = jnp.concatenate([grads_ref[...], other_grads_ref[...]], axis=0)
-    for _ in range(3):
+    for _ in range(PIECES):
         part = left.astype(jnp.bfloat16)
         left = left - part.astype(jnp.float32)
         parts.append(part)
-    for turn in range(GRAD_SLOTS // per):
+
+    @pl.loop(0, GRAD_SLOTS // per)
+    def _(turn):
         first = (number * GRAD_SLOTS + turn * per).astype(jnp.float32)
         found = jnp.zeros((devices, 128), jnp.float32)
         for slot in range(per):
@@ -108,11 +126,12 @@
                 by = (target - block) * per % 128
                 turned = pltpu.roll(taken, by, 1) if by else taken
                 message[block] = jnp.where(places == target, turned, message[block])
-        left = jnp.concatenate(message, axis=0)
-        for place in range(3):
-            part = left.astype(jnp.bfloat16).astype(jnp.float32)
-            left = left - part
-            rows_ref[pl.ds(POINT_SLOTS + 3 * turn + place, devices, stride=SLOTS), :] = part
+        rest = jnp.concatenate(message, axis=0)
+        for place in range(PIECES):
+            part = rest.astype(jnp.bfloat16).astype(jnp.float32)
+            rest = rest - part
+            rows_ref[pl.ds(POINT_SLOTS + PIECES * turn + place, devices, stride=SLOTS), :] = part
+
     out_ref[...] = rows_ref[...].astype(jnp.bfloat16)
 
 
@@ -138,7 +157,7 @@
 def ranks_kernel(here_ref, one_ref, two_ref, three_ref, block_row_ref, block_column_ref, rounds_ref, rank_ref):
     tables = (here_ref, one_ref, two_ref, three_ref)
     per_shard, width = here_ref.shape
-    share = width // 16
+    share = SHARE
     segments = iota((width, 128), 0) // share == iota((width, 128), 1)
     segments = segments | (iota((width, 128), 1) == 127)
     segments = segments.astype(jnp.bfloat16)
@@ -204,26 +223,27 @@
     ).astype(jnp.int32)
     slot = rank - number * POINT_SLOTS
     code = jnp.where((slot >= 0) & (slot < POINT_SLOTS), column_owner * SLOTS + slot, -1)
-    pick = (iota((share, length), 1) == code).astype(jnp.bfloat16)
-    piece = jnp.dot(pick, message_ref[...], preferred_element_type=jnp.float32).astype(jnp.bfloat16)
-    for copy in range(piece_ref.shape[0]):
-        piece_ref[copy] = piece
-
     slot = rank_ref[...] - number * GRAD_SLOTS
     wanted = owner_place(block_ref[...], OWN, XS, CHIPS // XS) * turns + slot // per
     wanted = jnp.where((slot >= 0) & (slot < GRAD_SLOTS), wanted, -NONE)
     step = 256
-    def gather(number, found):
+    def gather(number, state):
+        found, piece = state
         start = pl.multiple_of(number * step, step)
+        message = message_ref[pl.ds(start, step), :]
         line = iota((step, width), 0)
-        turn = (line % SLOTS - POINT_SLOTS + 3) // 3 - 1
+        turn = (line % SLOTS - POINT_SLOTS + PIECES) // PIECES - 1
         source = jnp.where((turn >= 0) & (turn < turns), line // SLOTS * turns + turn, 2 * NONE)
         pick = (source == wanted - number * (step // SLOTS * turns)).astype(jnp.bfloat16)
-        return found + lax.dot_general(
-            message_ref[pl.ds(start, step), :], pick, FIRST, preferred_element_type=jnp.float32
-        )
-
-    found = lax.fori_loop(0, length // step, gather, jnp.zeros((128, width), jnp.float32), unroll=2)
+        found = found + lax.dot_general(message, pick, FIRST, preferred_element_type=jnp.float32)
+        pick = (iota((share, step), 1) == code - start).astype(jnp.bfloat16)
+        return found, piece + jnp.dot(pick, message, preferred_element_type=jnp.float32)
+
+    state = jnp.zeros((128, width), jnp.float32), jnp.zeros((share, 128), jnp.float32)
+    found, piece = lax.fori_loop(0, length // step, gather, state)
+    piece = piece.astype(jnp.bfloat16)
+    for copy in range(piece_ref.shape[0]):
+        piece_ref[copy] = piece
     here = iota((per, width), 0) == slot % per
     for target in range(FEW):
         part = found[target * per : (target + 1) * per]
@@ -430,18 +450,17 @@
     targets = gradient.shape[1]
     blocks, width = panel_index.shape
     shard = blocks * width
-    zs, ys, xs, ks = (lax.axis_size(name) for name in DEVICES)
-    z, y, x, core = (lax.axis_index(name) for name in DEVICES)
-    rows, cols = zs * ys, xs * ks
-    row = z * ys + y
+    rows, near, xs, ks = (lax.axis_size(name) for name in (ROWS, NEAR, "x", "k"))
+    cols = xs * ks
+    row, x, core = lax.axis_index(ROWS), lax.axis_index("x"), lax.axis_index("k")
     group_start = row * own * cols
-    share = shard // rows
+    share = shard // near
     groups = targets // FEW
 
     tables = [panel_index] + [shift(panel_index, "x", by) for by in range(1, xs)]
     other_points = shift(points, "k", 1)
     other_grads = shift(gradient, "k", 1)
-    own_share = lax.dynamic_index_in_dim(panel_index.reshape(rows, share), row, 0, False)
+    own_share = lax.dynamic_index_in_dim(panel_index.reshape(near, share), row % near, 0, False)
     block = row // groups
     block_index = lax.dynamic_index_in_dim(panel_index, block, 0, False)
     start = (row * xs + x) * own * ks
@@ -452,7 +471,7 @@
         return lax.all_to_all(message, ROUTE, 0, 0)
 
     def exchange_by_axis(message):
-        message = message.reshape(xs, zs, ys, SLOTS, 128)
+        message = message.reshape(*(lax.axis_size(axis) for axis in ROUTE), SLOTS, 128)
         for dim, axis in enumerate(ROUTE):
             message = lax.all_to_all(message, axis, dim, dim, tiled=True)
         return message
@@ -461,7 +480,7 @@
         scalars = jnp.stack([number, start, x, core]).astype(jnp.int32)
         message = pack(scalars, tables, points, other_points, gradient, other_grads).reshape(rows * xs, SLOTS, 128)
         message = exchange(message).reshape(rows * xs * SLOTS, 128)
-        return place(scalars, message, own_share, block_index, rank, rows)
+        return place(scalars, message, own_share, block_index, rank, near)
 
     def further(state):
         number, piece, right = state
@@ -473,7 +492,7 @@
     _, piece, right_side = lax.while_loop(
         lambda state: state[0] < last, further, (jnp.int32(1), piece, right_side)
     )
-    chosen = lax.all_to_all(piece, ROWS, 0, 0).reshape(shard, features)
+    chosen = lax.all_to_all(piece, NEAR, 0, 0).reshape(shard, features)
 
     own_block = lax.dynamic_index_in_dim(chosen.reshape(blocks, width, features), block, 0, False)
     half, rest = solve(own_block, right_side, rows)
@@ -508,7 +527,7 @@
 
 
 def solution(mesh):
-    fine = Mesh(mesh.devices.reshape(8, 4, 4, 2), DEVICES)
+    fine = Mesh(mesh.devices.reshape(4, 2, 4, 4, 2), DEVICES)
     in_specs = (P(DEVICES, None), P(DEVICES, None), P(("x", "k"), None))
     out_specs = (P(DEVICES, None), P(("x", "k"), None))
     return jax.shard_map(on_device, mesh=fine, in_specs=in_specs, out_specs=out_specs, check_vma=False)

time: 133 us -> 131 us (0.985)
  waiting for transfers between devices: 23.1 us -> 16.5 us
  Pallas kernels: 44.3 us -> 47.8 us
  starting transfers between devices: 54.1 us -> 55.7 us
    all_to_all x1, waiting for transfers between devices: 7.18 us -> 0.01 us  [on_device(): chosen = lax.all_to_all(piece, NEAR, 0, 0).reshape(shard, features)]
    pallas_call x1, Pallas kernels: 3.37 us -> 5.51 us  [place(): pl.pallas_call(place_kernel, out_shape=(jax.ShapeDtypeStruct((copies, sha...]
    pallas_call x1, Pallas kernels: 4.28 us -> 5.7 us  [pack(): pl.pallas_call(pack_kernel, out_shape=jax.ShapeDtypeStruct((devices * SLO...]
  transfers between devices with their start and end apart: 21 -> 21, of which waited for: 6 -> 6; matrix products, arithmetic and copies ran while one was open for 6% -> 6% of each run, Pallas kernels for 33% -> 36%
where the time goes in v3:
time: 131 us; the launch traced here: 130 us
  starting transfers between devices  55.7 us (43%)
  Pallas kernels  47.8 us (36%)
  waiting for transfers between devices  16.5 us (13%)
  local copies, waits for them, and re-layouts  4.58 us (3%)
  other arithmetic  3.01 us (2%)
  between operations  2.24 us (2%)
    ppermute x17, starting transfers between devices, shift(): lax.ppermute(value, axis, [(i, (i + by) % size) for i in range(size)])  20 us
    all_to_all x1, starting transfers between devices, exchange(): return lax.all_to_all(message, ROUTE, 0, 0)  15 us
    pallas_call x1, Pallas kernels, build_tile(): pl.pallas_call(tile_kernel, grid=(count // block,), out_shape=jax.ShapeDt...  14.7 us
    pallas_call x3, Pallas kernels, product(): pl.pallas_call(product_kernel, grid=(count // line,), out_shape=jax.Shape...  11.4 us
    all_to_all x1, starting transfers between devices, on_device(): rest = lax.all_to_all(rest, ROWS, 0, 0).reshape(blocks, targets, width)  8.63 us
    all_to_all x1, waiting for transfers between devices, exchange(): return lax.all_to_all(message, ROUTE, 0, 0)  8.21 us
    ppermute x17, waiting for transfers between devices, shift(): lax.ppermute(value, axis, [(i, (i + by) % size) for i in range(size)])  7.2 us
    all_to_all x1, starting transfers between devices, on_device(): half = lax.all_to_all(half, ROWS, 0, 0).reshape(blocks, targets, width)  7.05 us
  transfers between devices with their start and end apart: 21, of which 6 were waited for; matrix products, arithmetic and copies ran while one was open for 6% of the time, Pallas kernels for 36%

profile of v3, /device:TPU:8, one launch (start us, length us, event | category | flops | bytes accessed | tf_op | source)
XLA Modules:
  0.0 129.9 jit_solution(2595952029600659612)
XLA Ops:
  0.6 0.0 copy-start.2
  0.6 0.0 copy-start.1
  0.7 0.1 collective-permute-start.4
  0.8 0.5 collective-permute-start.3
  1.3 1.5 %collective-permute-start = (s32[2,1024]{1,0:T(2,128)}, s32[2,1024]{1,0:T(2,128)S(1)}, u32[]{:S(2)}, u32[]{:S(2)}) collective-permute-start(s32[2,1024]{1,0:T(2,128)} %here_ref.3), channel_id=1, source_target_pairs={{0,2},{2,4},{4,6},{6,0},{1,3},{3,5},{5,7},{7,1},{8,10},{10,12},{12... | collective-permute-start | bytes 24584 | tf_op jit(solution)/shard_map/ppermute | solution.py:436
  2.7 2.7 %collective-permute-start.1 = (s32[2,1024]{1,0:T(2,128)}, s32[2,1024]{1,0:T(2,128)S(1)}, u32[]{:S(2)}, u32[]{:S(2)}) collective-permute-start(s32[2,1024]{1,0:T(2,128)} %here_ref.3), channel_id=1, source_target_pairs={{0,4},{2,6},{4,0},{6,2},{1,5},{3,7},{5,1},{7,3},{8,12},{10,14},{12... | collective-permute-start | bytes 24584 | tf_op jit(solution)/shard_map/ppermute | solution.py:436
  5.5 1.4 %collective-permute-start.2 = (s32[2,1024]{1,0:T(2,128)}, s32[2,1024]{1,0:T(2,128)S(1)}, u32[]{:S(2)}, u32[]{:S(2)}) collective-permute-start(s32[2,1024]{1,0:T(2,128)} %here_ref.3), channel_id=1, source_target_pairs={{0,6},{2,0},{4,2},{6,4},{1,7},{3,1},{5,3},{7,5},{8,14},{10,8},{12,... | collective-permute-start | bytes 24584 | tf_op jit(solution)/shard_map/ppermute | solution.py:436
  6.9 0.1 pad_add_fusion.2.scalar_ref
  7.0 0.7 reshape.60
  7.7 0.7 copy.33
  8.4 0.9 collective-permute-done.2.three_ref
  9.3 5.7 %pack.2 = bf16[2048,128]{1,0:T(8,128)(2,1)} custom-call(s32[4]{0:T(128)S(1)} %pad_add_fusion.2.scalar_ref, s32[2,1024]{1,0:T(2,128)} %here_ref.3, s32[2,1024]{1,0:T(2,128)S(1)} %collective-permute-done.one_ref, s32[2,1024]{1,0:T(2,128)S(1)} %collective-permute-done.1.two_ref, s32[2,1024]{1,0:T(2,128)S(1)} %collective-permute-done.2.three_ref, ...), custom_call_target="tpu_custom_call" | custom-call | tf_op jit(solution)/shard_map/pack/pallas_call | solution.py:142
  15.0 15.0 %all-to-all-start.4 = ((bf16[128,16,128]{2,1,0:T(8,128)(2,1)}), bf16[128,16,128]{2,1,0:T(8,128)(2,1)S(1)}, u32[]{:S(2)}, u32[]{:S(2)}) async-start(bf16[128,16,128]{2,1,0:T(8,128)(2,1)} %bitcast.12), calls=%async_computation.4 | async-start | bytes 1048576 | tf_op jit(solution)/shard_map/all_to_all | solution.py:471
  30.0 0.2 copy.25.block_column_ref
  30.3 0.1 copy.26.column_ref
  30.5 1.6 %collective-permute-start.6 = (bf16[512,128]{1,0:T(8,128)(2,1)}, bf16[512,128]{1,0:T(8,128)(2,1)S(1)}, u32[]{:S(2)}, u32[]{:S(2)}) collective-permute-start(bf16[512,128]{1,0:T(8,128)(2,1)} %points_ref.1), channel_id=1, source_target_pairs={{0,2},{2,4},{4,6},{6,0},{1,3},{3,5},{5,7},{7,1},{8,10},{10,12},{12... | collective-permute-start | bytes 393224 | tf_op jit(solution)/shard_map/ppermute | solution.py:436
  32.2 1.7 %collective-permute-start.8 = (bf16[512,128]{1,0:T(8,128)(2,1)}, bf16[512,128]{1,0:T(8,128)(2,1)S(1)}, u32[]{:S(2)}, u32[]{:S(2)}) collective-permute-start(bf16[512,128]{1,0:T(8,128)(2,1)} %points_ref.1), channel_id=1, source_target_pairs={{0,6},{2,0},{4,2},{6,4},{1,7},{3,1},{5,3},{7,5},{8,14},{10,8},{12,... | collective-permute-start | bytes 393224 | tf_op jit(solution)/shard_map/ppermute | solution.py:436
  33.9 2.7 %ranks.1 = (s32[1,1]{1,0:T(1,128)}, s32[1,1024]{1,0:T(1,128)S(1)}) custom-call(s32[2,1024]{1,0:T(2,128)S(1)} %copy-done.1, s32[2,1024]{1,0:T(2,128)S(1)} %collective-permute-done.one_ref, s32[2,1024]{1,0:T(2,128)S(1)} %collective-permute-done.1.two_ref, s32[2,1024]{1,0:T(2,128)S(1)} %collective-permute-done.2.three_ref, ...), custom_call_target="tpu_custom_call" | custom-call | flops 4000000000 | bytes 100000 | tf_op jit(solution)/shard_map/ranks/pallas_call | solution.py:197
  36.6 1.3 %collective-permute-done.5 = s32[1,1]{1,0:T(1,128)} collective-permute-done((s32[1,1]{1,0:T(1,128)}, s32[1,1]{1,0:T(1,128)}, u32[]{:S(2)}, u32[]{:S(2)}) %collective-permute-start.5) | collective-permute-done | bytes 36 | tf_op jit(solution)/shard_map/ppermute | solution.py:436
  39.2 8.2 %all-to-all-done.4 = bf16[128,16,128]{2,1,0:T(8,128)(2,1)S(1)} async-done(((bf16[128,16,128]{2,1,0:T(8,128)(2,1)}), bf16[128,16,128]{2,1,0:T(8,128)(2,1)S(1)}, u32[]{:S(2)}, u32[]{:S(2)}) %all-to-all-start.4) | async-done | bytes 524320 | tf_op jit(solution)/shard_map/all_to_all | solution.py:471
  47.4 5.5 %place.2 = (bf16[8,256,128]{2,1,0:T(8,128)(2,1)}, f32[8,1024]{1,0:T(8,128)S(1)}) custom-call(s32[4]{0:T(128)S(1)} %pad_add_fusion.2.scalar_ref, bf16[2048,128]{1,0:T(8,128)(2,1)S(1)} %bitcast.64, s32[1,256]{1,0:T(1,128)S(1)} %constant_dynamic-slice_fusion.1.row_ref, s32[256,1]{1,0:T(8,128)S(1)} %copy.26.column_ref, ...), custom_call_target="tpu_custom_call" | custom-call | tf_op jit(solution)/shard_map/place/pallas_call | solution.py:256
  52.9 5.0 %all-to-all-start.5 = ((bf16[8,256,128]{2,1,0:T(8,128)(2,1)}), bf16[8,256,128]{2,1,0:T(8,128)(2,1)S(1)}, u32[]{:S(2)}, u32[]{:S(2)}) async-start(bf16[8,256,128]{2,1,0:T(8,128)(2,1)} %get-tuple-element.112), calls=%async_computation.5 | async-start | bytes 1048576 | tf_op jit(solution)/shard_map/all_to_all | solution.py:495
  57.9 0.1 add_bitcast_fusion
  58.0 1.3 %copy.30 = s32[1,2048]{0,1:T(8,128)} copy(s32[1,2048]{1,0:T(1,128)S(1)} %bitcast.80) | data formatting | bytes 16384
  59.4 0.8 collective-permute-start.7
  60.2 2.6 %collective-permute-start.9 = (bf16[256,128]{1,0:T(8,128)(2,1)S(1)}, bf16[256,128]{1,0:T(8,128)(2,1)S(1)}, u32[]{:S(2)}, u32[]{:S(2)}) collective-permute-start(bf16[256,128]{1,0:T(8,128)(2,1)S(1)} %slice.33), channel_id=1, source_target_pairs={{0,6},{2,0},{4,2},{6,4},{1,7},{3,1},{5,3},{7,5},{8,14},{10,8},{12,... | collective-permute-start | bytes 196616 | tf_op jit(solution)/shard_map/ppermute | solution.py:436
  62.8 2.1 %collective-permute-done.7 = bf16[256,128]{1,0:T(8,128)(2,1)S(1)} collective-permute-done((bf16[256,128]{1,0:T(8,128)(2,1)S(1)}, bf16[256,128]{1,0:T(8,128)(2,1)S(1)}, u32[]{:S(2)}, u32[]{:S(2)}) %collective-permute-start.7) | collective-permute-done | bytes 65568 | tf_op jit(solution)/shard_map/ppermute | solution.py:436
  65.0 0.9 constant_dynamic-update-slice_fusion.points_ref
  65.9 0.3 multiply_reduce_fusion.1
  66.3 0.4 copy.27.column_ref
  66.7 0.1 collective-permute-start.10
  66.8 6.6 %solve.1 = (bf16[32,8,1024]{2,1,0:T(8,128)(2,1)}, bf16[32,8,1024]{2,1,0:T(8,128)(2,1)}) custom-call(bf16[1024,128]{1,0:T(8,128)(2,1)S(1)} %dynamic-slice_bitcast_fusion.points_ref, f32[8,1024]{1,0:T(8,128)S(1)} %get-tuple-element.113.right_ref), custom_call_target="tpu_custom_call" | custom-call | flops 6000000000 | bytes 1000000 | tf_op jit(solution)/shard_map/solve/pallas_call | solution.py:327
  73.4 7.1 %all-to-all-start.6 = ((bf16[32,8,1024]{2,1,0:T(8,128)(2,1)}), bf16[32,8,1024]{2,1,0:T(8,128)(2,1)S(1)}, u32[]{:S(2)}, u32[]{:S(2)}) async-start(bf16[32,8,1024]{2,1,0:T(8,128)(2,1)} %get-tuple-element.114), calls=%async_computation.6 | async-start | bytes 1048576 | tf_op jit(solution)/shard_map/all_to_all | solution.py:499
  80.5 1.1 pad_maximum_fusion.chosen_ref
  81.5 0.6 multiply_reduce_fusion
  82.1 14.7 %tile.1.refs_0_.refs_1_.refs_2_.refs_3_ = bf16[2048,4096]{1,0:T(8,128)(2,1)} custom-call(bf16[2048,128]{1,0:T(8,128)(2,1)S(1)} %constant_dynamic-update-slice_fusion.points_ref, f32[2048,1]{1,0:T(8,128)S(1)} %copy.27.column_ref, s32[2048,1]{1,0:T(8,128)} %bitcast.72, bf16[4096,128]{1,0:T(8,128)(2,1)} %pad_maximum_fusion.chosen_ref, f32[1,4096]{1,0:T(1,128)S(1)} %bitcast.66, ...), custom_call_target="tpu_custom_call" | custom-call | flops 8589934592 | bytes 16777216 | tf_op jit(solution)/shard_map/tile/pallas_call | solution.py:359
  96.8 1.1 all-to-all-done.6
  98.0 8.6 %all-to-all-start.7 = ((bf16[32,8,1024]{2,1,0:T(8,128)(2,1)}), bf16[32,8,1024]{2,1,0:T(8,128)(2,1)S(1)}, u32[]{:S(2)}, u32[]{:S(2)}) async-start(bf16[32,8,1024]{2,1,0:T(8,128)(2,1)} %get-tuple-element.119), calls=%async_computation.7 | async-start | bytes 1048576 | tf_op jit(solution)/shard_map/all_to_all | solution.py:512
  106.6 3.0 %product.5 = f32[512,128]{1,0:T(8,128)S(1)} custom-call(bf16[2048,4096]{1,0:T(8,128)(2,1)} %tile.1.refs_0_.refs_1_.refs_2_.refs_3_, bf16[2048,4096]{1,0:T(8,128)(2,1)} %tile.1.refs_0_.refs_1_.refs_2_.refs_3_, bf16[2048,4096]{1,0:T(8,128)(2,1)} %tile.1.refs_0_.refs_1_.refs_2_.refs_3_, bf16[2048,4096]{1,0:T(8,128)(2,1)} %tile.1.refs_0_.refs_1_.refs_2_.refs_3_, ...), custom_call_target="tpu_custom_call" | custom-call | flops 1073741824 | bytes 4194304 | tf_op jit(solution)/shard_map/product/pallas_call | solution.py:399
  109.6 0.1 collective-permute-start.13
  109.7 3.4 %collective-permute-start.15 = (f32[256,128]{1,0:T(8,128)S(1)}, f32[256,128]{1,0:T(8,128)S(1)}, u32[]{:S(2)}, u32[]{:S(2)}) collective-permute-start(f32[256,128]{1,0:T(8,128)S(1)} %get-tuple-element.161), channel_id=1, source_target_pairs={{0,6},{2,0},{4,2},{6,4},{1,7},{3,1},{5,3},{7,5},{8,14},{10,8},{12,... | collective-permute-start | bytes 393224 | tf_op jit(solution)/shard_map/ppermute | solution.py:436
  113.2 5.4 %product.4 = f32[1024,128]{1,0:T(8,128)S(1)} custom-call(bf16[2048,4096]{1,0:T(8,128)(2,1)} %tile.1.refs_0_.refs_1_.refs_2_.refs_3_, bf16[2048,4096]{1,0:T(8,128)(2,1)} %tile.1.refs_0_.refs_1_.refs_2_.refs_3_, bf16[2048,4096]{1,0:T(8,128)(2,1)} %tile.1.refs_0_.refs_1_.refs_2_.refs_3_, bf16[2048,4096]{1,0:T(8,128)(2,1)} %tile.1.refs_0_.refs_1_.refs_2_.refs_3_, ...), custom_call_target="tpu_custom_call" | custom-call | flops 2147483648 | bytes 8388608 | tf_op jit(solution)/shard_map/product/pallas_call | solution.py:399
  118.6 0.1 collective-permute-start.14
  118.8 3.3 %collective-permute-start.16 = (f32[512,128]{1,0:T(8,128)S(1)}, f32[512,128]{1,0:T(8,128)S(1)}, u32[]{:S(2)}, u32[]{:S(2)}) collective-permute-start(f32[512,128]{1,0:T(8,128)S(1)} %pad_maximum_fusion.2), channel_id=1, source_target_pairs={{0,6},{2,0},{4,2},{6,4},{1,7},{3,1},{5,3},{7,5},{8,14},{10,8},{12,... | collective-permute-start | bytes 786440 | tf_op jit(solution)/shard_map/ppermute | solution.py:436
  122.1 3.0 %product.3 = f32[512,128]{1,0:T(8,128)S(1)} custom-call(bf16[2048,4096]{1,0:T(8,128)(2,1)} %tile.1.refs_0_.refs_1_.refs_2_.refs_3_, bf16[2048,4096]{1,0:T(8,128)(2,1)} %tile.1.refs_0_.refs_1_.refs_2_.refs_3_, bf16[2048,4096]{1,0:T(8,128)(2,1)} %tile.1.refs_0_.refs_1_.refs_2_.refs_3_, bf16[2048,4096]{1,0:T(8,128)(2,1)} %tile.1.refs_0_.refs_1_.refs_2_.refs_3_, ...), custom_call_target="tpu_custom_call" | custom-call | flops 1073741824 | bytes 4194304 | tf_op jit(solution)/shard_map/product/pallas_call | solution.py:399
  125.1 2.7 %collective-permute-done.14 = f32[512,128]{1,0:T(8,128)S(1)} collective-permute-done((f32[512,128]{1,0:T(8,128)S(1)}, f32[512,128]{1,0:T(8,128)S(1)}, u32[]{:S(2)}, u32[]{:S(2)}) %collective-permute-start.14) | collective-permute-done | bytes 262176 | tf_op jit(solution)/shard_map/ppermute | solution.py:436
  127.8 0.8 add_add_fusion
  128.6 1.3 %finish.1 = f32[2048,128]{1,0:T(8,128)} custom-call(bf16[2,128,1024]{2,1,0:T(8,128)(2,1)S(1)} %bitcast.63, bf16[2,128,1024]{2,1,0:T(8,128)(2,1)S(1)} %bitcast.65), custom_call_target="tpu_custom_call" | custom-call | flops 1000000 | bytes 2000000 | tf_op jit(solution)/shard_map/finish/pallas_call | solution.py:423
  (41 shorter events, 0.3 us)
Async XLA Ops:
  0.6 29.9 %copy-start.2 = (s32[4]{0:T(128)S(1)}, s32[4]{0:T(128)}, u32[]{:S(2)}) copy-start(s32[4]{0:T(128)} %constant.91.clone) | copy-start | bytes 52
  0.6 29.4 %copy-start.1 = (s32[2,1024]{1,0:T(2,128)S(1)}, s32[2,1024]{1,0:T(2,128)}, u32[]{:S(2)}) copy-start(s32[2,1024]{1,0:T(2,128)} %here_ref.3) | copy-start | bytes 24580
  0.7 8.7 %collective-permute-start.4 = (f32[512,128]{1,0:T(8,128)}, f32[512,128]{1,0:T(8,128)S(1)}, u32[]{:S(2)}, u32[]{:S(2)}) collective-permute-start(f32[512,128]{1,0:T(8,128)} %grads_ref.1), channel_id=1, source_target_pairs={{0,1},{1,0},{2,3},{3,2},{4,5},{5,4},{6,7},{7,6},{8,9},{9,8},{10,11... | collective-permute-start | bytes 786440 | tf_op jit(solution)/shard_map/ppermute | solution.py:436
  0.8 8.6 %collective-permute-start.3 = (bf16[512,128]{1,0:T(8,128)(2,1)}, bf16[512,128]{1,0:T(8,128)(2,1)S(1)}, u32[]{:S(2)}, u32[]{:S(2)}) collective-permute-start(bf16[512,128]{1,0:T(8,128)(2,1)} %points_ref.1), channel_id=1, source_target_pairs={{0,1},{1,0},{2,3},{3,2},{4,5},{5,4},{6,7},{7,6},{8,9},{9,8},{10,11... | collective-permute-start | bytes 393224 | tf_op jit(solution)/shard_map/ppermute | solution.py:436
  1.3 7.1 %collective-permute-start = (s32[2,1024]{1,0:T(2,128)}, s32[2,1024]{1,0:T(2,128)S(1)}, u32[]{:S(2)}, u32[]{:S(2)}) collective-permute-start(s32[2,1024]{1,0:T(2,128)} %here_ref.3), channel_id=1, source_target_pairs={{0,2},{2,4},{4,6},{6,0},{1,3},{3,5},{5,7},{7,1},{8,10},{10,12},{12... | collective-permute-start | bytes 24584 | tf_op jit(solution)/shard_map/ppermute | solution.py:436
  2.7 5.7 %collective-permute-start.1 = (s32[2,1024]{1,0:T(2,128)}, s32[2,1024]{1,0:T(2,128)S(1)}, u32[]{:S(2)}, u32[]{:S(2)}) collective-permute-start(s32[2,1024]{1,0:T(2,128)} %here_ref.3), channel_id=1, source_target_pairs={{0,4},{2,6},{4,0},{6,2},{1,5},{3,7},{5,1},{7,3},{8,12},{10,14},{12... | collective-permute-start | bytes 24584 | tf_op jit(solution)/shard_map/ppermute | solution.py:436
  5.5 3.9 %collective-permute-start.2 = (s32[2,1024]{1,0:T(2,128)}, s32[2,1024]{1,0:T(2,128)S(1)}, u32[]{:S(2)}, u32[]{:S(2)}) collective-permute-start(s32[2,1024]{1,0:T(2,128)} %here_ref.3), channel_id=1, source_target_pairs={{0,6},{2,0},{4,2},{6,4},{1,7},{3,1},{5,3},{7,5},{8,14},{10,8},{12,... | collective-permute-start | bytes 24584 | tf_op jit(solution)/shard_map/ppermute | solution.py:436
  8.4 51.7 %collective-permute-start.11 = (s32[2048]{0:T(1024)S(1)}, s32[2048]{0:T(1024)S(1)}, u32[]{:S(2)}, u32[]{:S(2)}) collective-permute-start(s32[2048]{0:T(1024)S(1)} %bitcast.81), channel_id=1, source_target_pairs={{0,1},{1,0},{2,3},{3,2},{4,5},{5,4},{6,7},{7,6},{8,9},{9,8},{10,11... | collective-permute-start | bytes 24584 | tf_op jit(solution)/shard_map/ppermute | solution.py:436
  15.0 32.4 %all-to-all-start.4 = ((bf16[128,16,128]{2,1,0:T(8,128)(2,1)}), bf16[128,16,128]{2,1,0:T(8,128)(2,1)S(1)}, u32[]{:S(2)}, u32[]{:S(2)}) async-start(bf16[128,16,128]{2,1,0:T(8,128)(2,1)} %bitcast.12), calls=%async_computation.4 | async-start | bytes 1048576 | tf_op jit(solution)/shard_map/all_to_all | solution.py:471
  30.5 22.4 %copy-start = (f32[512,128]{1,0:T(8,128)S(1)}, f32[512,128]{1,0:T(8,128)}, u32[]{:S(2)}) copy-start(f32[512,128]{1,0:T(8,128)} %grads_ref.1) | copy-start | bytes 786436
  30.5 28.8 %collective-permute-start.6 = (bf16[512,128]{1,0:T(8,128)(2,1)}, bf16[512,128]{1,0:T(8,128)(2,1)S(1)}, u32[]{:S(2)}, u32[]{:S(2)}) collective-permute-start(bf16[512,128]{1,0:T(8,128)(2,1)} %points_ref.1), channel_id=1, source_target_pairs={{0,2},{2,4},{4,6},{6,0},{1,3},{3,5},{5,7},{7,1},{8,10},{10,12},{12... | collective-permute-start | bytes 393224 | tf_op jit(solution)/shard_map/ppermute | solution.py:436
  32.2 28.0 %collective-permute-start.8 = (bf16[512,128]{1,0:T(8,128)(2,1)}, bf16[512,128]{1,0:T(8,128)(2,1)S(1)}, u32[]{:S(2)}, u32[]{:S(2)}) collective-permute-start(bf16[512,128]{1,0:T(8,128)(2,1)} %points_ref.1), channel_id=1, source_target_pairs={{0,6},{2,0},{4,2},{6,4},{1,7},{3,1},{5,3},{7,5},{8,14},{10,8},{12,... | collective-permute-start | bytes 393224 | tf_op jit(solution)/shard_map/ppermute | solution.py:436
  36.6 1.4 %collective-permute-start.5 = (s32[1,1]{1,0:T(1,128)}, s32[1,1]{1,0:T(1,128)}, u32[]{:S(2)}, u32[]{:S(2)}) collective-permute-start(s32[1,1]{1,0:T(1,128)} %get-tuple-element.111), channel_id=1, source_target_pairs={{0,1},{1,0},{2,3},{3,2},{4,5},{5,4},{6,7},{7,6},{8,9},{9,8},{10,11... | collective-permute-start | bytes 20 | tf_op jit(solution)/shard_map/ppermute | solution.py:436
  52.9 13.7 %all-to-all-start.5 = ((bf16[8,256,128]{2,1,0:T(8,128)(2,1)}), bf16[8,256,128]{2,1,0:T(8,128)(2,1)S(1)}, u32[]{:S(2)}, u32[]{:S(2)}) async-start(bf16[8,256,128]{2,1,0:T(8,128)(2,1)} %get-tuple-element.112), calls=%async_computation.5 | async-start | bytes 1048576 | tf_op jit(solution)/shard_map/all_to_all | solution.py:495
  59.4 5.6 %collective-permute-start.7 = (bf16[256,128]{1,0:T(8,128)(2,1)S(1)}, bf16[256,128]{1,0:T(8,128)(2,1)S(1)}, u32[]{:S(2)}, u32[]{:S(2)}) collective-permute-start(bf16[256,128]{1,0:T(8,128)(2,1)S(1)} %slice.32), channel_id=1, source_target_pairs={{0,2},{2,4},{4,6},{6,0},{1,3},{3,5},{5,7},{7,1},{8,10},{10,12},{12... | collective-permute-start | bytes 196616 | tf_op jit(solution)/shard_map/ppermute | solution.py:436
  60.2 4.8 %collective-permute-start.9 = (bf16[256,128]{1,0:T(8,128)(2,1)S(1)}, bf16[256,128]{1,0:T(8,128)(2,1)S(1)}, u32[]{:S(2)}, u32[]{:S(2)}) collective-permute-start(bf16[256,128]{1,0:T(8,128)(2,1)S(1)} %slice.33), channel_id=1, source_target_pairs={{0,6},{2,0},{4,2},{6,4},{1,7},{3,1},{5,3},{7,5},{8,14},{10,8},{12,... | collective-permute-start | bytes 196616 | tf_op jit(solution)/shard_map/ppermute | solution.py:436
  66.7 13.8 %collective-permute-start.10 = (bf16[2048,128]{1,0:T(8,128)(2,1)S(1)}, bf16[2048,128]{1,0:T(8,128)(2,1)S(1)}, u32[]{:S(2)}, u32[]{:S(2)}) collective-permute-start(bf16[2048,128]{1,0:T(8,128)(2,1)S(1)} %bitcast.68), channel_id=1, source_target_pairs={{0,1},{1,0},{2,3},{3,2},{4,5},{5,4},{6,7},{7,6},{8,9},{9,8},{10,11... | collective-permute-start | bytes 1572872 | tf_op jit(solution)/shard_map/ppermute | solution.py:436
  73.4 24.5 %all-to-all-start.6 = ((bf16[32,8,1024]{2,1,0:T(8,128)(2,1)}), bf16[32,8,1024]{2,1,0:T(8,128)(2,1)S(1)}, u32[]{:S(2)}, u32[]{:S(2)}) async-start(bf16[32,8,1024]{2,1,0:T(8,128)(2,1)} %get-tuple-element.114), calls=%async_computation.6 | async-start | bytes 1048576 | tf_op jit(solution)/shard_map/all_to_all | solution.py:499
  97.9 8.6 %collective-permute-start.12 = (bf16[2,128,1024]{2,1,0:T(8,128)(2,1)S(1)}, bf16[2,128,1024]{2,1,0:T(8,128)(2,1)S(1)}, u32[]{:S(2)}, u32[]{:S(2)}) collective-permute-start(bf16[2,128,1024]{2,1,0:T(8,128)(2,1)S(1)} %bitcast.59), channel_id=1, source_target_pairs={{0,1},{1,0},{2,3},{3,2},{4,5},{5,4},{6,7},{7,6},{8,9},{9,8},{10,11... | collective-permute-start | bytes 1572872 | tf_op jit(solution)/shard_map/ppermute | solution.py:436
  98.0 30.6 %all-to-all-start.7 = ((bf16[32,8,1024]{2,1,0:T(8,128)(2,1)}), bf16[32,8,1024]{2,1,0:T(8,128)(2,1)S(1)}, u32[]{:S(2)}, u32[]{:S(2)}) async-start(bf16[32,8,1024]{2,1,0:T(8,128)(2,1)} %get-tuple-element.119), calls=%async_computation.7 | async-start | bytes 1048576 | tf_op jit(solution)/shard_map/all_to_all | solution.py:512
  109.6 8.9 %collective-permute-start.13 = (f32[256,128]{1,0:T(8,128)S(1)}, f32[256,128]{1,0:T(8,128)S(1)}, u32[]{:S(2)}, u32[]{:S(2)}) collective-permute-start(f32[256,128]{1,0:T(8,128)S(1)} %get-tuple-element.160), channel_id=1, source_target_pairs={{0,2},{2,4},{4,6},{6,0},{1,3},{3,5},{5,7},{7,1},{8,10},{10,12},{12... | collective-permute-start | bytes 393224 | tf_op jit(solution)/shard_map/ppermute | solution.py:436
  109.7 8.8 %collective-permute-start.15 = (f32[256,128]{1,0:T(8,128)S(1)}, f32[256,128]{1,0:T(8,128)S(1)}, u32[]{:S(2)}, u32[]{:S(2)}) collective-permute-start(f32[256,128]{1,0:T(8,128)S(1)} %get-tuple-element.161), channel_id=1, source_target_pairs={{0,6},{2,0},{4,2},{6,4},{1,7},{3,1},{5,3},{7,5},{8,14},{10,8},{12,... | collective-permute-start | bytes 393224 | tf_op jit(solution)/shard_map/ppermute | solution.py:436
  118.6 9.2 %collective-permute-start.14 = (f32[512,128]{1,0:T(8,128)S(1)}, f32[512,128]{1,0:T(8,128)S(1)}, u32[]{:S(2)}, u32[]{:S(2)}) collective-permute-start(f32[512,128]{1,0:T(8,128)S(1)} %pad_maximum_fusion.1), channel_id=1, source_target_pairs={{0,2},{2,4},{4,6},{6,0},{1,3},{3,5},{5,7},{7,1},{8,10},{10,12},{12... | collective-permute-start | bytes 786440 | tf_op jit(solution)/shard_map/ppermute | solution.py:436
  118.8 9.0 %collective-permute-start.16 = (f32[512,128]{1,0:T(8,128)S(1)}, f32[512,128]{1,0:T(8,128)S(1)}, u32[]{:S(2)}, u32[]{:S(2)}) collective-permute-start(f32[512,128]{1,0:T(8,128)S(1)} %pad_maximum_fusion.2), channel_id=1, source_target_pairs={{0,6},{2,0},{4,2},{6,4},{1,7},{3,1},{5,3},{7,5},{8,14},{10,8},{12,... | collective-permute-start | bytes 786440 | tf_op jit(solution)/shard_map/ppermute | solution.py:436

commit v4 on v3

--- a/solution.py
+++ b/solution.py
@@ -1,3 +1,5 @@
+import functools
+
 import jax
 import jax.numpy as jnp
 from jax import lax
@@ -39,7 +41,7 @@
 
 def pack_kernel(
     scalar_ref, here_ref, one_ref, two_ref, three_ref, points_ref, other_points_ref, grads_ref, other_grads_ref,
-    out_ref, values_ref, rows_ref, table_ref,
+    out_ref, values_ref, rows_ref, table_ref, *, unroll,
 ):
     tables = (here_ref, one_ref, two_ref, three_ref)
     per_shard, width = here_ref.shape
@@ -104,7 +106,7 @@
         left = left - part.astype(jnp.float32)
         parts.append(part)
 
-    @pl.loop(0, GRAD_SLOTS // per)
+    @pl.loop(0, GRAD_SLOTS // per, unroll=unroll)
     def _(turn):
         first = (number * GRAD_SLOTS + turn * per).astype(jnp.float32)
         found = jnp.zeros((devices, 128), jnp.float32)
@@ -135,12 +137,12 @@
     out_ref[...] = rows_ref[...].astype(jnp.bfloat16)
 
 
-def pack(scalars, tables, points, other_points, grads, other_grads):
+def pack(scalars, tables, points, other_points, grads, other_grads, unroll):
     targets = grads.shape[1]
     devices = len(tables) * tables[0].shape[0] * targets // FEW
     vmem = pl.BlockSpec(memory_space=pltpu.VMEM)
     return pl.pallas_call(
-        pack_kernel,
+        functools.partial(pack_kernel, unroll=unroll),
         out_shape=jax.ShapeDtypeStruct((devices * SLOTS, 128), jnp.bfloat16),
         in_specs=[pl.BlockSpec(memory_space=pltpu.SMEM)] + [vmem] * 8,
         out_specs=vmem,
@@ -208,7 +210,7 @@
     )(*tables, block_index[None, :], block_index[:, None])
 
 
-def place_kernel(scalar_ref, message_ref, row_ref, column_ref, block_ref, rank_ref, piece_ref, right_ref):
+def place_kernel(scalar_ref, message_ref, row_ref, column_ref, block_ref, rank_ref, piece_ref, right_ref, *, unroll):
     length = message_ref.shape[0]
     share = column_ref.shape[0]
     width = block_ref.shape[1]
@@ -240,7 +242,7 @@
         return found, piece + jnp.dot(pick, message, preferred_element_type=jnp.float32)
 
     state = jnp.zeros((128, width), jnp.float32), jnp.zeros((share, 128), jnp.float32)
-    found, piece = lax.fori_loop(0, length // step, gather, state)
+    found, piece = lax.fori_loop(0, length // step, gather, state, unroll=unroll)
     piece = piece.astype(jnp.bfloat16)
     for copy in range(piece_ref.shape[0]):
         piece_ref[copy] = piece
@@ -250,11 +252,11 @@
         right_ref[pl.ds(target, 1), :] = -jnp.sum(jnp.where(here, part, 0.0), axis=0, keepdims=True)
 
 
-def place(scalars, message, index, block_index, rank, copies):
+def place(scalars, message, index, block_index, rank, copies, unroll):
     vmem = pl.BlockSpec(memory_space=pltpu.VMEM)
     share, width = index.shape[0], block_index.shape[0]
     return pl.pallas_call(
-        place_kernel,
+        functools.partial(place_kernel, unroll=unroll),
         out_shape=(
             jax.ShapeDtypeStruct((copies, share, 128), jnp.bfloat16),
             jax.ShapeDtypeStruct((FEW, width), jnp.float32),
@@ -339,8 +341,9 @@
 def tile_kernel(points_ref, column_ref, ids_ref, chosen_ref, row_ref, panel_ref, out_ref):
     scale = -2.0 / points_ref.shape[1] * LOG2E
     step = 512
-    for start in range(0, chosen_ref.shape[0], step):
-        piece = pl.ds(start, step)
+
+    def part(number, _):
+        piece = pl.ds(pl.multiple_of(number * step, step), step)
         inner = lax.dot_general(
             points_ref[...], chosen_ref[piece, :], TRANSPOSED, preferred_element_type=jnp.float32
         )
@@ -348,6 +351,9 @@
         values = jnp.exp2(distance * scale)
         values = jnp.where(ids_ref[...] == panel_ref[:, piece], values + RIDGE, values)
         out_ref[:, piece] = values.astype(jnp.bfloat16)
+        return 0
+
+    lax.fori_loop(0, chosen_ref.shape[0] // step, part, 0, unroll=4)
 
 
 def build_tile(points, ids, chosen, panel):
@@ -476,18 +482,18 @@
             message = lax.all_to_all(message, axis, dim, dim, tiled=True)
         return message
 
-    def route(number, exchange):
+    def route(number, exchange, unroll):
         scalars = jnp.stack([number, start, x, core]).astype(jnp.int32)
-        message = pack(scalars, tables, points, other_points, gradient, other_grads).reshape(rows * xs, SLOTS, 128)
+        message = pack(scalars, tables, points, other_points, gradient, other_grads, unroll).reshape(rows * xs, SLOTS, 128)
         message = exchange(message).reshape(rows * xs * SLOTS, 128)
-        return place(scalars, message, own_share, block_index, rank, near)
+        return place(scalars, message, own_share, block_index, rank, near, 8 if unroll else 1)
 
     def further(state):
         number, piece, right = state
-        more_piece, more_right = route(number, exchange_by_axis)
+        more_piece, more_right = route(number, exchange_by_axis, False)
         return number + 1, piece + more_piece, right + more_right
 
-    piece, right_side = route(jnp.int32(0), exchange)
+    piece, right_side = route(jnp.int32(0), exchange, True)
     last = rounds[0, 0]
     _, piece, right_side = lax.while_loop(
         lambda state: state[0] < last, further, (jnp.int32(1), piece, right_side)

time: 131 us -> 129 us (0.985)
  Pallas kernels: 47.8 us -> 45.7 us
    pallas_call x2, Pallas kernels: 11.2 us -> 7.66 us  [the longest x1 4.83 us: pack(): pl.pallas_call(functools.partial(pack_kernel, unroll=unroll), out_shape=j...]
    pallas_call x1, Pallas kernels: 14.7 us -> 16.1 us  [build_tile(): pl.pallas_call(tile_kernel, grid=(count // block,), out_shape=jax.ShapeDt...]
  transfers between devices with their start and end apart: 21 -> 21, of which waited for: 6 -> 5; matrix products, arithmetic and copies ran while one was open for 6% -> 6% of each run, Pallas kernels for 36% -> 35%
where the time goes in v4:
time: 129 us; the launch traced here: 128 us
  starting transfers between devices  57 us (44%)
  Pallas kernels  45.7 us (35%)
  waiting for transfers between devices  15.4 us (12%)
  local copies, waits for them, and re-layouts  4.58 us (4%)
  other arithmetic  3.01 us (2%)
  between operations  2.24 us (2%)
    ppermute x17, starting transfers between devices, shift(): lax.ppermute(value, axis, [(i, (i + by) % size) for i in range(size)])  20.2 us
    pallas_call x1, Pallas kernels, build_tile(): pl.pallas_call(tile_kernel, grid=(count // block,), out_shape=jax.ShapeDt...  16.1 us
    all_to_all x1, starting transfers between devices, exchange(): return lax.all_to_all(message, ROUTE, 0, 0)  15 us
    pallas_call x3, Pallas kernels, product(): pl.pallas_call(product_kernel, grid=(count // line,), out_shape=jax.Shape...  11.4 us
    all_to_all x1, starting transfers between devices, on_device(): rest = lax.all_to_all(rest, ROWS, 0, 0).reshape(blocks, targets, width)  9.79 us
    all_to_all x1, waiting for transfers between devices, exchange(): return lax.all_to_all(message, ROUTE, 0, 0)  8.2 us
    ppermute x17, waiting for transfers between devices, shift(): lax.ppermute(value, axis, [(i, (i + by) % size) for i in range(size)])  7.2 us
    all_to_all x1, starting transfers between devices, on_device(): half = lax.all_to_all(half, ROWS, 0, 0).reshape(blocks, targets, width)  7.06 us
  transfers between devices with their start and end apart: 21, of which 5 were waited for; matrix products, arithmetic and copies ran while one was open for 6% of the time, Pallas kernels for 35%

profile of v4, /device:TPU:8, one launch (start us, length us, event | category | flops | bytes accessed | tf_op | source)
XLA Modules:
  0.0 128.0 jit_solution(1833041713241546323)
XLA Ops:
  0.6 0.0 copy-start.2
  0.6 0.0 copy-start.1
  0.7 0.1 collective-permute-start.4
  0.8 0.5 collective-permute-start.3
  1.3 1.5 %collective-permute-start = (s32[2,1024]{1,0:T(2,128)}, s32[2,1024]{1,0:T(2,128)S(1)}, u32[]{:S(2)}, u32[]{:S(2)}) collective-permute-start(s32[2,1024]{1,0:T(2,128)} %here_ref.3), channel_id=1, source_target_pairs={{0,2},{2,4},{4,6},{6,0},{1,3},{3,5},{5,7},{7,1},{8,10},{10,12},{12... | collective-permute-start | bytes 24584 | tf_op jit(solution)/shard_map/ppermute | solution.py:442
  2.7 2.7 %collective-permute-start.1 = (s32[2,1024]{1,0:T(2,128)}, s32[2,1024]{1,0:T(2,128)S(1)}, u32[]{:S(2)}, u32[]{:S(2)}) collective-permute-start(s32[2,1024]{1,0:T(2,128)} %here_ref.3), channel_id=1, source_target_pairs={{0,4},{2,6},{4,0},{6,2},{1,5},{3,7},{5,1},{7,3},{8,12},{10,14},{12... | collective-permute-start | bytes 24584 | tf_op jit(solution)/shard_map/ppermute | solution.py:442
  5.5 1.4 %collective-permute-start.2 = (s32[2,1024]{1,0:T(2,128)}, s32[2,1024]{1,0:T(2,128)S(1)}, u32[]{:S(2)}, u32[]{:S(2)}) collective-permute-start(s32[2,1024]{1,0:T(2,128)} %here_ref.3), channel_id=1, source_target_pairs={{0,6},{2,0},{4,2},{6,4},{1,7},{3,1},{5,3},{7,5},{8,14},{10,8},{12,... | collective-permute-start | bytes 24584 | tf_op jit(solution)/shard_map/ppermute | solution.py:442
  6.9 0.1 pad_add_fusion.2.scalar_ref
  7.0 0.7 reshape.60
  7.7 0.7 copy.33
  8.4 0.9 collective-permute-done.2.three_ref
  9.3 4.8 %pack.2 = bf16[2048,128]{1,0:T(8,128)(2,1)} custom-call(s32[4]{0:T(128)S(1)} %pad_add_fusion.2.scalar_ref, s32[2,1024]{1,0:T(2,128)} %here_ref.3, s32[2,1024]{1,0:T(2,128)S(1)} %collective-permute-done.one_ref, s32[2,1024]{1,0:T(2,128)S(1)} %collective-permute-done.1.two_ref, s32[2,1024]{1,0:T(2,128)S(1)} %collective-permute-done.2.three_ref, ...), custom_call_target="tpu_custom_call" | custom-call | tf_op jit(solution)/shard_map/pack/pallas_call | solution.py:144
  14.2 15.0 %all-to-all-start.4 = ((bf16[128,16,128]{2,1,0:T(8,128)(2,1)}), bf16[128,16,128]{2,1,0:T(8,128)(2,1)S(1)}, u32[]{:S(2)}, u32[]{:S(2)}) async-start(bf16[128,16,128]{2,1,0:T(8,128)(2,1)} %bitcast.12), calls=%async_computation.4 | async-start | bytes 1048576 | tf_op jit(solution)/shard_map/all_to_all | solution.py:477
  29.2 0.2 copy.25.block_column_ref
  29.4 0.1 copy.26.column_ref
  29.6 0.0 copy-start
  29.6 1.6 %collective-permute-start.6 = (bf16[512,128]{1,0:T(8,128)(2,1)}, bf16[512,128]{1,0:T(8,128)(2,1)S(1)}, u32[]{:S(2)}, u32[]{:S(2)}) collective-permute-start(bf16[512,128]{1,0:T(8,128)(2,1)} %points_ref.1), channel_id=1, source_target_pairs={{0,2},{2,4},{4,6},{6,0},{1,3},{3,5},{5,7},{7,1},{8,10},{10,12},{12... | collective-permute-start | bytes 393224 | tf_op jit(solution)/shard_map/ppermute | solution.py:442
  31.3 1.7 %collective-permute-start.8 = (bf16[512,128]{1,0:T(8,128)(2,1)}, bf16[512,128]{1,0:T(8,128)(2,1)S(1)}, u32[]{:S(2)}, u32[]{:S(2)}) collective-permute-start(bf16[512,128]{1,0:T(8,128)(2,1)} %points_ref.1), channel_id=1, source_target_pairs={{0,6},{2,0},{4,2},{6,4},{1,7},{3,1},{5,3},{7,5},{8,14},{10,8},{12,... | collective-permute-start | bytes 393224 | tf_op jit(solution)/shard_map/ppermute | solution.py:442
  33.0 2.7 %ranks.1 = (s32[1,1]{1,0:T(1,128)}, s32[1,1024]{1,0:T(1,128)S(1)}) custom-call(s32[2,1024]{1,0:T(2,128)S(1)} %copy-done.1, s32[2,1024]{1,0:T(2,128)S(1)} %collective-permute-done.one_ref, s32[2,1024]{1,0:T(2,128)S(1)} %collective-permute-done.1.two_ref, s32[2,1024]{1,0:T(2,128)S(1)} %collective-permute-done.2.three_ref, ...), custom_call_target="tpu_custom_call" | custom-call | flops 4000000000 | bytes 100000 | tf_op jit(solution)/shard_map/ranks/pallas_call | solution.py:199
  35.7 1.3 %collective-permute-done.5 = s32[1,1]{1,0:T(1,128)} collective-permute-done((s32[1,1]{1,0:T(1,128)}, s32[1,1]{1,0:T(1,128)}, u32[]{:S(2)}, u32[]{:S(2)}) %collective-permute-start.5) | collective-permute-done | bytes 36 | tf_op jit(solution)/shard_map/ppermute | solution.py:442
  38.3 8.2 %all-to-all-done.4 = bf16[128,16,128]{2,1,0:T(8,128)(2,1)S(1)} async-done(((bf16[128,16,128]{2,1,0:T(8,128)(2,1)}), bf16[128,16,128]{2,1,0:T(8,128)(2,1)S(1)}, u32[]{:S(2)}, u32[]{:S(2)}) %all-to-all-start.4) | async-done | bytes 524320 | tf_op jit(solution)/shard_map/all_to_all | solution.py:477
  46.5 2.8 %place.2 = (bf16[8,256,128]{2,1,0:T(8,128)(2,1)}, f32[8,1024]{1,0:T(8,128)S(1)}) custom-call(s32[4]{0:T(128)S(1)} %pad_add_fusion.2.scalar_ref, bf16[2048,128]{1,0:T(8,128)(2,1)S(1)} %bitcast.64, s32[1,256]{1,0:T(1,128)S(1)} %constant_dynamic-slice_fusion.1.row_ref, s32[256,1]{1,0:T(8,128)S(1)} %copy.26.column_ref, ...), custom_call_target="tpu_custom_call" | custom-call | tf_op jit(solution)/shard_map/place/pallas_call | solution.py:258
  49.4 5.0 %all-to-all-start.5 = ((bf16[8,256,128]{2,1,0:T(8,128)(2,1)}), bf16[8,256,128]{2,1,0:T(8,128)(2,1)S(1)}, u32[]{:S(2)}, u32[]{:S(2)}) async-start(bf16[8,256,128]{2,1,0:T(8,128)(2,1)} %get-tuple-element.112), calls=%async_computation.5 | async-start | bytes 1048576 | tf_op jit(solution)/shard_map/all_to_all | solution.py:501
  54.4 0.1 add_bitcast_fusion
  54.5 1.3 %copy.30 = s32[1,2048]{0,1:T(8,128)} copy(s32[1,2048]{1,0:T(1,128)S(1)} %bitcast.80) | data formatting | bytes 16384
  55.8 0.8 collective-permute-start.7
  56.6 2.6 %collective-permute-start.9 = (bf16[256,128]{1,0:T(8,128)(2,1)S(1)}, bf16[256,128]{1,0:T(8,128)(2,1)S(1)}, u32[]{:S(2)}, u32[]{:S(2)}) collective-permute-start(bf16[256,128]{1,0:T(8,128)(2,1)S(1)} %slice.33), channel_id=1, source_target_pairs={{0,6},{2,0},{4,2},{6,4},{1,7},{3,1},{5,3},{7,5},{8,14},{10,8},{12,... | collective-permute-start | bytes 196616 | tf_op jit(solution)/shard_map/ppermute | solution.py:442
  59.2 2.1 %collective-permute-done.7 = bf16[256,128]{1,0:T(8,128)(2,1)S(1)} collective-permute-done((bf16[256,128]{1,0:T(8,128)(2,1)S(1)}, bf16[256,128]{1,0:T(8,128)(2,1)S(1)}, u32[]{:S(2)}, u32[]{:S(2)}) %collective-permute-start.7) | collective-permute-done | bytes 65568 | tf_op jit(solution)/shard_map/ppermute | solution.py:442
  61.5 0.9 constant_dynamic-update-slice_fusion.points_ref
  62.4 0.3 multiply_reduce_fusion.1
  62.7 0.4 copy.27.column_ref
  63.1 0.3 collective-permute-start.10
  63.5 6.6 %solve.1 = (bf16[32,8,1024]{2,1,0:T(8,128)(2,1)}, bf16[32,8,1024]{2,1,0:T(8,128)(2,1)}) custom-call(bf16[1024,128]{1,0:T(8,128)(2,1)S(1)} %dynamic-slice_bitcast_fusion.points_ref, f32[8,1024]{1,0:T(8,128)S(1)} %get-tuple-element.113.right_ref), custom_call_target="tpu_custom_call" | custom-call | flops 6000000000 | bytes 1000000 | tf_op jit(solution)/shard_map/solve/pallas_call | solution.py:329
  70.1 7.1 %all-to-all-start.6 = ((bf16[32,8,1024]{2,1,0:T(8,128)(2,1)}), bf16[32,8,1024]{2,1,0:T(8,128)(2,1)S(1)}, u32[]{:S(2)}, u32[]{:S(2)}) async-start(bf16[32,8,1024]{2,1,0:T(8,128)(2,1)} %get-tuple-element.114), calls=%async_computation.6 | async-start | bytes 1048576 | tf_op jit(solution)/shard_map/all_to_all | solution.py:505
  77.1 1.1 pad_maximum_fusion.chosen_ref
  78.2 0.6 multiply_reduce_fusion
  78.8 16.1 %tile.1.refs_0_.refs_1_.refs_2_.refs_3_ = bf16[2048,4096]{1,0:T(8,128)(2,1)} custom-call(bf16[2048,128]{1,0:T(8,128)(2,1)S(1)} %constant_dynamic-update-slice_fusion.points_ref, f32[2048,1]{1,0:T(8,128)S(1)} %copy.27.column_ref, s32[2048,1]{1,0:T(8,128)} %bitcast.72, bf16[4096,128]{1,0:T(8,128)(2,1)} %pad_maximum_fusion.chosen_ref, f32[1,4096]{1,0:T(1,128)S(1)} %bitcast.66, ...), custom_call_target="tpu_custom_call" | custom-call | flops 8589934592 | bytes 16777216 | tf_op jit(solution)/shard_map/tile/pallas_call | solution.py:365
  94.9 9.8 %all-to-all-start.7 = ((bf16[32,8,1024]{2,1,0:T(8,128)(2,1)}), bf16[32,8,1024]{2,1,0:T(8,128)(2,1)S(1)}, u32[]{:S(2)}, u32[]{:S(2)}) async-start(bf16[32,8,1024]{2,1,0:T(8,128)(2,1)} %get-tuple-element.119), calls=%async_computation.7 | async-start | bytes 1048576 | tf_op jit(solution)/shard_map/all_to_all | solution.py:518
  104.7 3.0 %product.5 = f32[512,128]{1,0:T(8,128)S(1)} custom-call(bf16[2048,4096]{1,0:T(8,128)(2,1)} %tile.1.refs_0_.refs_1_.refs_2_.refs_3_, bf16[2048,4096]{1,0:T(8,128)(2,1)} %tile.1.refs_0_.refs_1_.refs_2_.refs_3_, bf16[2048,4096]{1,0:T(8,128)(2,1)} %tile.1.refs_0_.refs_1_.refs_2_.refs_3_, bf16[2048,4096]{1,0:T(8,128)(2,1)} %tile.1.refs_0_.refs_1_.refs_2_.refs_3_, ...), custom_call_target="tpu_custom_call" | custom-call | flops 1073741824 | bytes 4194304 | tf_op jit(solution)/shard_map/product/pallas_call | solution.py:405
  107.7 0.1 collective-permute-start.13
  107.8 3.4 %collective-permute-start.15 = (f32[256,128]{1,0:T(8,128)S(1)}, f32[256,128]{1,0:T(8,128)S(1)}, u32[]{:S(2)}, u32[]{:S(2)}) collective-permute-start(f32[256,128]{1,0:T(8,128)S(1)} %get-tuple-element.161), channel_id=1, source_target_pairs={{0,6},{2,0},{4,2},{6,4},{1,7},{3,1},{5,3},{7,5},{8,14},{10,8},{12,... | collective-permute-start | bytes 393224 | tf_op jit(solution)/shard_map/ppermute | solution.py:442
  111.3 5.4 %product.4 = f32[1024,128]{1,0:T(8,128)S(1)} custom-call(bf16[2048,4096]{1,0:T(8,128)(2,1)} %tile.1.refs_0_.refs_1_.refs_2_.refs_3_, bf16[2048,4096]{1,0:T(8,128)(2,1)} %tile.1.refs_0_.refs_1_.refs_2_.refs_3_, bf16[2048,4096]{1,0:T(8,128)(2,1)} %tile.1.refs_0_.refs_1_.refs_2_.refs_3_, bf16[2048,4096]{1,0:T(8,128)(2,1)} %tile.1.refs_0_.refs_1_.refs_2_.refs_3_, ...), custom_call_target="tpu_custom_call" | custom-call | flops 2147483648 | bytes 8388608 | tf_op jit(solution)/shard_map/product/pallas_call | solution.py:405
  116.7 0.1 collective-permute-start.14
  116.9 3.3 %collective-permute-start.16 = (f32[512,128]{1,0:T(8,128)S(1)}, f32[512,128]{1,0:T(8,128)S(1)}, u32[]{:S(2)}, u32[]{:S(2)}) collective-permute-start(f32[512,128]{1,0:T(8,128)S(1)} %pad_maximum_fusion.2), channel_id=1, source_target_pairs={{0,6},{2,0},{4,2},{6,4},{1,7},{3,1},{5,3},{7,5},{8,14},{10,8},{12,... | collective-permute-start | bytes 786440 | tf_op jit(solution)/shard_map/ppermute | solution.py:442
  120.2 3.0 %product.3 = f32[512,128]{1,0:T(8,128)S(1)} custom-call(bf16[2048,4096]{1,0:T(8,128)(2,1)} %tile.1.refs_0_.refs_1_.refs_2_.refs_3_, bf16[2048,4096]{1,0:T(8,128)(2,1)} %tile.1.refs_0_.refs_1_.refs_2_.refs_3_, bf16[2048,4096]{1,0:T(8,128)(2,1)} %tile.1.refs_0_.refs_1_.refs_2_.refs_3_, bf16[2048,4096]{1,0:T(8,128)(2,1)} %tile.1.refs_0_.refs_1_.refs_2_.refs_3_, ...), custom_call_target="tpu_custom_call" | custom-call | flops 1073741824 | bytes 4194304 | tf_op jit(solution)/shard_map/product/pallas_call | solution.py:405
  123.1 2.7 %collective-permute-done.14 = f32[512,128]{1,0:T(8,128)S(1)} collective-permute-done((f32[512,128]{1,0:T(8,128)S(1)}, f32[512,128]{1,0:T(8,128)S(1)}, u32[]{:S(2)}, u32[]{:S(2)}) %collective-permute-start.14) | collective-permute-done | bytes 262176 | tf_op jit(solution)/shard_map/ppermute | solution.py:442
  125.9 0.8 add_add_fusion
  126.7 1.3 %finish.1 = f32[2048,128]{1,0:T(8,128)} custom-call(bf16[2,128,1024]{2,1,0:T(8,128)(2,1)S(1)} %bitcast.63, bf16[2,128,1024]{2,1,0:T(8,128)(2,1)S(1)} %bitcast.65), custom_call_target="tpu_custom_call" | custom-call | flops 1000000 | bytes 2000000 | tf_op jit(solution)/shard_map/finish/pallas_call | solution.py:429
  (41 shorter events, 0.3 us)
Async XLA Ops:
  0.6 29.0 %copy-start.2 = (s32[4]{0:T(128)S(1)}, s32[4]{0:T(128)}, u32[]{:S(2)}) copy-start(s32[4]{0:T(128)} %constant.91.clone) | copy-start | bytes 52
  0.6 28.5 %copy-start.1 = (s32[2,1024]{1,0:T(2,128)S(1)}, s32[2,1024]{1,0:T(2,128)}, u32[]{:S(2)}) copy-start(s32[2,1024]{1,0:T(2,128)} %here_ref.3) | copy-start | bytes 24580
  0.7 8.7 %collective-permute-start.4 = (f32[512,128]{1,0:T(8,128)}, f32[512,128]{1,0:T(8,128)S(1)}, u32[]{:S(2)}, u32[]{:S(2)}) collective-permute-start(f32[512,128]{1,0:T(8,128)} %grads_ref.1), channel_id=1, source_target_pairs={{0,1},{1,0},{2,3},{3,2},{4,5},{5,4},{6,7},{7,6},{8,9},{9,8},{10,11... | collective-permute-start | bytes 786440 | tf_op jit(solution)/shard_map/ppermute | solution.py:442
  0.8 8.6 %collective-permute-start.3 = (bf16[512,128]{1,0:T(8,128)(2,1)}, bf16[512,128]{1,0:T(8,128)(2,1)S(1)}, u32[]{:S(2)}, u32[]{:S(2)}) collective-permute-start(bf16[512,128]{1,0:T(8,128)(2,1)} %points_ref.1), channel_id=1, source_target_pairs={{0,1},{1,0},{2,3},{3,2},{4,5},{5,4},{6,7},{7,6},{8,9},{9,8},{10,11... | collective-permute-start | bytes 393224 | tf_op jit(solution)/shard_map/ppermute | solution.py:442
  1.3 7.1 %collective-permute-start = (s32[2,1024]{1,0:T(2,128)}, s32[2,1024]{1,0:T(2,128)S(1)}, u32[]{:S(2)}, u32[]{:S(2)}) collective-permute-start(s32[2,1024]{1,0:T(2,128)} %here_ref.3), channel_id=1, source_target_pairs={{0,2},{2,4},{4,6},{6,0},{1,3},{3,5},{5,7},{7,1},{8,10},{10,12},{12... | collective-permute-start | bytes 24584 | tf_op jit(solution)/shard_map/ppermute | solution.py:442
  2.7 5.7 %collective-permute-start.1 = (s32[2,1024]{1,0:T(2,128)}, s32[2,1024]{1,0:T(2,128)S(1)}, u32[]{:S(2)}, u32[]{:S(2)}) collective-permute-start(s32[2,1024]{1,0:T(2,128)} %here_ref.3), channel_id=1, source_target_pairs={{0,4},{2,6},{4,0},{6,2},{1,5},{3,7},{5,1},{7,3},{8,12},{10,14},{12... | collective-permute-start | bytes 24584 | tf_op jit(solution)/shard_map/ppermute | solution.py:442
  5.5 3.9 %collective-permute-start.2 = (s32[2,1024]{1,0:T(2,128)}, s32[2,1024]{1,0:T(2,128)S(1)}, u32[]{:S(2)}, u32[]{:S(2)}) collective-permute-start(s32[2,1024]{1,0:T(2,128)} %here_ref.3), channel_id=1, source_target_pairs={{0,6},{2,0},{4,2},{6,4},{1,7},{3,1},{5,3},{7,5},{8,14},{10,8},{12,... | collective-permute-start | bytes 24584 | tf_op jit(solution)/shard_map/ppermute | solution.py:442
  8.4 48.2 %collective-permute-start.11 = (s32[2048]{0:T(1024)S(1)}, s32[2048]{0:T(1024)S(1)}, u32[]{:S(2)}, u32[]{:S(2)}) collective-permute-start(s32[2048]{0:T(1024)S(1)} %bitcast.81), channel_id=1, source_target_pairs={{0,1},{1,0},{2,3},{3,2},{4,5},{5,4},{6,7},{7,6},{8,9},{9,8},{10,11... | collective-permute-start | bytes 24584 | tf_op jit(solution)/shard_map/ppermute | solution.py:442
  14.2 32.4 %all-to-all-start.4 = ((bf16[128,16,128]{2,1,0:T(8,128)(2,1)}), bf16[128,16,128]{2,1,0:T(8,128)(2,1)S(1)}, u32[]{:S(2)}, u32[]{:S(2)}) async-start(bf16[128,16,128]{2,1,0:T(8,128)(2,1)} %bitcast.12), calls=%async_computation.4 | async-start | bytes 1048576 | tf_op jit(solution)/shard_map/all_to_all | solution.py:477
  29.6 19.8 %copy-start = (f32[512,128]{1,0:T(8,128)S(1)}, f32[512,128]{1,0:T(8,128)}, u32[]{:S(2)}) copy-start(f32[512,128]{1,0:T(8,128)} %grads_ref.1) | copy-start | bytes 786436
  29.6 26.2 %collective-permute-start.6 = (bf16[512,128]{1,0:T(8,128)(2,1)}, bf16[512,128]{1,0:T(8,128)(2,1)S(1)}, u32[]{:S(2)}, u32[]{:S(2)}) collective-permute-start(bf16[512,128]{1,0:T(8,128)(2,1)} %points_ref.1), channel_id=1, source_target_pairs={{0,2},{2,4},{4,6},{6,0},{1,3},{3,5},{5,7},{7,1},{8,10},{10,12},{12... | collective-permute-start | bytes 393224 | tf_op jit(solution)/shard_map/ppermute | solution.py:442
  31.3 25.3 %collective-permute-start.8 = (bf16[512,128]{1,0:T(8,128)(2,1)}, bf16[512,128]{1,0:T(8,128)(2,1)S(1)}, u32[]{:S(2)}, u32[]{:S(2)}) collective-permute-start(bf16[512,128]{1,0:T(8,128)(2,1)} %points_ref.1), channel_id=1, source_target_pairs={{0,6},{2,0},{4,2},{6,4},{1,7},{3,1},{5,3},{7,5},{8,14},{10,8},{12,... | collective-permute-start | bytes 393224 | tf_op jit(solution)/shard_map/ppermute | solution.py:442
  35.7 1.4 %collective-permute-start.5 = (s32[1,1]{1,0:T(1,128)}, s32[1,1]{1,0:T(1,128)}, u32[]{:S(2)}, u32[]{:S(2)}) collective-permute-start(s32[1,1]{1,0:T(1,128)} %get-tuple-element.111), channel_id=1, source_target_pairs={{0,1},{1,0},{2,3},{3,2},{4,5},{5,4},{6,7},{7,6},{8,9},{9,8},{10,11... | collective-permute-start | bytes 20 | tf_op jit(solution)/shard_map/ppermute | solution.py:442
  49.4 13.7 %all-to-all-start.5 = ((bf16[8,256,128]{2,1,0:T(8,128)(2,1)}), bf16[8,256,128]{2,1,0:T(8,128)(2,1)S(1)}, u32[]{:S(2)}, u32[]{:S(2)}) async-start(bf16[8,256,128]{2,1,0:T(8,128)(2,1)} %get-tuple-element.112), calls=%async_computation.5 | async-start | bytes 1048576 | tf_op jit(solution)/shard_map/all_to_all | solution.py:501
  55.8 5.6 %collective-permute-start.7 = (bf16[256,128]{1,0:T(8,128)(2,1)S(1)}, bf16[256,128]{1,0:T(8,128)(2,1)S(1)}, u32[]{:S(2)}, u32[]{:S(2)}) collective-permute-start(bf16[256,128]{1,0:T(8,128)(2,1)S(1)} %slice.32), channel_id=1, source_target_pairs={{0,2},{2,4},{4,6},{6,0},{1,3},{3,5},{5,7},{7,1},{8,10},{10,12},{12... | collective-permute-start | bytes 196616 | tf_op jit(solution)/shard_map/ppermute | solution.py:442
  56.6 4.8 %collective-permute-start.9 = (bf16[256,128]{1,0:T(8,128)(2,1)S(1)}, bf16[256,128]{1,0:T(8,128)(2,1)S(1)}, u32[]{:S(2)}, u32[]{:S(2)}) collective-permute-start(bf16[256,128]{1,0:T(8,128)(2,1)S(1)} %slice.33), channel_id=1, source_target_pairs={{0,6},{2,0},{4,2},{6,4},{1,7},{3,1},{5,3},{7,5},{8,14},{10,8},{12,... | collective-permute-start | bytes 196616 | tf_op jit(solution)/shard_map/ppermute | solution.py:442
  63.1 14.0 %collective-permute-start.10 = (bf16[2048,128]{1,0:T(8,128)(2,1)S(1)}, bf16[2048,128]{1,0:T(8,128)(2,1)S(1)}, u32[]{:S(2)}, u32[]{:S(2)}) collective-permute-start(bf16[2048,128]{1,0:T(8,128)(2,1)S(1)} %bitcast.68), channel_id=1, source_target_pairs={{0,1},{1,0},{2,3},{3,2},{4,5},{5,4},{6,7},{7,6},{8,9},{9,8},{10,11... | collective-permute-start | bytes 1572872 | tf_op jit(solution)/shard_map/ppermute | solution.py:442
  70.1 24.8 %all-to-all-start.6 = ((bf16[32,8,1024]{2,1,0:T(8,128)(2,1)}), bf16[32,8,1024]{2,1,0:T(8,128)(2,1)S(1)}, u32[]{:S(2)}, u32[]{:S(2)}) async-start(bf16[32,8,1024]{2,1,0:T(8,128)(2,1)} %get-tuple-element.114), calls=%async_computation.6 | async-start | bytes 1048576 | tf_op jit(solution)/shard_map/all_to_all | solution.py:505
  94.9 9.8 %collective-permute-start.12 = (bf16[2,128,1024]{2,1,0:T(8,128)(2,1)S(1)}, bf16[2,128,1024]{2,1,0:T(8,128)(2,1)S(1)}, u32[]{:S(2)}, u32[]{:S(2)}) collective-permute-start(bf16[2,128,1024]{2,1,0:T(8,128)(2,1)S(1)} %bitcast.59), channel_id=1, source_target_pairs={{0,1},{1,0},{2,3},{3,2},{4,5},{5,4},{6,7},{7,6},{8,9},{9,8},{10,11... | collective-permute-start | bytes 1572872 | tf_op jit(solution)/shard_map/ppermute | solution.py:442
  94.9 31.8 %all-to-all-start.7 = ((bf16[32,8,1024]{2,1,0:T(8,128)(2,1)}), bf16[32,8,1024]{2,1,0:T(8,128)(2,1)S(1)}, u32[]{:S(2)}, u32[]{:S(2)}) async-start(bf16[32,8,1024]{2,1,0:T(8,128)(2,1)} %get-tuple-element.119), calls=%async_computation.7 | async-start | bytes 1048576 | tf_op jit(solution)/shard_map/all_to_all | solution.py:518
  107.7 8.9 %collective-permute-start.13 = (f32[256,128]{1,0:T(8,128)S(1)}, f32[256,128]{1,0:T(8,128)S(1)}, u32[]{:S(2)}, u32[]{:S(2)}) collective-permute-start(f32[256,128]{1,0:T(8,128)S(1)} %get-tuple-element.160), channel_id=1, source_target_pairs={{0,2},{2,4},{4,6},{6,0},{1,3},{3,5},{5,7},{7,1},{8,10},{10,12},{12... | collective-permute-start | bytes 393224 | tf_op jit(solution)/shard_map/ppermute | solution.py:442
  107.8 8.8 %collective-permute-start.15 = (f32[256,128]{1,0:T(8,128)S(1)}, f32[256,128]{1,0:T(8,128)S(1)}, u32[]{:S(2)}, u32[]{:S(2)}) collective-permute-start(f32[256,128]{1,0:T(8,128)S(1)} %get-tuple-element.161), channel_id=1, source_target_pairs={{0,6},{2,0},{4,2},{6,4},{1,7},{3,1},{5,3},{7,5},{8,14},{10,8},{12,... | collective-permute-start | bytes 393224 | tf_op jit(solution)/shard_map/ppermute | solution.py:442
  116.7 9.2 %collective-permute-start.14 = (f32[512,128]{1,0:T(8,128)S(1)}, f32[512,128]{1,0:T(8,128)S(1)}, u32[]{:S(2)}, u32[]{:S(2)}) collective-permute-start(f32[512,128]{1,0:T(8,128)S(1)} %pad_maximum_fusion.1), channel_id=1, source_target_pairs={{0,2},{2,4},{4,6},{6,0},{1,3},{3,5},{5,7},{7,1},{8,10},{10,12},{12... | collective-permute-start | bytes 786440 | tf_op jit(solution)/shard_map/ppermute | solution.py:442
  116.9 9.0 %collective-permute-start.16 = (f32[512,128]{1,0:T(8,128)S(1)}, f32[512,128]{1,0:T(8,128)S(1)}, u32[]{:S(2)}, u32[]{:S(2)}) collective-permute-start(f32[512,128]{1,0:T(8,128)S(1)} %pad_maximum_fusion.2), channel_id=1, source_target_pairs={{0,6},{2,0},{4,2},{6,4},{1,7},{3,1},{5,3},{7,5},{8,14},{10,8},{12,... | collective-permute-start | bytes 786440 | tf_op jit(solution)/shard_map/ppermute | solution.py:442

commit v5 on v4

--- a/solution.py
+++ b/solution.py
@@ -528,8 +528,9 @@
     send_before = jnp.concatenate([near[own : own + middle], near[own + middle :] + bottom])
     from_before = shift(send_after, "x", 1)
     from_after = shift(send_before, "x", -1)
-    new_gradient = gradient + (mine + from_before + from_after)
-    return new_gradient, finish(half, rest)
+    update = finish(half, rest)
+    from_before, from_after, update = lax.optimization_barrier((from_before, from_after, update))
+    return gradient + (mine + from_before + from_after), update
 
 
 def solution(mesh):

time: 129 us -> 129 us (level)
  waiting for transfers between devices: 15.4 us -> 16.8 us
  transfers between devices with their start and end apart: 21 -> 21, of which waited for: 5 -> 7; matrix products, arithmetic and copies ran while one was open for 6% -> 5% of each run, Pallas kernels for 35% -> 36%
where the time goes in v5:
time: 129 us; the launch traced here: 128 us
  starting transfers between devices  55.8 us (43%)
  Pallas kernels  45.7 us (35%)
  waiting for transfers between devices  16.8 us (13%)
  local copies, waits for them, and re-layouts  4.58 us (4%)
  other arithmetic  3.01 us (2%)
  between operations  2.23 us (2%)
    ppermute x17, starting transfers between devices, shift(): lax.ppermute(value, axis, [(i, (i + by) % size) for i in range(size)])  19 us
    pallas_call x1, Pallas kernels, build_tile(): pl.pallas_call(tile_kernel, grid=(count // block,), out_shape=jax.ShapeDt...  16.1 us
    all_to_all x1, starting transfers between devices, exchange(): return lax.all_to_all(message, ROUTE, 0, 0)  15 us
    pallas_call x3, Pallas kernels, product(): pl.pallas_call(product_kernel, grid=(count // line,), out_shape=jax.Shape...  11.4 us
    all_to_all x1, starting transfers between devices, on_device(): rest = lax.all_to_all(rest, ROWS, 0, 0).reshape(blocks, targets, width)  9.79 us
    ppermute x17, waiting for transfers between devices, shift(): lax.ppermute(value, axis, [(i, (i + by) % size) for i in range(size)])  8.31 us
    all_to_all x1, waiting for transfers between devices, exchange(): return lax.all_to_all(message, ROUTE, 0, 0)  8.2 us
    all_to_all x1, starting transfers between devices, on_device(): half = lax.all_to_all(half, ROWS, 0, 0).reshape(blocks, targets, width)  7.06 us
  transfers between devices with their start and end apart: 21, of which 7 were waited for; matrix products, arithmetic and copies ran while one was open for 5% of the time, Pallas kernels for 36%

profile of v5, /device:TPU:8, one launch (start us, length us, event | category | flops | bytes accessed | tf_op | source)
XLA Modules:
  0.0 128.1 jit_solution(14442524469305359579)
XLA Ops:
  0.6 0.0 copy-start.2
  0.7 0.1 collective-permute-start.4
  0.8 0.5 collective-permute-start.3
  1.3 1.5 %collective-permute-start = (s32[2,1024]{1,0:T(2,128)}, s32[2,1024]{1,0:T(2,128)S(1)}, u32[]{:S(2)}, u32[]{:S(2)}) collective-permute-start(s32[2,1024]{1,0:T(2,128)} %here_ref.3), channel_id=1, source_target_pairs={{0,2},{2,4},{4,6},{6,0},{1,3},{3,5},{5,7},{7,1},{8,10},{10,12},{12... | collective-permute-start | bytes 24584 | tf_op jit(solution)/shard_map/ppermute | solution.py:442
  2.7 2.7 %collective-permute-start.1 = (s32[2,1024]{1,0:T(2,128)}, s32[2,1024]{1,0:T(2,128)S(1)}, u32[]{:S(2)}, u32[]{:S(2)}) collective-permute-start(s32[2,1024]{1,0:T(2,128)} %here_ref.3), channel_id=1, source_target_pairs={{0,4},{2,6},{4,0},{6,2},{1,5},{3,7},{5,1},{7,3},{8,12},{10,14},{12... | collective-permute-start | bytes 24584 | tf_op jit(solution)/shard_map/ppermute | solution.py:442
  5.5 1.4 %collective-permute-start.2 = (s32[2,1024]{1,0:T(2,128)}, s32[2,1024]{1,0:T(2,128)S(1)}, u32[]{:S(2)}, u32[]{:S(2)}) collective-permute-start(s32[2,1024]{1,0:T(2,128)} %here_ref.3), channel_id=1, source_target_pairs={{0,6},{2,0},{4,2},{6,4},{1,7},{3,1},{5,3},{7,5},{8,14},{10,8},{12,... | collective-permute-start | bytes 24584 | tf_op jit(solution)/shard_map/ppermute | solution.py:442
  6.9 0.1 pad_add_fusion.2.scalar_ref
  7.0 0.7 reshape.60
  7.7 0.7 copy.33
  8.4 0.9 collective-permute-done.2.three_ref
  9.3 4.8 %pack.2 = bf16[2048,128]{1,0:T(8,128)(2,1)} custom-call(s32[4]{0:T(128)S(1)} %pad_add_fusion.2.scalar_ref, s32[2,1024]{1,0:T(2,128)} %here_ref.3, s32[2,1024]{1,0:T(2,128)S(1)} %collective-permute-done.one_ref, s32[2,1024]{1,0:T(2,128)S(1)} %collective-permute-done.1.two_ref, s32[2,1024]{1,0:T(2,128)S(1)} %collective-permute-done.2.three_ref, ...), custom_call_target="tpu_custom_call" | custom-call | tf_op jit(solution)/shard_map/pack/pallas_call | solution.py:144
  14.2 15.0 %all-to-all-start.4 = ((bf16[128,16,128]{2,1,0:T(8,128)(2,1)}), bf16[128,16,128]{2,1,0:T(8,128)(2,1)S(1)}, u32[]{:S(2)}, u32[]{:S(2)}) async-start(bf16[128,16,128]{2,1,0:T(8,128)(2,1)} %bitcast.12), calls=%async_computation.4 | async-start | bytes 1048576 | tf_op jit(solution)/shard_map/all_to_all | solution.py:477
  29.2 0.2 copy.25.block_column_ref
  29.4 0.1 copy.26.column_ref
  29.6 1.6 %collective-permute-start.6 = (bf16[512,128]{1,0:T(8,128)(2,1)}, bf16[512,128]{1,0:T(8,128)(2,1)S(1)}, u32[]{:S(2)}, u32[]{:S(2)}) collective-permute-start(bf16[512,128]{1,0:T(8,128)(2,1)} %points_ref.1), channel_id=1, source_target_pairs={{0,2},{2,4},{4,6},{6,0},{1,3},{3,5},{5,7},{7,1},{8,10},{10,12},{12... | collective-permute-start | bytes 393224 | tf_op jit(solution)/shard_map/ppermute | solution.py:442
  31.3 1.7 %collective-permute-start.8 = (bf16[512,128]{1,0:T(8,128)(2,1)}, bf16[512,128]{1,0:T(8,128)(2,1)S(1)}, u32[]{:S(2)}, u32[]{:S(2)}) collective-permute-start(bf16[512,128]{1,0:T(8,128)(2,1)} %points_ref.1), channel_id=1, source_target_pairs={{0,6},{2,0},{4,2},{6,4},{1,7},{3,1},{5,3},{7,5},{8,14},{10,8},{12,... | collective-permute-start | bytes 393224 | tf_op jit(solution)/shard_map/ppermute | solution.py:442
  33.0 2.7 %ranks.1 = (s32[1,1]{1,0:T(1,128)}, s32[1,1024]{1,0:T(1,128)S(1)}) custom-call(s32[2,1024]{1,0:T(2,128)S(1)} %copy-done.1, s32[2,1024]{1,0:T(2,128)S(1)} %collective-permute-done.one_ref, s32[2,1024]{1,0:T(2,128)S(1)} %collective-permute-done.1.two_ref, s32[2,1024]{1,0:T(2,128)S(1)} %collective-permute-done.2.three_ref, ...), custom_call_target="tpu_custom_call" | custom-call | flops 4000000000 | bytes 100000 | tf_op jit(solution)/shard_map/ranks/pallas_call | solution.py:199
  35.7 1.3 %collective-permute-done.5 = s32[1,1]{1,0:T(1,128)} collective-permute-done((s32[1,1]{1,0:T(1,128)}, s32[1,1]{1,0:T(1,128)}, u32[]{:S(2)}, u32[]{:S(2)}) %collective-permute-start.5) | collective-permute-done | bytes 36 | tf_op jit(solution)/shard_map/ppermute | solution.py:442
  38.3 8.2 %all-to-all-done.4 = bf16[128,16,128]{2,1,0:T(8,128)(2,1)S(1)} async-done(((bf16[128,16,128]{2,1,0:T(8,128)(2,1)}), bf16[128,16,128]{2,1,0:T(8,128)(2,1)S(1)}, u32[]{:S(2)}, u32[]{:S(2)}) %all-to-all-start.4) | async-done | bytes 524320 | tf_op jit(solution)/shard_map/all_to_all | solution.py:477
  46.5 2.8 %place.2 = (bf16[8,256,128]{2,1,0:T(8,128)(2,1)}, f32[8,1024]{1,0:T(8,128)S(1)}) custom-call(s32[4]{0:T(128)S(1)} %pad_add_fusion.2.scalar_ref, bf16[2048,128]{1,0:T(8,128)(2,1)S(1)} %bitcast.64, s32[1,256]{1,0:T(1,128)S(1)} %constant_dynamic-slice_fusion.1.row_ref, s32[256,1]{1,0:T(8,128)S(1)} %copy.26.column_ref, ...), custom_call_target="tpu_custom_call" | custom-call | tf_op jit(solution)/shard_map/place/pallas_call | solution.py:258
  49.4 5.0 %all-to-all-start.5 = ((bf16[8,256,128]{2,1,0:T(8,128)(2,1)}), bf16[8,256,128]{2,1,0:T(8,128)(2,1)S(1)}, u32[]{:S(2)}, u32[]{:S(2)}) async-start(bf16[8,256,128]{2,1,0:T(8,128)(2,1)} %get-tuple-element.115), calls=%async_computation.5 | async-start | bytes 1048576 | tf_op jit(solution)/shard_map/all_to_all | solution.py:501
  54.4 0.1 add_bitcast_fusion
  54.5 1.3 %copy.30 = s32[1,2048]{0,1:T(8,128)} copy(s32[1,2048]{1,0:T(1,128)S(1)} %bitcast.80) | data formatting | bytes 16384
  55.8 0.8 collective-permute-start.7
  56.6 2.6 %collective-permute-start.9 = (bf16[256,128]{1,0:T(8,128)(2,1)S(1)}, bf16[256,128]{1,0:T(8,128)(2,1)S(1)}, u32[]{:S(2)}, u32[]{:S(2)}) collective-permute-start(bf16[256,128]{1,0:T(8,128)(2,1)S(1)} %slice.33), channel_id=1, source_target_pairs={{0,6},{2,0},{4,2},{6,4},{1,7},{3,1},{5,3},{7,5},{8,14},{10,8},{12,... | collective-permute-start | bytes 196616 | tf_op jit(solution)/shard_map/ppermute | solution.py:442
  59.2 2.1 %collective-permute-done.7 = bf16[256,128]{1,0:T(8,128)(2,1)S(1)} collective-permute-done((bf16[256,128]{1,0:T(8,128)(2,1)S(1)}, bf16[256,128]{1,0:T(8,128)(2,1)S(1)}, u32[]{:S(2)}, u32[]{:S(2)}) %collective-permute-start.7) | collective-permute-done | bytes 65568 | tf_op jit(solution)/shard_map/ppermute | solution.py:442
  61.5 0.9 constant_dynamic-update-slice_fusion.points_ref
  62.4 0.3 multiply_reduce_fusion.1
  62.7 0.4 copy.27.column_ref
  63.1 0.3 collective-permute-start.10
  63.5 6.6 %solve.1 = (bf16[32,8,1024]{2,1,0:T(8,128)(2,1)}, bf16[32,8,1024]{2,1,0:T(8,128)(2,1)}) custom-call(bf16[1024,128]{1,0:T(8,128)(2,1)S(1)} %dynamic-slice_bitcast_fusion.points_ref, f32[8,1024]{1,0:T(8,128)S(1)} %get-tuple-element.116.right_ref), custom_call_target="tpu_custom_call" | custom-call | flops 6000000000 | bytes 1000000 | tf_op jit(solution)/shard_map/solve/pallas_call | solution.py:329
  70.1 7.1 %all-to-all-start.6 = ((bf16[32,8,1024]{2,1,0:T(8,128)(2,1)}), bf16[32,8,1024]{2,1,0:T(8,128)(2,1)S(1)}, u32[]{:S(2)}, u32[]{:S(2)}) async-start(bf16[32,8,1024]{2,1,0:T(8,128)(2,1)} %get-tuple-element.117), calls=%async_computation.6 | async-start | bytes 1048576 | tf_op jit(solution)/shard_map/all_to_all | solution.py:505
  77.1 1.1 pad_maximum_fusion.chosen_ref
  78.2 0.6 multiply_reduce_fusion
  78.8 16.1 %tile.1.refs_0_.refs_1_.refs_2_.refs_3_ = bf16[2048,4096]{1,0:T(8,128)(2,1)} custom-call(bf16[2048,128]{1,0:T(8,128)(2,1)S(1)} %constant_dynamic-update-slice_fusion.points_ref, f32[2048,1]{1,0:T(8,128)S(1)} %copy.27.column_ref, s32[2048,1]{1,0:T(8,128)} %bitcast.72, bf16[4096,128]{1,0:T(8,128)(2,1)} %pad_maximum_fusion.chosen_ref, f32[1,4096]{1,0:T(1,128)S(1)} %bitcast.66, ...), custom_call_target="tpu_custom_call" | custom-call | flops 8589934592 | bytes 16777216 | tf_op jit(solution)/shard_map/tile/pallas_call | solution.py:365
  94.9 9.8 %all-to-all-start.7 = ((bf16[32,8,1024]{2,1,0:T(8,128)(2,1)}), bf16[32,8,1024]{2,1,0:T(8,128)(2,1)S(1)}, u32[]{:S(2)}, u32[]{:S(2)}) async-start(bf16[32,8,1024]{2,1,0:T(8,128)(2,1)} %get-tuple-element.122), calls=%async_computation.7 | async-start | bytes 1048576 | tf_op jit(solution)/shard_map/all_to_all | solution.py:518
  104.7 3.0 %product.5 = f32[512,128]{1,0:T(8,128)S(1)} custom-call(bf16[2048,4096]{1,0:T(8,128)(2,1)} %tile.1.refs_0_.refs_1_.refs_2_.refs_3_, bf16[2048,4096]{1,0:T(8,128)(2,1)} %tile.1.refs_0_.refs_1_.refs_2_.refs_3_, bf16[2048,4096]{1,0:T(8,128)(2,1)} %tile.1.refs_0_.refs_1_.refs_2_.refs_3_, bf16[2048,4096]{1,0:T(8,128)(2,1)} %tile.1.refs_0_.refs_1_.refs_2_.refs_3_, ...), custom_call_target="tpu_custom_call" | custom-call | flops 1073741824 | bytes 4194304 | tf_op jit(solution)/shard_map/product/pallas_call | solution.py:405
  107.7 0.1 collective-permute-start.13
  107.8 3.4 %collective-permute-start.15 = (f32[256,128]{1,0:T(8,128)S(1)}, f32[256,128]{1,0:T(8,128)S(1)}, u32[]{:S(2)}, u32[]{:S(2)}) collective-permute-start(f32[256,128]{1,0:T(8,128)S(1)} %get-tuple-element.166), channel_id=1, source_target_pairs={{0,6},{2,0},{4,2},{6,4},{1,7},{3,1},{5,3},{7,5},{8,14},{10,8},{12,... | collective-permute-start | bytes 393224 | tf_op jit(solution)/shard_map/ppermute | solution.py:442
  111.3 5.4 %product.4 = f32[1024,128]{1,0:T(8,128)S(1)} custom-call(bf16[2048,4096]{1,0:T(8,128)(2,1)} %tile.1.refs_0_.refs_1_.refs_2_.refs_3_, bf16[2048,4096]{1,0:T(8,128)(2,1)} %tile.1.refs_0_.refs_1_.refs_2_.refs_3_, bf16[2048,4096]{1,0:T(8,128)(2,1)} %tile.1.refs_0_.refs_1_.refs_2_.refs_3_, bf16[2048,4096]{1,0:T(8,128)(2,1)} %tile.1.refs_0_.refs_1_.refs_2_.refs_3_, ...), custom_call_target="tpu_custom_call" | custom-call | flops 2147483648 | bytes 8388608 | tf_op jit(solution)/shard_map/product/pallas_call | solution.py:405
  116.7 2.0 %collective-permute-start.16 = (f32[512,128]{1,0:T(8,128)S(1)}, f32[512,128]{1,0:T(8,128)S(1)}, u32[]{:S(2)}, u32[]{:S(2)}) collective-permute-start(f32[512,128]{1,0:T(8,128)S(1)} %pad_maximum_fusion.2), channel_id=1, source_target_pairs={{0,6},{2,0},{4,2},{6,4},{1,7},{3,1},{5,3},{7,5},{8,14},{10,8},{12,... | collective-permute-start | bytes 786440 | tf_op jit(solution)/shard_map/ppermute | solution.py:442
  118.8 0.2 collective-permute-start.14
  118.9 3.0 %product.3 = f32[512,128]{1,0:T(8,128)S(1)} custom-call(bf16[2048,4096]{1,0:T(8,128)(2,1)} %tile.1.refs_0_.refs_1_.refs_2_.refs_3_, bf16[2048,4096]{1,0:T(8,128)(2,1)} %tile.1.refs_0_.refs_1_.refs_2_.refs_3_, bf16[2048,4096]{1,0:T(8,128)(2,1)} %tile.1.refs_0_.refs_1_.refs_2_.refs_3_, bf16[2048,4096]{1,0:T(8,128)(2,1)} %tile.1.refs_0_.refs_1_.refs_2_.refs_3_, ...), custom_call_target="tpu_custom_call" | custom-call | flops 1073741824 | bytes 4194304 | tf_op jit(solution)/shard_map/product/pallas_call | solution.py:405
  121.9 0.3 all-to-all-done.7
  122.2 1.3 %finish.1 = f32[2048,128]{1,0:T(8,128)} custom-call(bf16[2,128,1024]{2,1,0:T(8,128)(2,1)S(1)} %bitcast.63, bf16[2,128,1024]{2,1,0:T(8,128)(2,1)S(1)} %bitcast.65), custom_call_target="tpu_custom_call" | custom-call | flops 1000000 | bytes 2000000 | tf_op jit(solution)/shard_map/finish/pallas_call | solution.py:429
  123.5 1.2 collective-permute-done.16
  124.7 2.7 %collective-permute-done.14 = f32[512,128]{1,0:T(8,128)S(1)} collective-permute-done((f32[512,128]{1,0:T(8,128)S(1)}, f32[512,128]{1,0:T(8,128)S(1)}, u32[]{:S(2)}, u32[]{:S(2)}) %collective-permute-start.14) | collective-permute-done | bytes 262176 | tf_op jit(solution)/shard_map/ppermute | solution.py:442
  127.4 0.8 add_add_fusion
  (41 shorter events, 0.3 us)
Async XLA Ops:
  0.6 29.0 %copy-start.2 = (s32[4]{0:T(128)S(1)}, s32[4]{0:T(128)}, u32[]{:S(2)}) copy-start(s32[4]{0:T(128)} %constant.91.clone) | copy-start | bytes 52
  0.6 28.5 %copy-start.1 = (s32[2,1024]{1,0:T(2,128)S(1)}, s32[2,1024]{1,0:T(2,128)}, u32[]{:S(2)}) copy-start(s32[2,1024]{1,0:T(2,128)} %here_ref.3) | copy-start | bytes 24580
  0.7 8.7 %collective-permute-start.4 = (f32[512,128]{1,0:T(8,128)}, f32[512,128]{1,0:T(8,128)S(1)}, u32[]{:S(2)}, u32[]{:S(2)}) collective-permute-start(f32[512,128]{1,0:T(8,128)} %grads_ref.1), channel_id=1, source_target_pairs={{0,1},{1,0},{2,3},{3,2},{4,5},{5,4},{6,7},{7,6},{8,9},{9,8},{10,11... | collective-permute-start | bytes 786440 | tf_op jit(solution)/shard_map/ppermute | solution.py:442
  0.8 8.6 %collective-permute-start.3 = (bf16[512,128]{1,0:T(8,128)(2,1)}, bf16[512,128]{1,0:T(8,128)(2,1)S(1)}, u32[]{:S(2)}, u32[]{:S(2)}) collective-permute-start(bf16[512,128]{1,0:T(8,128)(2,1)} %points_ref.1), channel_id=1, source_target_pairs={{0,1},{1,0},{2,3},{3,2},{4,5},{5,4},{6,7},{7,6},{8,9},{9,8},{10,11... | collective-permute-start | bytes 393224 | tf_op jit(solution)/shard_map/ppermute | solution.py:442
  1.3 7.1 %collective-permute-start = (s32[2,1024]{1,0:T(2,128)}, s32[2,1024]{1,0:T(2,128)S(1)}, u32[]{:S(2)}, u32[]{:S(2)}) collective-permute-start(s32[2,1024]{1,0:T(2,128)} %here_ref.3), channel_id=1, source_target_pairs={{0,2},{2,4},{4,6},{6,0},{1,3},{3,5},{5,7},{7,1},{8,10},{10,12},{12... | collective-permute-start | bytes 24584 | tf_op jit(solution)/shard_map/ppermute | solution.py:442
  2.7 5.7 %collective-permute-start.1 = (s32[2,1024]{1,0:T(2,128)}, s32[2,1024]{1,0:T(2,128)S(1)}, u32[]{:S(2)}, u32[]{:S(2)}) collective-permute-start(s32[2,1024]{1,0:T(2,128)} %here_ref.3), channel_id=1, source_target_pairs={{0,4},{2,6},{4,0},{6,2},{1,5},{3,7},{5,1},{7,3},{8,12},{10,14},{12... | collective-permute-start | bytes 24584 | tf_op jit(solution)/shard_map/ppermute | solution.py:442
  5.5 3.9 %collective-permute-start.2 = (s32[2,1024]{1,0:T(2,128)}, s32[2,1024]{1,0:T(2,128)S(1)}, u32[]{:S(2)}, u32[]{:S(2)}) collective-permute-start(s32[2,1024]{1,0:T(2,128)} %here_ref.3), channel_id=1, source_target_pairs={{0,6},{2,0},{4,2},{6,4},{1,7},{3,1},{5,3},{7,5},{8,14},{10,8},{12,... | collective-permute-start | bytes 24584 | tf_op jit(solution)/shard_map/ppermute | solution.py:442
  8.4 48.2 %collective-permute-start.11 = (s32[2048]{0:T(1024)S(1)}, s32[2048]{0:T(1024)S(1)}, u32[]{:S(2)}, u32[]{:S(2)}) collective-permute-start(s32[2048]{0:T(1024)S(1)} %bitcast.81), channel_id=1, source_target_pairs={{0,1},{1,0},{2,3},{3,2},{4,5},{5,4},{6,7},{7,6},{8,9},{9,8},{10,11... | collective-permute-start | bytes 24584 | tf_op jit(solution)/shard_map/ppermute | solution.py:442
  14.2 32.4 %all-to-all-start.4 = ((bf16[128,16,128]{2,1,0:T(8,128)(2,1)}), bf16[128,16,128]{2,1,0:T(8,128)(2,1)S(1)}, u32[]{:S(2)}, u32[]{:S(2)}) async-start(bf16[128,16,128]{2,1,0:T(8,128)(2,1)} %bitcast.12), calls=%async_computation.4 | async-start | bytes 1048576 | tf_op jit(solution)/shard_map/all_to_all | solution.py:477
  29.6 19.8 %copy-start = (f32[512,128]{1,0:T(8,128)S(1)}, f32[512,128]{1,0:T(8,128)}, u32[]{:S(2)}) copy-start(f32[512,128]{1,0:T(8,128)} %grads_ref.1) | copy-start | bytes 786436
  29.6 26.2 %collective-permute-start.6 = (bf16[512,128]{1,0:T(8,128)(2,1)}, bf16[512,128]{1,0:T(8,128)(2,1)S(1)}, u32[]{:S(2)}, u32[]{:S(2)}) collective-permute-start(bf16[512,128]{1,0:T(8,128)(2,1)} %points_ref.1), channel_id=1, source_target_pairs={{0,2},{2,4},{4,6},{6,0},{1,3},{3,5},{5,7},{7,1},{8,10},{10,12},{12... | collective-permute-start | bytes 393224 | tf_op jit(solution)/shard_map/ppermute | solution.py:442
  31.3 25.3 %collective-permute-start.8 = (bf16[512,128]{1,0:T(8,128)(2,1)}, bf16[512,128]{1,0:T(8,128)(2,1)S(1)}, u32[]{:S(2)}, u32[]{:S(2)}) collective-permute-start(bf16[512,128]{1,0:T(8,128)(2,1)} %points_ref.1), channel_id=1, source_target_pairs={{0,6},{2,0},{4,2},{6,4},{1,7},{3,1},{5,3},{7,5},{8,14},{10,8},{12,... | collective-permute-start | bytes 393224 | tf_op jit(solution)/shard_map/ppermute | solution.py:442
  35.7 1.4 %collective-permute-start.5 = (s32[1,1]{1,0:T(1,128)}, s32[1,1]{1,0:T(1,128)}, u32[]{:S(2)}, u32[]{:S(2)}) collective-permute-start(s32[1,1]{1,0:T(1,128)} %get-tuple-element.114), channel_id=1, source_target_pairs={{0,1},{1,0},{2,3},{3,2},{4,5},{5,4},{6,7},{7,6},{8,9},{9,8},{10,11... | collective-permute-start | bytes 20 | tf_op jit(solution)/shard_map/ppermute | solution.py:442
  49.4 13.7 %all-to-all-start.5 = ((bf16[8,256,128]{2,1,0:T(8,128)(2,1)}), bf16[8,256,128]{2,1,0:T(8,128)(2,1)S(1)}, u32[]{:S(2)}, u32[]{:S(2)}) async-start(bf16[8,256,128]{2,1,0:T(8,128)(2,1)} %get-tuple-element.115), calls=%async_computation.5 | async-start | bytes 1048576 | tf_op jit(solution)/shard_map/all_to_all | solution.py:501
  55.8 5.6 %collective-permute-start.7 = (bf16[256,128]{1,0:T(8,128)(2,1)S(1)}, bf16[256,128]{1,0:T(8,128)(2,1)S(1)}, u32[]{:S(2)}, u32[]{:S(2)}) collective-permute-start(bf16[256,128]{1,0:T(8,128)(2,1)S(1)} %slice.32), channel_id=1, source_target_pairs={{0,2},{2,4},{4,6},{6,0},{1,3},{3,5},{5,7},{7,1},{8,10},{10,12},{12... | collective-permute-start | bytes 196616 | tf_op jit(solution)/shard_map/ppermute | solution.py:442
  56.6 4.8 %collective-permute-start.9 = (bf16[256,128]{1,0:T(8,128)(2,1)S(1)}, bf16[256,128]{1,0:T(8,128)(2,1)S(1)}, u32[]{:S(2)}, u32[]{:S(2)}) collective-permute-start(bf16[256,128]{1,0:T(8,128)(2,1)S(1)} %slice.33), channel_id=1, source_target_pairs={{0,6},{2,0},{4,2},{6,4},{1,7},{3,1},{5,3},{7,5},{8,14},{10,8},{12,... | collective-permute-start | bytes 196616 | tf_op jit(solution)/shard_map/ppermute | solution.py:442
  63.1 14.0 %collective-permute-start.10 = (bf16[2048,128]{1,0:T(8,128)(2,1)S(1)}, bf16[2048,128]{1,0:T(8,128)(2,1)S(1)}, u32[]{:S(2)}, u32[]{:S(2)}) collective-permute-start(bf16[2048,128]{1,0:T(8,128)(2,1)S(1)} %bitcast.68), channel_id=1, source_target_pairs={{0,1},{1,0},{2,3},{3,2},{4,5},{5,4},{6,7},{7,6},{8,9},{9,8},{10,11... | collective-permute-start | bytes 1572872 | tf_op jit(solution)/shard_map/ppermute | solution.py:442
  70.1 24.8 %all-to-all-start.6 = ((bf16[32,8,1024]{2,1,0:T(8,128)(2,1)}), bf16[32,8,1024]{2,1,0:T(8,128)(2,1)S(1)}, u32[]{:S(2)}, u32[]{:S(2)}) async-start(bf16[32,8,1024]{2,1,0:T(8,128)(2,1)} %get-tuple-element.117), calls=%async_computation.6 | async-start | bytes 1048576 | tf_op jit(solution)/shard_map/all_to_all | solution.py:505
  94.9 9.8 %collective-permute-start.12 = (bf16[2,128,1024]{2,1,0:T(8,128)(2,1)S(1)}, bf16[2,128,1024]{2,1,0:T(8,128)(2,1)S(1)}, u32[]{:S(2)}, u32[]{:S(2)}) collective-permute-start(bf16[2,128,1024]{2,1,0:T(8,128)(2,1)S(1)} %bitcast.59), channel_id=1, source_target_pairs={{0,1},{1,0},{2,3},{3,2},{4,5},{5,4},{6,7},{7,6},{8,9},{9,8},{10,11... | collective-permute-start | bytes 1572872 | tf_op jit(solution)/shard_map/ppermute | solution.py:442
  94.9 27.3 %all-to-all-start.7 = ((bf16[32,8,1024]{2,1,0:T(8,128)(2,1)}), bf16[32,8,1024]{2,1,0:T(8,128)(2,1)S(1)}, u32[]{:S(2)}, u32[]{:S(2)}) async-start(bf16[32,8,1024]{2,1,0:T(8,128)(2,1)} %get-tuple-element.122), calls=%async_computation.7 | async-start | bytes 1048576 | tf_op jit(solution)/shard_map/all_to_all | solution.py:518
  107.7 8.9 %collective-permute-start.13 = (f32[256,128]{1,0:T(8,128)S(1)}, f32[256,128]{1,0:T(8,128)S(1)}, u32[]{:S(2)}, u32[]{:S(2)}) collective-permute-start(f32[256,128]{1,0:T(8,128)S(1)} %get-tuple-element.167), channel_id=1, source_target_pairs={{0,2},{2,4},{4,6},{6,0},{1,3},{3,5},{5,7},{7,1},{8,10},{10,12},{12... | collective-permute-start | bytes 393224 | tf_op jit(solution)/shard_map/ppermute | solution.py:442
  107.8 8.8 %collective-permute-start.15 = (f32[256,128]{1,0:T(8,128)S(1)}, f32[256,128]{1,0:T(8,128)S(1)}, u32[]{:S(2)}, u32[]{:S(2)}) collective-permute-start(f32[256,128]{1,0:T(8,128)S(1)} %get-tuple-element.166), channel_id=1, source_target_pairs={{0,6},{2,0},{4,2},{6,4},{1,7},{3,1},{5,3},{7,5},{8,14},{10,8},{12,... | collective-permute-start | bytes 393224 | tf_op jit(solution)/shard_map/ppermute | solution.py:442
  116.7 7.9 %collective-permute-start.16 = (f32[512,128]{1,0:T(8,128)S(1)}, f32[512,128]{1,0:T(8,128)S(1)}, u32[]{:S(2)}, u32[]{:S(2)}) collective-permute-start(f32[512,128]{1,0:T(8,128)S(1)} %pad_maximum_fusion.2), channel_id=1, source_target_pairs={{0,6},{2,0},{4,2},{6,4},{1,7},{3,1},{5,3},{7,5},{8,14},{10,8},{12,... | collective-permute-start | bytes 786440 | tf_op jit(solution)/shard_map/ppermute | solution.py:442
  118.8 8.6 %collective-permute-start.14 = (f32[512,128]{1,0:T(8,128)S(1)}, f32[512,128]{1,0:T(8,128)S(1)}, u32[]{:S(2)}, u32[]{:S(2)}) collective-permute-start(f32[512,128]{1,0:T(8,128)S(1)} %pad_maximum_fusion.1), channel_id=1, source_target_pairs={{0,2},{2,4},{4,6},{6,0},{1,3},{3,5},{5,7},{7,1},{8,10},{10,12},{12... | collective-permute-start | bytes 786440 | tf_op jit(solution)/shard_map/ppermute | solution.py:442
